TPU v7x, 512 devices: a whole 4x8x8 slice. The times are simulated.
512 devices in a mesh: fsdp: 32 (over z, y_lo, core), dp: 4 (over y_hi), tensor: 4 (over x).
Axes of the slice: x: 4, y: 8 (y_hi: 4, y_lo: 2; y = y_hi * 2 + y_lo), z: 8, core: 2. Of those that a mesh axis runs over, the one named last changes fastest.
Arguments:
- master_weight: float32 [4096, 14336], P(('fsdp', 'dp'), 'tensor'), may hold values from -0.09375 to 0.09375
- first_moment: bfloat16 [4096, 14336], P(('fsdp', 'dp'), 'tensor'), may hold values from -6 to 6
- second_moment: bfloat16 [4096, 14336], P(('fsdp', 'dp'), 'tensor'), may hold values from 0.25 to 16
- teacher_weight: float32 [4096, 14336], P(('fsdp', 'dp'), 'tensor'), may hold values from -0.09375 to 0.09375
- grad_parts: bfloat16 [4, 4096, 14336], P('dp', 'fsdp', 'tensor'), may hold values from -6 to 6
- embed_table: bfloat16 [4096, 64128], P(('fsdp', 'dp', 'tensor')), may hold values from -6 to 6
- token_ids: int32 [32, 256], P('fsdp'), may hold values from 0 to 64127
- pair_ids: int32 [32, 256], P('fsdp'), may hold values from 0 to 7, never falling along the last dimension, each value on 1 to 64 neighbouring positions
- class_head: bfloat16 [4, 3584, 256], P('tensor', 'dp'), may hold values from -0.046875 to 0.046875
Outputs:
- master_new: float32 [4096, 14336], P(('fsdp', 'dp'), 'tensor')
- first_new: bfloat16 [4096, 14336], P(('fsdp', 'dp'), 'tensor')
- second_new: bfloat16 [4096, 14336], P(('fsdp', 'dp'), 'tensor')
- teacher_new: float32 [4096, 14336], P(('fsdp', 'dp'), 'tensor')
- class_logits: float32 [32, 8, 256], P('fsdp')
Inputs may be any that keep to these rules, and one draw needn't show every extreme that they name: `pair_ids`: in every row the pair numbers never fall, and each of the 8 pairs holds 1 to 64 tokens, one of them exactly 64.
All inputs are finite; a program needn't handle non-finite values.
Results may differ from a plain program's by a relative error of at most 0.0055.
Values may be sent and summed in bfloat16 or wider, within the bound.
No kernel may reach another device: no remote copies, remote signals or barrier semaphores. Data moves between devices by JAX's collectives and lax.ppermute only.
A program may use at most 128 MiB of HBM per device.

v0:
```python
import jax
import jax.numpy as jnp
from jax import lax
from jax.sharding import PartitionSpec as P

PAIRS = 8


beta_one = 0.9
beta_two = 0.95
learn_rate = 0.001
decay_rate = 0.1
ema_keep = 0.99


def optimizer_step(master_weight, first_moment, second_moment, teacher_weight, grad_parts):
    gradient = lax.psum_scatter(
        grad_parts[0].astype(jnp.float32).astype(jnp.bfloat16),
        "dp",
        scatter_dimension=0,
        tiled=True,
    ).astype(jnp.float32)
    first_full = beta_one * first_moment.astype(jnp.float32) + (1.0 - beta_one) * gradient
    second_full = (
        beta_two * second_moment.astype(jnp.float32) + (1.0 - beta_two) * gradient * gradient
    )
    master_new = master_weight - learn_rate * (
        first_full / (jnp.sqrt(second_full) + 1e-08) + decay_rate * master_weight
    )
    teacher_new = ema_keep * teacher_weight + (1.0 - ema_keep) * master_new
    return (
        master_new,
        first_full.astype(jnp.bfloat16),
        second_full.astype(jnp.bfloat16),
        teacher_new,
    )


def embed_inputs(embed_table, token_ids, pair_ids):
    every_id, every_pair = (
        lax.all_gather(token_ids, "fsdp", axis=0, tiled=True),
        lax.all_gather(pair_ids, "fsdp", axis=0, tiled=True),
    )
    picked = jnp.take(embed_table, every_id.reshape(-1), axis=1)
    received = lax.all_to_all(picked, "fsdp", split_axis=1, concat_axis=0, tiled=True)
    stacked = lax.all_gather(received, ("dp", "tensor"), axis=0, tiled=True)
    inner_count = lax.axis_size(("dp", "tensor"))
    shard_count = lax.axis_size("fsdp")
    piece_rows = embed_table.shape[0]
    ordered = stacked.reshape(inner_count, shard_count, piece_rows, -1).transpose(1, 0, 2, 3)
    ordered = ordered.reshape(inner_count * shard_count * piece_rows, -1)
    values = ordered.astype(jnp.float32)
    scale = lax.rsqrt(jnp.mean(values * values, axis=0, keepdims=True) + 1e-05)
    return ((values * scale).astype(jnp.bfloat16), every_pair)


def label_tokens(teacher_new, normed, every_pair, class_head):
    teacher_half = teacher_new.astype(jnp.bfloat16)
    shard_count = lax.axis_size("fsdp")
    replica_count = lax.axis_size("dp")
    place = lax.axis_index("fsdp")
    width = teacher_half.shape[1] // replica_count
    group_pairs = lax.dynamic_slice_in_dim(every_pair, place, 1, 0)
    row_block = lax.all_gather(teacher_half, "fsdp", axis=0, tiled=True)
    split_block = lax.all_to_all(row_block, "dp", split_axis=1, concat_axis=0, tiled=True)
    own_rows = teacher_half.shape[0]
    arranged = split_block.reshape(replica_count, shard_count, own_rows, -1)
    inputs = normed.reshape(shard_count, replica_count, own_rows, -1)
    hidden = jnp.einsum("fdrk,dfro->ko", inputs, arranged, preferred_element_type=jnp.float32)
    group_count = group_pairs.shape[0]
    active = jax.nn.silu(hidden).reshape(group_count, -1, width)
    member_of = (
        group_pairs[:, None, :] == jnp.arange(PAIRS, dtype=jnp.int32)[None, :, None]
    ).astype(jnp.float32)
    totals = jnp.einsum("gpt,gtk->gpk", member_of, active, precision=lax.Precision.HIGHEST)
    pooled = (totals / jnp.sum(member_of, axis=2, keepdims=True)).astype(jnp.bfloat16)
    head_part = class_head[0]
    partial_terms = jnp.einsum("gpk,kc->gpc", pooled, head_part, preferred_element_type=jnp.float32)
    partial_logits = partial_terms[0]
    return lax.psum(partial_logits, ("dp", "tensor"))[None]


def shards(
    master_weight,
    first_moment,
    second_moment,
    teacher_weight,
    grad_parts,
    embed_table,
    token_ids,
    pair_ids,
    class_head,
):
    master_new, first_new, second_new, teacher_new = optimizer_step(
        master_weight, first_moment, second_moment, teacher_weight, grad_parts
    )
    normed, every_pair = embed_inputs(embed_table, token_ids, pair_ids)
    class_logits = label_tokens(teacher_new, normed, every_pair, class_head)
    return (master_new, first_new, second_new, teacher_new, class_logits)


def solution(mesh):
    placed = (
        P(("fsdp", "dp"), "tensor"),
        P(("fsdp", "dp"), "tensor"),
        P(("fsdp", "dp"), "tensor"),
        P(("fsdp", "dp"), "tensor"),
        P("dp", "fsdp", "tensor"),
        P(("fsdp", "dp", "tensor"), None),
        P("fsdp", None),
        P("fsdp", None),
        P("tensor", "dp", None),
    )
    return jax.shard_map(
        shards,
        mesh=mesh,
        in_specs=placed,
        out_specs=(
            P(("fsdp", "dp"), "tensor"),
            P(("fsdp", "dp"), "tensor"),
            P(("fsdp", "dp"), "tensor"),
            P(("fsdp", "dp"), "tensor"),
            P("fsdp", None, None),
        ),
        check_vma=False,
    )
```

profile of v0, /device:TPU:64, one launch (start us, length us, event | category | flops | bytes accessed | tf_op | source)
XLA Modules:
  0.0 421.8 jit_solution(11677021534816718183)
XLA Ops:
  8.0 0.0 copy-start
  8.0 0.0 reduce-scatter.2.cloned.1.call-start
  8.1 0.7 reduce-scatter.2.cloned.1.call-update
  8.8 0.0 all-gather.7.cloned.1.call-start
  8.8 41.9 %reduce-scatter.2.cloned.1.call-done = bf16[32,3584]{1,0:T(8,128)(2,1)} async-done(((bf16[128,3584]{1,0:T(8,128)(2,1)}), bf16[32,3584]{1,0:T(8,128)(2,1)}) %reduce-scatter.2.cloned.1.call-update) | async-done | bytes 229392 | tf_op jit(solution)/shard_map/reduce_scatter | solution.py:17
  50.7 3.0 fusion.19
  53.7 0.0 all-gather.7.cloned.1.call-update
  53.7 0.0 copy-start.4
  53.7 10.6 %copy.26 = bf16[8,64128]{0,1:T(8,128)(2,1)} copy(bf16[8,64128]{1,0:T(8,128)(2,1)S(1)} %copy-done.2) | data formatting | bytes 2052096 | tf_op args[5]
  64.4 31.9 %all-gather.1 = s32[32,1,256]{2,1,0:T(1,128)S(1)} all-gather(s32[1,1,256]{2,1,0:T(1,128)S(1)} %bitcast.48), channel_id=1, replica_groups=mesh['fsdp'=32,'dp'=4,'tensor'=4] {'fsdp'}, dimensions={0}, use_global_device_ids=true | all-gather | bytes 33792 | tf_op jit(solution)/shard_map/all_gather | solution.py:41
  96.4 29.9 %gather_fusion = bf16[8192,8]{1,0:T(8,128)(2,1)S(1)} fusion(bf16[8,64128]{0,1:T(8,128)(2,1)} %copy.26, s32[8192]{0:T(1024)S(1)} %broadcast_clamp_fusion), kind=kCustom, calls=%fused_computation | custom fusion | bytes 294912 | tf_op jit(solution)/shard_map/jit(_take)/gather | solution.py:44
  126.3 0.8 copy.27
  127.1 0.7 broadcast_select_fusion
  127.8 7.8 %all-to-all-start = ((bf16[8,32,256]{2,0,1:T(8,128)(2,1)}), bf16[8,32,256]{2,0,1:T(8,128)(2,1)S(1)}, u32[]{:S(2)}, u32[]{:S(2)}) async-start(bf16[8,32,256]{2,0,1:T(8,128)(2,1)} %broadcast_select_fusion), calls=%async_computation.1 | async-start | bytes 262144 | tf_op jit(solution)/shard_map/all_to_all | solution.py:45
  135.6 0.0 all-gather.7.cloned.1.call-done
  135.6 6.6 %copy.42 = bf16[128,4,8,896]{3,2,0,1:T(8,128)(2,1)} copy(bf16[128,4,8,896]{3,2,1,0:T(8,128)(2,1)} %bitcast.42) | data formatting | bytes 14680064 | tf_op jit(solution)/shard_map/all_to_all | solution.py:65
  142.2 1.7 all-to-all-done
  144.0 0.6 copy-done.3
  144.6 5.5 %all-to-all-start.1 = ((bf16[1024,4,896]{2,0,1:T(8,128)(2,1)}), bf16[1024,4,896]{2,0,1:T(8,128)(2,1)}, u32[]{:S(2)}, u32[]{:S(2)}) async-start(bf16[1024,4,896]{2,0,1:T(8,128)(2,1)} %bitcast.39), calls=%async_computation.2 | async-start | bytes 14680064 | tf_op jit(solution)/shard_map/all_to_all | solution.py:65
  150.1 0.0 all-gather.5.cloned.1.call-start
  150.2 0.5 all-gather.5.cloned.1.call-update
  150.7 202.1 %all-gather = s32[32,1,256]{2,1,0:T(1,128)S(1)} all-gather(s32[1,1,256]{2,1,0:T(1,128)S(1)} %bitcast.49), channel_id=1, replica_groups=mesh['fsdp'=32,'dp'=4,'tensor'=4] {'fsdp'}, dimensions={0}, use_global_device_ids=true | all-gather | bytes 33792 | tf_op jit(solution)/shard_map/all_gather | solution.py:42
  352.8 0.1 convert_reduce_fusion
  352.9 0.0 all-gather.5.cloned.1.call-done
  352.9 4.2 %copy.28 = f32[16,32,8,256]{3,2,0,1:T(8,128)} copy(bf16[16,32,8,256]{3,2,1,0:T(8,128)(2,1)} %bitcast.41) | data formatting | bytes 6291456 | tf_op jit(solution)/shard_map/convert_element_type | solution.py:52
  357.2 0.0 copy-done.1
  357.2 0.6 multiply_reduce_fusion
  357.8 0.0 all-to-all-done.1
  357.8 6.7 %fusion.2 = f32[256,896]{1,0:T(8,128)S(1)} fusion(bf16[4,32,32,896]{3,2,1,0:T(8,128)(2,1)} %bitcast.14, f32[32,4,32,256]{3,2,1,0:T(8,128)} %bitcast.40, f32[256]{0:T(256)S(1)} %add_rsqrt_fusion), kind=kOutput, calls=%fused_computation.6 | convolution fusion | flops 1881145344 | bytes 12452864 | tf_op jit(solution)/shard_map/fdrk,dfro->ko/dot_general | solution.py:69
  364.5 0.6 fusion.5
  365.1 0.2 convolution_bitcast_fusion
  365.3 49.1 %psum.7 = f32[1,8,256]{2,1,0:T(8,128)} all-reduce(f32[1,8,256]{2,1,0:T(8,128)S(1)} %convolution_bitcast_fusion), channel_id=1, replica_groups=mesh['fsdp'=32,'dp'=4,'tensor'=4] {'dp','tensor'}, use_global_device_ids=true, to_apply=%region_3.4 | all-reduce | flops 2048 | bytes 16384 | tf_op jit(solution)/shard_map/psum | solution.py:80
  (13 shorter events, 0.1 us)
Async XLA Ops:
  8.0 357.1 %copy-start = (bf16[1,896,256]{2,1,0:T(8,128)(2,1)S(1)}, bf16[1,896,256]{2,1,0:T(8,128)(2,1)}, u32[]{:S(2)}) copy-start(bf16[1,896,256]{2,1,0:T(8,128)(2,1)} %param.17) | copy-start | bytes 1376260
  8.0 45.7 %copy-start.2 = (bf16[8,64128]{1,0:T(8,128)(2,1)S(1)}, bf16[8,64128]{1,0:T(8,128)(2,1)}, u32[]{:S(2)}) copy-start(bf16[8,64128]{1,0:T(8,128)(2,1)} %param.14) | copy-start | bytes 3078148
  8.0 42.7 %reduce-scatter.2.cloned.1.call-start = ((), (), s32[]{:S(2)}) async-start(), calls=%async_computation.3 | async-start | bytes 1146880 | tf_op jit(solution)/shard_map/reduce_scatter | solution.py:17
  8.8 126.9 %all-gather.7.cloned.1.call-start = ((), (), s32[]{:S(2)}) async-start(), calls=%async_computation.5 | async-start | bytes 7569408 | tf_op jit(solution)/shard_map/all_gather | solution.py:64
  53.7 10.6 %copy-start.4 = (s32[1,256]{1,0:T(1,128)S(1)}, s32[1,256]{1,0:T(1,128)}, u32[]{:S(2)}) copy-start(s32[1,256]{1,0:T(1,128)} %param.15) | copy-start | bytes 3076
  127.8 16.2 %all-to-all-start = ((bf16[8,32,256]{2,0,1:T(8,128)(2,1)}), bf16[8,32,256]{2,0,1:T(8,128)(2,1)S(1)}, u32[]{:S(2)}, u32[]{:S(2)}) async-start(bf16[8,32,256]{2,0,1:T(8,128)(2,1)} %broadcast_select_fusion), calls=%async_computation.1 | async-start | bytes 262144 | tf_op jit(solution)/shard_map/all_to_all | solution.py:45
  144.0 0.7 copy-start.3
  144.0 6.7 %copy-start.5 = (s32[1,256]{1,0:T(1,128)S(1)}, s32[1,256]{1,0:T(1,128)}, u32[]{:S(2)}) copy-start(s32[1,256]{1,0:T(1,128)} %param.16) | copy-start | bytes 3076
  144.6 213.2 %all-to-all-start.1 = ((bf16[1024,4,896]{2,0,1:T(8,128)(2,1)}), bf16[1024,4,896]{2,0,1:T(8,128)(2,1)}, u32[]{:S(2)}, u32[]{:S(2)}) async-start(bf16[1024,4,896]{2,0,1:T(8,128)(2,1)} %bitcast.39), calls=%async_computation.2 | async-start | bytes 14680064 | tf_op jit(solution)/shard_map/all_to_all | solution.py:65
  150.1 202.8 %all-gather.5.cloned.1.call-start = ((), (), s32[]{:S(2)}) async-start(), calls=%async_computation.4 | async-start | bytes 2228224 | tf_op jit(solution)/shard_map/all_gather | solution.py:46
  352.9 4.2 %copy-start.1 = (bf16[4096,256]{1,0:T(8,128)(2,1)S(1)}, bf16[4096,256]{1,0:T(8,128)(2,1)}, u32[]{:S(2)}) copy-start(bf16[4096,256]{1,0:T(8,128)(2,1)} %all-gather.5.cloned.1.call-done) | copy-start | bytes 6291460
Sparse Core Ops, SparseCore 0:
  11.7 38.9 reduce-scatter.1
  53.8 71.7 all-gather.6
Sparse Core Ops, SparseCore 1:
  153.6 182.3 all-gather.4
where the time goes:
time: 422 us
  blocking collectives  283 us (67%)
  local copies, waits for them, and re-layouts  52.9 us (13%)
  waiting for transfers between devices  44.9 us (11%)
  between operations  15.6 us (4%)
  starting transfers between devices  13.4 us (3%)
  matrix products  7.51 us (2%)
  other arithmetic  4.42 us (1%)
    all_gather x1, blocking collectives, embed_inputs(): lax.all_gather(pair_ids, 'fsdp', axis=0, tiled=True)  202 us
    psum x1, blocking collectives, label_tokens(): return lax.psum(partial_logits, ('dp', 'tensor'))[None]  49.1 us
    reduce_scatter x1, waiting for transfers between devices, optimizer_step(): lax.psum_scatter(grad_parts[0].astype(jnp.float32).astype(jnp.bfloat16),...  41.9 us
    all_gather x1, blocking collectives, embed_inputs(): lax.all_gather(token_ids, 'fsdp', axis=0, tiled=True)  31.9 us
    gather x2, local copies, waits for them, and re-layouts, embed_inputs(): picked = jnp.take(embed_table, every_id.reshape(-1), axis=1)  30.7 us
    unnamed x13, local copies, waits for them, and re-layouts  11.3 us
  transfers between devices with their start and end apart: 5, of which 2 were waited for; matrix products, arithmetic and copies ran while one was open for 13% of the time, Pallas kernels for 0%

commit v1 on v0

v1 whole, which is shorter than its diff:
```python
import jax
import jax.numpy as jnp
from jax import lax
from jax.sharding import PartitionSpec as P

PAIRS = 8


beta_one = 0.9
beta_two = 0.95
learn_rate = 0.001
decay_rate = 0.1
ema_keep = 0.99


def optimizer_step(master_weight, first_moment, second_moment, teacher_weight, grad_parts):
    gradient = lax.psum_scatter(
        grad_parts[0], "dp", scatter_dimension=0, tiled=True
    ).astype(jnp.float32)
    first_full = beta_one * first_moment.astype(jnp.float32) + (1.0 - beta_one) * gradient
    second_full = (
        beta_two * second_moment.astype(jnp.float32) + (1.0 - beta_two) * gradient * gradient
    )
    master_new = master_weight - learn_rate * (
        first_full / (jnp.sqrt(second_full) + 1e-08) + decay_rate * master_weight
    )
    teacher_new = ema_keep * teacher_weight + (1.0 - ema_keep) * master_new
    return (
        master_new,
        first_full.astype(jnp.bfloat16),
        second_full.astype(jnp.bfloat16),
        teacher_new,
    )


def ring_gather(block, axis):
    count = lax.axis_size(axis)
    right = [(i, (i + 1) % count) for i in range(count)]
    left = [(i, (i - 1) % count) for i in range(count)]
    place = lax.axis_index(axis)
    half = block.shape[0] // 2
    whole = jnp.zeros((count,) + block.shape, block.dtype)
    whole = lax.dynamic_update_index_in_dim(whole, block, place, 0)
    going_right = going_left = block
    for step in range(1, count // 2):
        going_right = lax.ppermute(going_right, axis, right)
        going_left = lax.ppermute(going_left, axis, left)
        whole = lax.dynamic_update_index_in_dim(whole, going_right, (place - step) % count, 0)
        whole = lax.dynamic_update_index_in_dim(whole, going_left, (place + step) % count, 0)
    first = lax.ppermute(going_right[:half], axis, right)
    second = lax.ppermute(going_left[half:], axis, left)
    last = jnp.concatenate([first, second], axis=0)
    return lax.dynamic_update_index_in_dim(whole, last, (place + count // 2) % count, 0)


def embed_inputs(embed_table, token_ids):
    every_id = lax.all_to_all(
        jnp.broadcast_to(token_ids, (32, token_ids.shape[1])), "fsdp", 0, 0, tiled=True
    )
    picked = embed_table.at[:, every_id.reshape(-1)].get(mode="promise_in_bounds")
    received = lax.all_to_all(
        picked.reshape(8, 32, 256).transpose(1, 0, 2), "fsdp", split_axis=0, concat_axis=0, tiled=True
    )
    part = lax.all_gather(received.reshape(256, 256), "dp", axis=0, tiled=True)
    return ring_gather(part, "tensor")


def label_tokens(teacher_new, stacked, group_pairs, class_head):
    teacher_half = teacher_new.astype(jnp.bfloat16)
    replica_count = lax.axis_size("dp")
    rows = teacher_half.shape[0]
    width = teacher_half.shape[1] // replica_count
    split = teacher_half.reshape(rows, replica_count, width).transpose(1, 0, 2)
    block = lax.all_to_all(split.reshape(-1, width), "dp", 0, 0, tiled=True)
    row_block = lax.all_gather(block, "fsdp", axis=0, tiled=True)
    inputs = stacked.reshape(4, 4, 32, 8, 256).transpose(2, 1, 0, 3, 4).reshape(4096, 256)
    values = inputs.astype(jnp.float32)
    scale = lax.rsqrt(jnp.mean(values * values, axis=0, keepdims=True) + 1e-05)
    normed = (values * scale).astype(jnp.bfloat16)
    hidden = jnp.einsum("fk,fo->ko", normed, row_block, preferred_element_type=jnp.float32)
    group_count = group_pairs.shape[0]
    active = jax.nn.silu(hidden).reshape(group_count, -1, width)
    member_of = (
        group_pairs[:, None, :] == jnp.arange(PAIRS, dtype=jnp.int32)[None, :, None]
    ).astype(jnp.float32)
    totals = jnp.einsum("gpt,gtk->gpk", member_of, active, precision=lax.Precision.HIGHEST)
    pooled = (totals / jnp.sum(member_of, axis=2, keepdims=True)).astype(jnp.bfloat16)
    head_part = class_head[0]
    partial_terms = jnp.einsum("gpk,kc->gpc", pooled, head_part, preferred_element_type=jnp.float32)
    return lax.psum(lax.psum(partial_terms, "dp"), "tensor")


def shards(
    master_weight,
    first_moment,
    second_moment,
    teacher_weight,
    grad_parts,
    embed_table,
    token_ids,
    pair_ids,
    class_head,
):
    master_new, first_new, second_new, teacher_new = optimizer_step(
        master_weight, first_moment, second_moment, teacher_weight, grad_parts
    )
    stacked = embed_inputs(embed_table, token_ids)
    class_logits = label_tokens(teacher_new, stacked, pair_ids, class_head)
    return (master_new, first_new, second_new, teacher_new, class_logits)


def solution(mesh):
    placed = (
        P(("fsdp", "dp"), "tensor"),
        P(("fsdp", "dp"), "tensor"),
        P(("fsdp", "dp"), "tensor"),
        P(("fsdp", "dp"), "tensor"),
        P("dp", "fsdp", "tensor"),
        P(("fsdp", "dp", "tensor"), None),
        P("fsdp", None),
        P("fsdp", None),
        P("tensor", "dp", None),
    )
    return jax.shard_map(
        shards,
        mesh=mesh,
        in_specs=placed,
        out_specs=(
            P(("fsdp", "dp"), "tensor"),
            P(("fsdp", "dp"), "tensor"),
            P(("fsdp", "dp"), "tensor"),
            P(("fsdp", "dp"), "tensor"),
            P("fsdp", None, None),
        ),
        check_vma=False,
    )
```

time: 422 us -> 217 us (0.51)
  the two profiles are of different devices: /device:TPU:64 before, /device:TPU:8 now
where the time goes in v1:
time: 217 us
  blocking collectives  72.7 us (34%)
  waiting for transfers between devices  53.3 us (25%)
  local copies, waits for them, and re-layouts  43 us (20%)
  starting transfers between devices  22.8 us (11%)
  between operations  14.3 us (7%)
  matrix products  6.27 us (3%)
  other arithmetic  4.68 us (2%)
    reduce_scatter x1, waiting for transfers between devices, optimizer_step(): lax.psum_scatter(grad_parts[0], 'dp', scatter_dimension=0, tiled=True)  42.5 us
    gather x1, local copies, waits for them, and re-layouts, embed_inputs(): embed_table.at[:, every_id.reshape(-1)].get(mode='promise_in_bounds')  29.9 us
    psum x2, blocking collectives, label_tokens(): return lax.psum(lax.psum(partial_terms, 'dp'), 'tensor')  24.5 us
    all_to_all x1, blocking collectives, embed_inputs(): lax.all_to_all(picked.reshape(8, 32, 256).transpose(1, 0, 2), 'fsdp', spl...  17.7 us
    all_gather x1, blocking collectives, embed_inputs(): part = lax.all_gather(received.reshape(256, 256), 'dp', axis=0, tiled=True)  16.4 us
    all_to_all x1, blocking collectives, label_tokens(): block = lax.all_to_all(split.reshape(-1, width), 'dp', 0, 0, tiled=True)  14.2 us
    unnamed x9, local copies, waits for them, and re-layouts  10.7 us
    all_to_all x1, starting transfers between devices, embed_inputs(): lax.all_to_all(jnp.broadcast_to(token_ids, (32, token_ids.shape[1])), 'fs...  8.59 us
  transfers between devices with their start and end apart: 7, of which 4 were waited for; matrix products, arithmetic and copies ran while one was open for 21% of the time, Pallas kernels for 0%

profile of v1, /device:TPU:8, one launch (start us, length us, event | category | flops | bytes accessed | tf_op | source)
XLA Modules:
  0.0 217.0 jit_solution(6691346589471912774)
XLA Ops:
  7.2 0.0 reduce-scatter.2.cloned.1.call-start
  7.2 0.7 reduce-scatter.2.cloned.1.call-update
  7.9 0.0 all-gather.2.cloned.1.call-start
  8.0 42.5 %reduce-scatter.2.cloned.1.call-done = bf16[32,3584]{1,0:T(8,128)(2,1)} async-done(((bf16[128,3584]{1,0:T(8,128)(2,1)}), bf16[32,3584]{1,0:T(8,128)(2,1)}) %reduce-scatter.2.cloned.1.call-update) | async-done | bytes 229392 | tf_op jit(solution)/shard_map/reduce_scatter | solution.py:17
  50.4 2.9 %fusion.16 = (bf16[32,3584]{1,0:T(8,128)(2,1)S(1)}, f32[32,3584]{1,0:T(8,128)}, f32[32,3584]{1,0:T(8,128)}, bf16[32,3584]{1,0:T(8,128)(2,1)}, bf16[32,3584]{1,0:T(8,128)(2,1)}) fusion(f32[32,3584]{1,0:T(8,128)} %param.12, f32[32,3584]{1,0:T(8,128)} %param.9, bf16[32,3584]{1,0:T(8,128)(2,1)} %param.11, bf16[32,3584]{1,0:T(8,128)(2,1)} %reduce-scatter.2.cloned.1.call-done, ...), kind=kLoop, calls=%fused_computation.35 | loop fusion | flops 2523136 | bytes 3211264 | tf_op jit(solution)/shard_map/convert_element_type | solution.py:69
  53.4 0.1 reshape.152
  53.5 14.2 %all_to_all.20 = bf16[4,32,896]{2,1,0:T(8,128)(2,1)} all-to-all(bf16[4,32,896]{2,1,0:T(8,128)(2,1)S(1)} %copy.28), channel_id=1, replica_groups=mesh['fsdp'=32,'dp'=4,'tensor'=4] {'dp'}, dimensions={0} | all-to-all | bytes 458752 | tf_op jit(solution)/shard_map/all_to_all | solution.py:74
  67.7 0.6 broadcast_in_dim.27
  68.3 8.6 %all-to-all-start = ((s32[32,1,256]{2,1,0:T(1,128)}), s32[32,1,256]{2,1,0:T(1,128)S(1)}, u32[]{:S(2)}, u32[]{:S(2)}) async-start(s32[32,1,256]{2,1,0:T(1,128)} %broadcast_in_dim.27), calls=%async_computation.1 | async-start | bytes 65536 | tf_op jit(solution)/shard_map/all_to_all | solution.py:57
  76.9 10.7 %copy.25 = bf16[8,64128]{0,1:T(8,128)(2,1)} copy(bf16[8,64128]{1,0:T(8,128)(2,1)S(1)} %copy-done.1) | data formatting | bytes 2052096 | tf_op args[5]
  87.6 29.9 %gather_fusion = bf16[8192,8]{1,0:T(8,128)(2,1)S(1)} fusion(bf16[8,64128]{0,1:T(8,128)(2,1)} %copy.25, s32[8192]{0:T(1024)S(1)} %broadcast_clamp_fusion), kind=kCustom, calls=%fused_computation | custom fusion | bytes 294912 | tf_op jit(solution)/shard_map/gather | solution.py:60
  117.6 0.8 copy.26
  118.3 17.7 %all_to_all.21 = bf16[32,8,256]{2,1,0:T(8,128)(2,1)S(1)} all-to-all(bf16[32,8,256]{2,1,0:T(8,128)(2,1)S(1)} %bitcast.42), channel_id=1, replica_groups=mesh['fsdp'=32,'dp'=4,'tensor'=4] {'fsdp'}, dimensions={0} | all-to-all | bytes 262144 | tf_op jit(solution)/shard_map/all_to_all | solution.py:61
  136.0 16.4 %all_gather.6 = bf16[1024,256]{1,0:T(8,128)(2,1)S(1)} all-gather(bf16[256,256]{1,0:T(8,128)(2,1)S(1)} %bitcast.43), channel_id=1, replica_groups=mesh['fsdp'=32,'dp'=4,'tensor'=4] {'dp'}, dimensions={0}, use_global_device_ids=true | all-gather | bytes 655360 | tf_op jit(solution)/shard_map/all_gather | solution.py:64
  152.4 2.9 %collective-permute-start = (bf16[1024,256]{1,0:T(8,128)(2,1)S(1)}, bf16[1024,256]{1,0:T(8,128)(2,1)S(1)}, u32[]{:S(2)}, u32[]{:S(2)}) collective-permute-start(bf16[1024,256]{1,0:T(8,128)(2,1)S(1)} %all_gather.6), channel_id=1, source_target_pairs={{0,1},{1,2},{2,3},{3,0},{4,5},{5,6},{6,7},{7,4},{8,9},{9,10},{10,1... | collective-permute-start | bytes 1572872 | tf_op jit(solution)/shard_map/ppermute | solution.py:46
  155.3 4.1 %collective-permute-start.1 = (bf16[1024,256]{1,0:T(8,128)(2,1)S(1)}, bf16[1024,256]{1,0:T(8,128)(2,1)S(1)}, u32[]{:S(2)}, u32[]{:S(2)}) collective-permute-start(bf16[1024,256]{1,0:T(8,128)(2,1)S(1)} %all_gather.6), channel_id=1, source_target_pairs={{0,3},{1,0},{2,1},{3,2},{4,7},{5,4},{6,5},{7,6},{8,11},{9,8},{10,9... | collective-permute-start | bytes 1572872 | tf_op jit(solution)/shard_map/ppermute | solution.py:47
  159.5 0.1 convert_reduce_fusion
  159.6 0.1 broadcast_in_dim.26
  159.8 6.4 %collective-permute-done = bf16[1024,256]{1,0:T(8,128)(2,1)S(1)} collective-permute-done((bf16[1024,256]{1,0:T(8,128)(2,1)S(1)}, bf16[1024,256]{1,0:T(8,128)(2,1)S(1)}, u32[]{:S(2)}, u32[]{:S(2)}) %collective-permute-start) | collective-permute-done | bytes 524320 | tf_op jit(solution)/shard_map/ppermute | solution.py:46
  166.2 1.9 collective-permute-start.2
  168.2 5.1 %collective-permute-start.3 = (bf16[512,256]{1,0:T(8,128)(2,1)S(1)}, bf16[512,256]{1,0:T(8,128)(2,1)S(1)}, u32[]{:S(2)}, u32[]{:S(2)}) collective-permute-start(bf16[512,256]{1,0:T(8,128)(2,1)S(1)} %slice.11), channel_id=1, source_target_pairs={{0,3},{1,0},{2,1},{3,2},{4,7},{5,4},{6,5},{7,6},{8,11},{9,8},{10,9... | collective-permute-start | bytes 786440 | tf_op jit(solution)/shard_map/ppermute | solution.py:51
  173.4 2.3 %collective-permute-done.2 = bf16[512,256]{1,0:T(8,128)(2,1)S(1)} collective-permute-done((bf16[512,256]{1,0:T(8,128)(2,1)S(1)}, bf16[512,256]{1,0:T(8,128)(2,1)S(1)}, u32[]{:S(2)}, u32[]{:S(2)}) %collective-permute-start.2) | collective-permute-done | bytes 262176 | tf_op jit(solution)/shard_map/ppermute | solution.py:50
  175.7 1.5 collective-permute-done.3
  177.2 0.4 convert_element_type.69
  177.6 0.6 copy.27
  178.2 0.6 multiply_reduce_fusion
  178.8 0.6 fusion
  179.5 5.5 %fusion.17 = f32[256,896]{1,0:T(8,128)S(1)} fusion(bf16[4096,256]{1,0:T(8,128)(2,1)S(1)} %fusion, bf16[4096,896]{1,0:T(8,128)(2,1)} %all-gather.2.cloned.1.call-done), kind=kOutput, calls=%fused_computation.36 | convolution fusion | flops 1879048192 | bytes 10354688 | tf_op jit(solution)/shard_map/fk,fo->ko/dot_general | solution.py:80
  185.0 0.6 fusion.1
  185.6 0.2 convolution_bitcast_fusion
  185.7 12.3 %psum.14 = f32[1,8,256]{2,1,0:T(8,128)S(1)} all-reduce(f32[1,8,256]{2,1,0:T(8,128)S(1)} %convolution_bitcast_fusion), channel_id=1, replica_groups=mesh['fsdp'=32,'dp'=4,'tensor'=4] {'dp'}, use_global_device_ids=true, to_apply=%region_3.4 | all-reduce | flops 2048 | bytes 16384 | tf_op jit(solution)/shard_map/psum | solution.py:90
  198.1 12.1 %psum.15 = f32[1,8,256]{2,1,0:T(8,128)} all-reduce(f32[1,8,256]{2,1,0:T(8,128)S(1)} %psum.14), channel_id=1, replica_groups=mesh['fsdp'=32,'dp'=4,'tensor'=4] {'tensor'}, use_global_device_ids=true, to_apply=%region_4.5 | all-reduce | flops 2048 | bytes 16384 | tf_op jit(solution)/shard_map/psum | solution.py:90
  (22 shorter events, 0.3 us)
Async XLA Ops:
  7.2 178.4 %copy-start = (bf16[1,896,256]{2,1,0:T(8,128)(2,1)S(1)}, bf16[1,896,256]{2,1,0:T(8,128)(2,1)}, u32[]{:S(2)}) copy-start(bf16[1,896,256]{2,1,0:T(8,128)(2,1)} %param.17) | copy-start | bytes 1376260
  7.2 43.3 %reduce-scatter.2.cloned.1.call-start = ((), (), s32[]{:S(2)}) async-start(), calls=%async_computation.4 | async-start | bytes 1146880 | tf_op jit(solution)/shard_map/reduce_scatter | solution.py:17
  7.9 59.7 %copy-start.2 = (s32[1,256]{1,0:T(1,128)S(1)}, s32[1,256]{1,0:T(1,128)}, u32[]{:S(2)}) copy-start(s32[1,256]{1,0:T(1,128)} %param.15) | copy-start | bytes 3076
  7.9 69.0 %copy-start.1 = (bf16[8,64128]{1,0:T(8,128)(2,1)S(1)}, bf16[8,64128]{1,0:T(8,128)(2,1)}, u32[]{:S(2)}) copy-start(bf16[8,64128]{1,0:T(8,128)(2,1)} %param.14) | copy-start | bytes 3078148
  7.9 171.5 %all-gather.2.cloned.1.call-start = ((), (), s32[]{:S(2)}) async-start(), calls=%async_computation.5 | async-start | bytes 7569408 | tf_op jit(solution)/shard_map/all_gather | solution.py:75
  68.3 19.3 %all-to-all-start = ((s32[32,1,256]{2,1,0:T(1,128)}), s32[32,1,256]{2,1,0:T(1,128)S(1)}, u32[]{:S(2)}, u32[]{:S(2)}) async-start(s32[32,1,256]{2,1,0:T(1,128)} %broadcast_in_dim.27), calls=%async_computation.1 | async-start | bytes 65536 | tf_op jit(solution)/shard_map/all_to_all | solution.py:57
  87.6 71.9 %copy-start.3 = (s32[1,256]{1,0:T(1,128)S(1)}, s32[1,256]{1,0:T(1,128)}, u32[]{:S(2)}) copy-start(s32[1,256]{1,0:T(1,128)} %param.16) | copy-start | bytes 3076
  152.4 13.8 %collective-permute-start = (bf16[1024,256]{1,0:T(8,128)(2,1)S(1)}, bf16[1024,256]{1,0:T(8,128)(2,1)S(1)}, u32[]{:S(2)}, u32[]{:S(2)}) collective-permute-start(bf16[1024,256]{1,0:T(8,128)(2,1)S(1)} %all_gather.6), channel_id=1, source_target_pairs={{0,1},{1,2},{2,3},{3,0},{4,5},{5,6},{6,7},{7,4},{8,9},{9,10},{10,1... | collective-permute-start | bytes 1572872 | tf_op jit(solution)/shard_map/ppermute | solution.py:46
  155.3 12.8 %collective-permute-start.1 = (bf16[1024,256]{1,0:T(8,128)(2,1)S(1)}, bf16[1024,256]{1,0:T(8,128)(2,1)S(1)}, u32[]{:S(2)}, u32[]{:S(2)}) collective-permute-start(bf16[1024,256]{1,0:T(8,128)(2,1)S(1)} %all_gather.6), channel_id=1, source_target_pairs={{0,3},{1,0},{2,1},{3,2},{4,7},{5,4},{6,5},{7,6},{8,11},{9,8},{10,9... | collective-permute-start | bytes 1572872 | tf_op jit(solution)/shard_map/ppermute | solution.py:47
  166.2 9.5 %collective-permute-start.2 = (bf16[512,256]{1,0:T(8,128)(2,1)S(1)}, bf16[512,256]{1,0:T(8,128)(2,1)S(1)}, u32[]{:S(2)}, u32[]{:S(2)}) collective-permute-start(bf16[512,256]{1,0:T(8,128)(2,1)S(1)} %slice.10), channel_id=1, source_target_pairs={{0,1},{1,2},{2,3},{3,0},{4,5},{5,6},{6,7},{7,4},{8,9},{9,10},{10,1... | collective-permute-start | bytes 786440 | tf_op jit(solution)/shard_map/ppermute | solution.py:50
  168.2 9.0 %collective-permute-start.3 = (bf16[512,256]{1,0:T(8,128)(2,1)S(1)}, bf16[512,256]{1,0:T(8,128)(2,1)S(1)}, u32[]{:S(2)}, u32[]{:S(2)}) collective-permute-start(bf16[512,256]{1,0:T(8,128)(2,1)S(1)} %slice.11), channel_id=1, source_target_pairs={{0,3},{1,0},{2,1},{3,2},{4,7},{5,4},{6,5},{7,6},{8,11},{9,8},{10,9... | collective-permute-start | bytes 786440 | tf_op jit(solution)/shard_map/ppermute | solution.py:51
Sparse Core Ops, SparseCore 0:
  10.8 39.5 reduce-scatter.1
  67.8 72.7 all-gather.1

commit v2 on v0

v2 whole, which is shorter than its diff:
```python
import functools

import jax
import jax.numpy as jnp
from jax import lax
from jax.experimental import pallas as pl
from jax.experimental.pallas import tpu as pltpu
from jax.sharding import Mesh
from jax.sharding import PartitionSpec as P

PAIRS = 8
TOKENS = 256
WIDTH = 896
UPPER = 512

beta_one = 0.9
beta_two = 0.95
learn_rate = 0.001
decay_rate = 0.1
ema_keep = 0.99

f32 = jnp.float32
bf16 = jnp.bfloat16
VMEM = pltpu.VMEM


def optimizer_kernel(
    place_ref, master_ref, first_ref, second_ref, teacher_ref, parts_ref,
    master_out, first_out, second_out, teacher_out, columns_out,
):
    gradient = parts_ref[0].astype(f32)
    for member in range(1, 4):
        gradient = gradient + parts_ref[member].astype(f32)
    first_full = beta_one * first_ref[...].astype(f32) + (1.0 - beta_one) * gradient
    second_full = (
        beta_two * second_ref[...].astype(f32) + (1.0 - beta_two) * gradient * gradient
    )
    master = master_ref[...]
    master_new = master - learn_rate * (
        first_full / (jnp.sqrt(second_full) + 1e-08) + decay_rate * master
    )
    teacher_new = ema_keep * teacher_ref[...] + (1.0 - ema_keep) * master_new
    master_out[...] = master_new
    first_out[...] = first_full.astype(bf16)
    second_out[...] = second_full.astype(bf16)
    teacher_out[...] = teacher_new
    columns_out[0] = teacher_new.astype(bf16)


def optimizer_step(place, master_weight, first_moment, second_moment, teacher_weight, parts):
    block = pl.BlockSpec((32, WIDTH), lambda k, place: (0, (place[0] + k) % 4))
    shape = master_weight.shape
    return pl.pallas_call(
        optimizer_kernel,
        grid_spec=pltpu.PrefetchScalarGridSpec(
            num_scalar_prefetch=1,
            grid=(4,),
            in_specs=[block] * 4
            + [pl.BlockSpec((4, 32, WIDTH), lambda k, place: (0, 0, (place[0] + k) % 4))],
            out_specs=[block] * 4 + [pl.BlockSpec((1, 32, WIDTH), lambda k, place: (k, 0, 0))],
        ),
        out_shape=[
            jax.ShapeDtypeStruct(shape, f32),
            jax.ShapeDtypeStruct(shape, bf16),
            jax.ShapeDtypeStruct(shape, bf16),
            jax.ShapeDtypeStruct(shape, f32),
            jax.ShapeDtypeStruct((4, 32, WIDTH), bf16),
        ],
        cost_estimate=pl.CostEstimate(flops=1 << 21, bytes_accessed=1 << 23, transcendentals=0),
        name="optimizer_step",
    )(place, master_weight, first_moment, second_moment, teacher_weight, parts)


def turn_table_kernel(table_ref, out_ref, wide, turned):
    count = table_ref.shape[0]
    wide[pl.ds(0, count)] = table_ref[...].astype(f32)
    wide[pl.ds(count, UPPER - count)] = jnp.zeros((UPPER - count, 8, 128), f32)
    for part in range(UPPER // 128):
        for row in range(8):
            turned[:, row, pl.ds(part * 128, 128)] = wide[pl.ds(part * 128, 128), row, :].T
    out_ref[...] = turned[...].reshape(1024, UPPER).astype(bf16)


def turn_table(table):
    tiles = table.reshape(8, -1, 128).transpose(1, 0, 2)
    return pl.pallas_call(
        turn_table_kernel,
        out_shape=jax.ShapeDtypeStruct((1024, UPPER), bf16),
        in_specs=[pl.BlockSpec(memory_space=VMEM)],
        out_specs=pl.BlockSpec(memory_space=VMEM),
        scratch_shapes=[VMEM((UPPER, 8, 128), f32), VMEM((128, 8, UPPER), f32)],
        cost_estimate=pl.CostEstimate(flops=0, bytes_accessed=1 << 24, transcendentals=0),
        name="turn_table",
    )(tiles)


def pick_kernel(ids_ref, table_ref, out_ref):
    ids = ids_ref[0]
    count = ids.shape[1]
    upper = ids >> 7
    lower = jnp.broadcast_to(ids & 127, (8, count))
    rows = lax.broadcasted_iota(jnp.int32, (UPPER, count), 0)
    hot = jnp.where(rows == upper, 1.0, 0.0).astype(bf16)
    picked = jnp.zeros((8, count), f32)
    for part in range(4):
        lines = jnp.dot(table_ref[pl.ds(part * 256, 256), :], hot, preferred_element_type=f32)
        for k in range(32):
            picked = jnp.where(lower == part * 32 + k, lines[k * 8 : (k + 1) * 8, :], picked)
    for copy in range(out_ref.shape[1]):
        out_ref[0, copy] = picked.astype(bf16)


def pick_tokens(ids, table):
    chips, _, count = ids.shape
    return pl.pallas_call(
        pick_kernel,
        grid=(chips,),
        in_specs=[
            pl.BlockSpec((1, 1, count), lambda i: (i, 0, 0)),
            pl.BlockSpec((1024, UPPER), lambda i: (0, 0)),
        ],
        out_specs=pl.BlockSpec((1, 4, 8, count), lambda i: (i, 0, 0, 0)),
        out_shape=jax.ShapeDtypeStruct((chips, 4, 8, count), bf16),
        cost_estimate=pl.CostEstimate(
            flops=2 * 1024 * UPPER * chips * count, bytes_accessed=1 << 21, transcendentals=0
        ),
        name="pick_tokens",
    )(ids, table)


def turn_tokens_kernel(place_ref, in_ref, out_ref, square_ref):
    @pl.when(pl.program_id(0) == 0)
    def _():
        square_ref[...] = jnp.zeros_like(square_ref)

    for line in range(2):
        rows = [
            in_ref[t, 0, line, (place_ref[0] + 4 - k) % 4].astype(f32)
            for k in range(4)
            for t in range(4)
        ]
        turned = jnp.concatenate(rows, axis=0).T
        square_ref[...] += turned * turned
        out_ref[:, pl.ds(line * 128, 128)] = turned.astype(bf16)


def turn_tokens(place, stacked):
    count = stacked.shape[-1]
    return pl.pallas_call(
        turn_tokens_kernel,
        grid_spec=pltpu.PrefetchScalarGridSpec(
            num_scalar_prefetch=1,
            grid=(8,),
            in_specs=[pl.BlockSpec((4, 1, 2, 4, 8, count), lambda i, place: (0, i, 0, 0, 0, 0))],
            out_specs=(
                pl.BlockSpec((count, 256), lambda i, place: (0, i)),
                pl.BlockSpec((count, 128), lambda i, place: (0, 0)),
            ),
        ),
        out_shape=(
            jax.ShapeDtypeStruct((count, 2048), bf16),
            jax.ShapeDtypeStruct((count, 128), f32),
        ),
        cost_estimate=pl.CostEstimate(flops=1 << 21, bytes_accessed=1 << 23, transcendentals=0),
        name="turn_tokens",
    )(place, stacked)


def hidden_kernel(group_ref, place_ref, side_ref, square_ref, *refs):
    pieces, (out_ref, rows, sems) = refs[:-3], refs[-3:]
    copies = []
    for piece in pieces:
        for j in range(piece.shape[0]):
            start = pl.multiple_of(place_ref[len(copies)] * 128, 128)
            copies.append(
                pltpu.make_async_copy(piece.at[j], rows.at[pl.ds(start, 128)], sems.at[len(copies)])
            )
            copies[-1].start()
    out_ref[:, WIDTH:] = square_ref[...]
    for copy in copies:
        copy.wait()
    out_ref[:, :WIDTH] = jnp.dot(side_ref[...], rows[...], preferred_element_type=f32)


def partial_hidden(place, group, side, square, pieces):
    total = sum(piece.shape[0] for piece in pieces)
    return pl.pallas_call(
        hidden_kernel,
        grid_spec=pltpu.PrefetchScalarGridSpec(
            num_scalar_prefetch=2,
            grid=(1,),
            in_specs=[
                pl.BlockSpec((TOKENS, 2048), lambda i, group, place: (group[0], 0)),
                pl.BlockSpec((TOKENS, 128), lambda i, group, place: (group[0], 0)),
            ]
            + [pl.BlockSpec(memory_space=pl.ANY)] * len(pieces),
            out_specs=pl.BlockSpec((TOKENS, 1024), lambda i, group, place: (0, 0)),
            scratch_shapes=[VMEM((2048, WIDTH), bf16), pltpu.SemaphoreType.DMA((total,))],
        ),
        out_shape=jax.ShapeDtypeStruct((TOKENS, 1024), f32),
        cost_estimate=pl.CostEstimate(
            flops=2 * TOKENS * 2048 * WIDTH, bytes_accessed=6 << 20, transcendentals=0
        ),
        name="partial_hidden",
    )(group, place, side, square, *pieces)


def label_kernel(own_ref, other_ref, pair_ref, head_ref, out_ref):
    both = own_ref[...] + other_ref[...]
    mean = jnp.sum(both[:, WIDTH:], axis=1, keepdims=True) / 4096.0
    hidden = both[:, :WIDTH] * lax.rsqrt(mean + 1e-05)
    active = hidden / (1.0 + jnp.exp(-hidden))
    pairs = lax.broadcasted_iota(jnp.int32, (PAIRS, TOKENS), 0)
    member = jnp.where(pair_ref[...] == pairs, 1.0, 0.0)
    hot = member.astype(bf16)
    dot = functools.partial(jnp.dot, preferred_element_type=f32)
    first = active.astype(bf16)
    rest = active - first.astype(f32)
    second = rest.astype(bf16)
    third = (rest - second.astype(f32)).astype(bf16)
    totals = dot(hot, first) + (dot(hot, second) + dot(hot, third))
    pooled = (totals / jnp.sum(member, axis=1, keepdims=True)).astype(bf16)
    out_ref[...] = dot(pooled, head_ref[...])


def label_pairs(own, other, pairs, head):
    return pl.pallas_call(
        label_kernel,
        out_shape=jax.ShapeDtypeStruct((PAIRS, 256), f32),
        in_specs=[pl.BlockSpec(memory_space=VMEM)] * 4,
        out_specs=pl.BlockSpec(memory_space=VMEM),
        cost_estimate=pl.CostEstimate(
            flops=2 * 32 * TOKENS * WIDTH, bytes_accessed=3 << 20, transcendentals=TOKENS * WIDTH
        ),
        name="label_pairs",
    )(own, other, pairs, head)


def send_columns(columns):
    got = [columns[0]]
    for hop in range(1, 4):
        got.append(lax.ppermute(columns[hop], "dp", [(i, (i + hop) % 4) for i in range(4)]))
    return jnp.concatenate(got)[None]


def exchange_rows(block):
    count = 8
    up = [(i, i ^ 1) for i in range(count)]
    down = [(i, (i - 1) % count) if i % 2 == 0 else (i, (i + 1) % count) for i in range(count)]
    z, line = lax.axis_index("z"), lax.axis_index("yl")
    sign = 1 - 2 * (z % 2)
    halves = [block, lax.ppermute(block, "yl", [(0, 1), (1, 0)])]
    lines = [line, 1 - line]
    pieces, places = [], []
    last = list(halves)
    for half in range(2):
        pieces.append(halves[half])
        places.append(z * 2 + lines[half])
    for step in range(4):
        for half in range(2):
            got = lax.ppermute(last[half], "z", up if (step + half) % 2 == 0 else down)
            way = sign if half == 0 else -sign
            offsets = ((1,), (-1, -2), (2, 3), (-3, -4))[step]
            pieces.append(got)
            places += [((z + way * k + 16) % count) * 2 + lines[half] for k in offsets]
            last[half] = jnp.concatenate([halves[half], got]) if step == 0 else got
    return pieces, jnp.stack(places).astype(jnp.int32)


def shards(
    master_weight,
    first_moment,
    second_moment,
    teacher_weight,
    grad_parts,
    embed_table,
    token_ids,
    pair_ids,
    class_head,
):
    every_id = lax.all_to_all(
        jnp.broadcast_to(token_ids[None], (32, 1, TOKENS)), ("z", "yl", "c"), 0, 0, tiled=True
    )
    parts = lax.all_to_all(grad_parts.reshape(4, 32, -1), "dp", 0, 0, tiled=True)
    table = turn_table(embed_table)
    picked = pick_tokens(every_id.reshape(16, 1, 2 * TOKENS), table)
    received = lax.all_to_all(
        picked.reshape(64, 8, 2 * TOKENS), ("z", "yl", "dp"), 0, 0, tiled=True
    )
    place = lax.axis_index("dp").astype(jnp.int32).reshape(1)
    master_new, first_new, second_new, teacher_new, columns = optimizer_step(
        place, master_weight, first_moment, second_moment, teacher_weight, parts
    )
    block = send_columns(columns)
    stacked = lax.all_to_all(
        jnp.broadcast_to(received[None], (4, 64, 8, 2 * TOKENS)), "t", 0, 0, tiled=True
    )
    side, square = turn_tokens(place, stacked.reshape(4, 8, 2, 4, 8, 2 * TOKENS))
    pieces, places = exchange_rows(block)
    core = lax.axis_index("c").astype(jnp.int32).reshape(1)
    sent = partial_hidden(places, 1 - core, side, square, pieces)
    other = lax.ppermute(sent, "c", [(0, 1), (1, 0)])
    own = partial_hidden(places, core, side, square, pieces)
    terms = label_pairs(own, other, pair_ids, class_head[0])
    every_term = lax.all_to_all(
        jnp.broadcast_to(terms[None], (16, PAIRS, 256)), ("dp", "t"), 0, 0, tiled=True
    )
    class_logits = jnp.sum(every_term, axis=0, keepdims=True)
    return (master_new, first_new, second_new, teacher_new, class_logits)


def solution(mesh):
    fine = Mesh(mesh.devices.reshape(8, 2, 2, 4, 4), ("z", "yl", "c", "dp", "t"))
    fsdp = ("z", "yl", "c")
    rows = P(fsdp + ("dp",), "t")
    return jax.shard_map(
        shards,
        mesh=fine,
        in_specs=(
            rows,
            rows,
            rows,
            rows,
            P("dp", fsdp, "t"),
            P(fsdp + ("dp", "t"), None),
            P(fsdp, None),
            P(fsdp, None),
            P("t", "dp", None),
        ),
        out_specs=(rows, rows, rows, rows, P(fsdp, None, None)),
        check_vma=False,
    )
```

time: 422 us -> 183 us (0.43)
  the two profiles are of different devices: /device:TPU:64 before, /device:TPU:1 now
where the time goes in v2:
time: 183 us; the launch traced here: 181 us
  starting transfers between devices  64.2 us (35%)
  Pallas kernels  44.7 us (24%)
  blocking collectives  42.1 us (23%)
  waiting for transfers between devices  21.6 us (12%)
  local copies, waits for them, and re-layouts  6.85 us (4%)
    ppermute x8, starting transfers between devices, exchange_rows(): got = lax.ppermute(last[half], 'z', up if (step + half) % 2 == 0 else down)  24.4 us
    all_to_all x1, blocking collectives, shards(): lax.all_to_all(jnp.broadcast_to(terms[None], (16, PAIRS, 256)), ('dp', 't...  21.1 us
    all_to_all x1, blocking collectives, shards(): lax.all_to_all(jnp.broadcast_to(token_ids[None], (32, 1, TOKENS)), ('z',...  21 us
    pallas_call x1, Pallas kernels, pick_tokens(): pl.pallas_call(pick_kernel, grid=(chips,), in_specs=[pl.BlockSpec((1, 1,...  13.8 us
    ppermute x8, waiting for transfers between devices, exchange_rows(): got = lax.ppermute(last[half], 'z', up if (step + half) % 2 == 0 else down)  13.3 us
    ppermute x3, starting transfers between devices, send_columns(): lax.ppermute(columns[hop], 'dp', [(i, (i + hop) % 4) for i in range(4)])  13 us
    pallas_call x2, Pallas kernels, partial_hidden(): pl.pallas_call(hidden_kernel, grid_spec=pltpu.PrefetchScalarGridSpec(num_...  12.8 us
    ppermute x1, starting transfers between devices, shards(): other = lax.ppermute(sent, 'c', [(0, 1), (1, 0)])  7.27 us
  transfers between devices with their start and end apart: 16, of which 7 were waited for; matrix products, arithmetic and copies ran while one was open for 2% of the time, Pallas kernels for 19%

profile of v2, /device:TPU:1, one launch (start us, length us, event | category | flops | bytes accessed | tf_op | source)
XLA Modules:
  0.0 181.4 jit_solution(14982346590218140802)
XLA Ops:
  1.3 21.0 %all_to_all.25 = s32[32,1,256]{2,1,0:T(1,128)} all-to-all(s32[32,1,256]{2,1,0:T(1,128)S(1)} %broadcast_in_dim.13), channel_id=1, replica_groups=mesh['z'=8,'yl'=2,'c'=2,'dp'=4,'t'=4] {'z','yl','c'}, dimensions={0} | all-to-all | bytes 65536 | tf_op jit(solution)/shard_map/all_to_all | solution.py:281
  22.3 5.9 %all-to-all-start = ((bf16[4,32,3584]{2,1,0:T(8,128)(2,1)}), bf16[4,32,3584]{2,1,0:T(8,128)(2,1)S(1)}, u32[]{:S(2)}, u32[]{:S(2)}) async-start(bf16[4,32,3584]{2,1,0:T(8,128)(2,1)} %bitcast.40), calls=%async_computation | async-start | bytes 1835008 | tf_op jit(solution)/shard_map/all_to_all | solution.py:284
  28.3 4.7 %turn_table.1.table_ref = bf16[1024,512]{1,0:T(8,128)(2,1)} custom-call(bf16[501,8,128]{2,1,0:T(8,128)(2,1)} %bitcast.39), custom_call_target="tpu_custom_call" | custom-call | bytes 16777216 | tf_op jit(solution)/shard_map/turn_table/pallas_call | solution.py:86
  33.0 13.8 %pick_tokens.1 = bf16[16,4,8,512]{3,2,1,0:T(8,128)(2,1)} custom-call(s32[16,1,512]{2,1,0:T(1,128)} %bitcast.43, bf16[1024,512]{1,0:T(8,128)(2,1)} %turn_table.1.table_ref), custom_call_target="tpu_custom_call" | custom-call | flops 8589934592 | bytes 2097152 | tf_op jit(solution)/shard_map/pick_tokens/pallas_call | solution.py:115
  46.8 4.6 %all-to-all-done.parts_ref = bf16[4,32,3584]{2,1,0:T(8,128)(2,1)S(1)} async-done(((bf16[4,32,3584]{2,1,0:T(8,128)(2,1)}), bf16[4,32,3584]{2,1,0:T(8,128)(2,1)S(1)}, u32[]{:S(2)}, u32[]{:S(2)}) %all-to-all-start) | async-done | bytes 917536 | tf_op jit(solution)/shard_map/all_to_all | solution.py:284
  51.4 5.6 %all-to-all-start.2 = ((bf16[64,8,512]{2,1,0:T(8,128)(2,1)}), bf16[64,8,512]{2,1,0:T(8,128)(2,1)S(1)}, u32[]{:S(2)}, u32[]{:S(2)}) async-start(bf16[64,8,512]{2,1,0:T(8,128)(2,1)} %bitcast.41), calls=%async_computation.2 | async-start | bytes 1048576 | tf_op jit(solution)/shard_map/all_to_all | solution.py:287
  57.1 4.0 %optimizer_step.1 = (f32[32,3584]{1,0:T(8,128)}, bf16[32,3584]{1,0:T(8,128)(2,1)}, bf16[32,3584]{1,0:T(8,128)(2,1)}, f32[32,3584]{1,0:T(8,128)}, bf16[4,32,896]{2,1,0:T(8,128)(2,1)}) custom-call(s32[1]{0:T(128)} %bitcast.place_ref, f32[32,3584]{1,0:T(8,128)} %master_ref.1, bf16[32,3584]{1,0:T(8,128)(2,1)} %first_ref.1, bf16[32,3584]{1,0:T(8,128)(2,1)} %second_ref.1, ...), custom_call_target="tpu_custom_call" | custom-call | flops 2097152 | bytes 8388608 | tf_op jit(solution)/shard_map/optimizer_step/pallas_call | solution.py:53
  61.9 5.0 %collective-permute-start.2 = (bf16[32,896]{1,0:T(8,128)(2,1)S(1)}, bf16[32,896]{1,0:T(8,128)(2,1)S(1)}, u32[]{:S(2)}, u32[]{:S(2)}) collective-permute-start(bf16[32,896]{1,0:T(8,128)(2,1)S(1)} %get-tuple-element.20), channel_id=1, source_target_pairs={{0,12},{4,0},{8,4},{12,8},{1,13},{5,1},{9,5},{13,9},{2,14},{6,2},{... | collective-permute-start | bytes 172040 | tf_op jit(solution)/shard_map/ppermute | solution.py:242
  67.0 4.0 %collective-permute-start.1 = (bf16[32,896]{1,0:T(8,128)(2,1)S(1)}, bf16[32,896]{1,0:T(8,128)(2,1)S(1)}, u32[]{:S(2)}, u32[]{:S(2)}) collective-permute-start(bf16[32,896]{1,0:T(8,128)(2,1)S(1)} %get-tuple-element.21), channel_id=1, source_target_pairs={{0,8},{4,12},{8,0},{12,4},{1,9},{5,13},{9,1},{13,5},{2,10},{6,14},... | collective-permute-start | bytes 172040 | tf_op jit(solution)/shard_map/ppermute | solution.py:242
  71.0 4.0 %collective-permute-start = (bf16[32,896]{1,0:T(8,128)(2,1)S(1)}, bf16[32,896]{1,0:T(8,128)(2,1)S(1)}, u32[]{:S(2)}, u32[]{:S(2)}) collective-permute-start(bf16[32,896]{1,0:T(8,128)(2,1)S(1)} %get-tuple-element.22), channel_id=1, source_target_pairs={{0,4},{4,8},{8,12},{12,0},{1,5},{5,9},{9,13},{13,1},{2,6},{6,10},{... | collective-permute-start | bytes 172040 | tf_op jit(solution)/shard_map/ppermute | solution.py:242
  75.0 1.1 collective-permute-done.1
  76.1 2.3 %collective-permute-done = bf16[32,896]{1,0:T(8,128)(2,1)S(1)} collective-permute-done((bf16[32,896]{1,0:T(8,128)(2,1)S(1)}, bf16[32,896]{1,0:T(8,128)(2,1)S(1)}, u32[]{:S(2)}, u32[]{:S(2)}) %collective-permute-start) | collective-permute-done | bytes 57376 | tf_op jit(solution)/shard_map/ppermute | solution.py:242
  78.4 3.9 %collective-permute-start.3 = (bf16[1,128,896]{2,1,0:T(8,128)(2,1)S(1)}, bf16[1,128,896]{2,1,0:T(8,128)(2,1)S(1)}, u32[]{:S(2)}, u32[]{:S(2)}) collective-permute-start(bf16[1,128,896]{2,1,0:T(8,128)(2,1)S(1)} %maximum_bitcast_fusion.refs_0_), channel_id=1, source_target_pairs={{0,32},{32,0},{1,33},{33,1},{2,34},{34,2},{3,35},{35,3},{4,36},{36... | collective-permute-start | bytes 688136 | tf_op jit(solution)/shard_map/ppermute | solution.py:252
  82.3 3.1 %collective-permute-start.4 = (bf16[1,128,896]{2,1,0:T(8,128)(2,1)S(1)}, bf16[1,128,896]{2,1,0:T(8,128)(2,1)S(1)}, u32[]{:S(2)}, u32[]{:S(2)}) collective-permute-start(bf16[1,128,896]{2,1,0:T(8,128)(2,1)S(1)} %maximum_bitcast_fusion.refs_0_), channel_id=1, source_target_pairs={{0,64},{64,0},{128,192},{192,128},{256,320},{320,256},{384,448},{4... | collective-permute-start | bytes 688136 | tf_op jit(solution)/shard_map/ppermute | solution.py:261
  85.7 4.6 %collective-permute-start.5 = (bf16[1,128,896]{2,1,0:T(8,128)(2,1)S(1)}, bf16[1,128,896]{2,1,0:T(8,128)(2,1)S(1)}, u32[]{:S(2)}, u32[]{:S(2)}) collective-permute-start(bf16[1,128,896]{2,1,0:T(8,128)(2,1)S(1)} %collective-permute-done.3.refs_1_), channel_id=1, source_target_pairs={{0,448},{64,128},{128,64},{192,256},{256,192},{320,384},{384,320},... | collective-permute-start | bytes 688136 | tf_op jit(solution)/shard_map/ppermute | solution.py:261
  90.3 1.5 broadcast_in_dim.28
  91.8 4.0 %all-to-all-start.3 = ((bf16[4,64,8,512]{3,2,1,0:T(8,128)(2,1)}), bf16[4,64,8,512]{3,2,1,0:T(8,128)(2,1)S(1)}, u32[]{:S(2)}, u32[]{:S(2)}) async-start(bf16[4,64,8,512]{3,2,1,0:T(8,128)(2,1)} %broadcast_in_dim.28), calls=%async_computation.3 | async-start | bytes 4194304 | tf_op jit(solution)/shard_map/all_to_all | solution.py:295
  95.9 1.9 %collective-permute-start.6 = (bf16[2,128,896]{2,1,0:T(8,128)(2,1)S(1)}, bf16[2,128,896]{2,1,0:T(8,128)(2,1)S(1)}, u32[]{:S(2)}, u32[]{:S(2)}) collective-permute-start(bf16[2,128,896]{2,1,0:T(8,128)(2,1)S(1)} %pad_maximum_fusion), channel_id=1, source_target_pairs={{0,448},{64,128},{128,64},{192,256},{256,192},{320,384},{384,320},... | collective-permute-start | bytes 1376264 | tf_op jit(solution)/shard_map/ppermute | solution.py:261
  97.9 1.9 %collective-permute-start.7 = (bf16[2,128,896]{2,1,0:T(8,128)(2,1)S(1)}, bf16[2,128,896]{2,1,0:T(8,128)(2,1)S(1)}, u32[]{:S(2)}, u32[]{:S(2)}) collective-permute-start(bf16[2,128,896]{2,1,0:T(8,128)(2,1)S(1)} %pad_maximum_fusion.1), channel_id=1, source_target_pairs={{0,64},{64,0},{128,192},{192,128},{256,320},{320,256},{384,448},{4... | collective-permute-start | bytes 1376264 | tf_op jit(solution)/shard_map/ppermute | solution.py:261
  99.9 7.3 %collective-permute-done.6.refs_4_ = bf16[2,128,896]{2,1,0:T(8,128)(2,1)S(1)} collective-permute-done((bf16[2,128,896]{2,1,0:T(8,128)(2,1)S(1)}, bf16[2,128,896]{2,1,0:T(8,128)(2,1)S(1)}, u32[]{:S(2)}, u32[]{:S(2)}) %collective-permute-start.6) | collective-permute-done | bytes 458784 | tf_op jit(solution)/shard_map/ppermute | solution.py:261
  107.2 1.9 %collective-permute-start.8 = (bf16[2,128,896]{2,1,0:T(8,128)(2,1)S(1)}, bf16[2,128,896]{2,1,0:T(8,128)(2,1)}, u32[]{:S(2)}, u32[]{:S(2)}) collective-permute-start(bf16[2,128,896]{2,1,0:T(8,128)(2,1)S(1)} %collective-permute-done.6.refs_4_), channel_id=1, source_target_pairs={{0,64},{64,0},{128,192},{192,128},{256,320},{320,256},{384,448},{4... | collective-permute-start | bytes 1376264 | tf_op jit(solution)/shard_map/ppermute | solution.py:261
  109.1 3.2 %collective-permute-start.9 = (bf16[2,128,896]{2,1,0:T(8,128)(2,1)S(1)}, bf16[2,128,896]{2,1,0:T(8,128)(2,1)}, u32[]{:S(2)}, u32[]{:S(2)}) collective-permute-start(bf16[2,128,896]{2,1,0:T(8,128)(2,1)S(1)} %collective-permute-done.7.refs_5_), channel_id=1, source_target_pairs={{0,448},{64,128},{128,64},{192,256},{256,192},{320,384},{384,320},... | collective-permute-start | bytes 1376264 | tf_op jit(solution)/shard_map/ppermute | solution.py:261
  112.3 5.4 %collective-permute-done.8.refs_6_ = bf16[2,128,896]{2,1,0:T(8,128)(2,1)} collective-permute-done((bf16[2,128,896]{2,1,0:T(8,128)(2,1)S(1)}, bf16[2,128,896]{2,1,0:T(8,128)(2,1)}, u32[]{:S(2)}, u32[]{:S(2)}) %collective-permute-start.8) | collective-permute-done | bytes 458784 | tf_op jit(solution)/shard_map/ppermute | solution.py:261
  117.7 5.9 %collective-permute-start.10 = (bf16[2,128,896]{2,1,0:T(8,128)(2,1)}, bf16[2,128,896]{2,1,0:T(8,128)(2,1)}, u32[]{:S(2)}, u32[]{:S(2)}) collective-permute-start(bf16[2,128,896]{2,1,0:T(8,128)(2,1)} %collective-permute-done.8.refs_6_), channel_id=1, source_target_pairs={{0,448},{64,128},{128,64},{192,256},{256,192},{320,384},{384,320},... | collective-permute-start | bytes 1376264 | tf_op jit(solution)/shard_map/ppermute | solution.py:261
  123.6 1.9 %collective-permute-start.11 = (bf16[2,128,896]{2,1,0:T(8,128)(2,1)}, bf16[2,128,896]{2,1,0:T(8,128)(2,1)}, u32[]{:S(2)}, u32[]{:S(2)}) collective-permute-start(bf16[2,128,896]{2,1,0:T(8,128)(2,1)} %collective-permute-done.9.refs_7_), channel_id=1, source_target_pairs={{0,64},{64,0},{128,192},{192,128},{256,320},{320,256},{384,448},{4... | collective-permute-start | bytes 1376264 | tf_op jit(solution)/shard_map/ppermute | solution.py:261
  126.4 1.3 copy-done
  127.8 6.2 %turn_tokens.1 = (bf16[512,2048]{1,0:T(8,128)(2,1)}, f32[512,128]{1,0:T(8,128)}) custom-call(s32[1]{0:T(128)} %bitcast.place_ref, bf16[4,8,2,4,8,512]{5,4,3,2,1,0:T(8,128)(2,1)} %bitcast.38), custom_call_target="tpu_custom_call" | custom-call | flops 2097152 | bytes 8388608 | tf_op jit(solution)/shard_map/turn_tokens/pallas_call | solution.py:149
  134.6 6.4 %partial_hidden.3 = f32[256,1024]{1,0:T(8,128)} custom-call(s32[1]{0:T(128)S(6)} %sub.11.group_ref, s32[16]{0:T(128)} %stack.67.place_ref, bf16[512,2048]{1,0:T(8,128)(2,1)} %get-tuple-element.16.side_ref, f32[512,128]{1,0:T(8,128)} %get-tuple-element.17.square_ref, bf16[1,128,896]{2,1,0:T(8,128)(2,1)} %copy-done.2, bf16[1,128,896]{2,1,0:T(8,128)(2,1)} %copy-done.3, ...), custom_call_target="tpu_custom_call" | custom-call | flops 939524096 | bytes 6291456 | tf_op jit(solution)/shard_map/partial_hidden/pallas_call | solution.py:187
  141.0 7.3 %collective-permute-start.12 = (f32[256,1024]{1,0:T(8,128)}, f32[256,1024]{1,0:T(8,128)S(1)}, u32[]{:S(2)}, u32[]{:S(2)}) collective-permute-start(f32[256,1024]{1,0:T(8,128)} %partial_hidden.3), channel_id=1, source_target_pairs={{0,16},{16,0},{1,17},{17,1},{2,18},{18,2},{3,19},{19,3},{4,20},{20... | collective-permute-start | bytes 3145736 | tf_op jit(solution)/shard_map/ppermute | solution.py:302
  148.3 6.4 %partial_hidden.2.own_ref = f32[256,1024]{1,0:T(8,128)} custom-call(s32[1]{0:T(128)} %bitcast.2.group_ref, s32[16]{0:T(128)} %stack.67.place_ref, bf16[512,2048]{1,0:T(8,128)(2,1)} %get-tuple-element.16.side_ref, f32[512,128]{1,0:T(8,128)} %get-tuple-element.17.square_ref, bf16[1,128,896]{2,1,0:T(8,128)(2,1)} %copy-done.2, bf16[1,128,896]{2,1,0:T(8,128)(2,1)} %copy-done.3, ...), custom_call_target="tpu_custom_call" | custom-call | flops 939524096 | bytes 6291456 | tf_op jit(solution)/shard_map/partial_hidden/pallas_call | solution.py:187
  155.7 3.2 %label_pairs.1 = f32[8,256]{1,0:T(8,128)} custom-call(f32[256,1024]{1,0:T(8,128)} %partial_hidden.2.own_ref, f32[256,1024]{1,0:T(8,128)} %copy-done.8, s32[1,256]{1,0:T(1,128)} %pair_ref.1, bf16[896,256]{1,0:T(8,128)(2,1)} %bitcast.42), custom_call_target="tpu_custom_call" | custom-call | flops 14680064 | bytes 3145728 | tf_op jit(solution)/shard_map/label_pairs/pallas_call | solution.py:227
  159.6 21.1 %all_to_all.26 = f32[16,8,256]{2,1,0:T(8,128)S(1)} all-to-all(f32[16,8,256]{2,1,0:T(8,128)S(1)} %broadcast_in_dim.30), channel_id=1, replica_groups=mesh['z'=8,'yl'=2,'c'=2,'dp'=4,'t'=4] {'dp','t'}, dimensions={0} | all-to-all | bytes 262144 | tf_op jit(solution)/shard_map/all_to_all | solution.py:305
  (36 shorter events, 5.7 us)
Async XLA Ops:
  22.3 29.1 %all-to-all-start = ((bf16[4,32,3584]{2,1,0:T(8,128)(2,1)}), bf16[4,32,3584]{2,1,0:T(8,128)(2,1)S(1)}, u32[]{:S(2)}, u32[]{:S(2)}) async-start(bf16[4,32,3584]{2,1,0:T(8,128)(2,1)} %bitcast.40), calls=%async_computation | async-start | bytes 1835008 | tf_op jit(solution)/shard_map/all_to_all | solution.py:284
  51.4 5.7 %copy-start.1 = (bf16[4,32,3584]{2,1,0:T(8,128)(2,1)}, bf16[4,32,3584]{2,1,0:T(8,128)(2,1)S(1)}, u32[]{:S(2)}) copy-start(bf16[4,32,3584]{2,1,0:T(8,128)(2,1)S(1)} %all-to-all-done.parts_ref) | copy-start | bytes 2752516
  51.4 38.9 %all-to-all-start.2 = ((bf16[64,8,512]{2,1,0:T(8,128)(2,1)}), bf16[64,8,512]{2,1,0:T(8,128)(2,1)S(1)}, u32[]{:S(2)}, u32[]{:S(2)}) async-start(bf16[64,8,512]{2,1,0:T(8,128)(2,1)} %bitcast.41), calls=%async_computation.2 | async-start | bytes 1048576 | tf_op jit(solution)/shard_map/all_to_all | solution.py:287
  61.9 13.0 %collective-permute-start.2 = (bf16[32,896]{1,0:T(8,128)(2,1)S(1)}, bf16[32,896]{1,0:T(8,128)(2,1)S(1)}, u32[]{:S(2)}, u32[]{:S(2)}) collective-permute-start(bf16[32,896]{1,0:T(8,128)(2,1)S(1)} %get-tuple-element.20), channel_id=1, source_target_pairs={{0,12},{4,0},{8,4},{12,8},{1,13},{5,1},{9,5},{13,9},{2,14},{6,2},{... | collective-permute-start | bytes 172040 | tf_op jit(solution)/shard_map/ppermute | solution.py:242
  67.0 9.1 %collective-permute-start.1 = (bf16[32,896]{1,0:T(8,128)(2,1)S(1)}, bf16[32,896]{1,0:T(8,128)(2,1)S(1)}, u32[]{:S(2)}, u32[]{:S(2)}) collective-permute-start(bf16[32,896]{1,0:T(8,128)(2,1)S(1)} %get-tuple-element.21), channel_id=1, source_target_pairs={{0,8},{4,12},{8,0},{12,4},{1,9},{5,13},{9,1},{13,5},{2,10},{6,14},... | collective-permute-start | bytes 172040 | tf_op jit(solution)/shard_map/ppermute | solution.py:242
  71.0 7.4 %collective-permute-start = (bf16[32,896]{1,0:T(8,128)(2,1)S(1)}, bf16[32,896]{1,0:T(8,128)(2,1)S(1)}, u32[]{:S(2)}, u32[]{:S(2)}) collective-permute-start(bf16[32,896]{1,0:T(8,128)(2,1)S(1)} %get-tuple-element.22), channel_id=1, source_target_pairs={{0,4},{4,8},{8,12},{12,0},{1,5},{5,9},{9,13},{13,1},{2,6},{6,10},{... | collective-permute-start | bytes 172040 | tf_op jit(solution)/shard_map/ppermute | solution.py:242
  78.4 17.4 %copy-start.2 = (bf16[1,128,896]{2,1,0:T(8,128)(2,1)}, bf16[1,128,896]{2,1,0:T(8,128)(2,1)S(1)}, u32[]{:S(2)}) copy-start(bf16[1,128,896]{2,1,0:T(8,128)(2,1)S(1)} %maximum_bitcast_fusion.refs_0_) | copy-start | bytes 688132
  78.4 7.3 %collective-permute-start.3 = (bf16[1,128,896]{2,1,0:T(8,128)(2,1)S(1)}, bf16[1,128,896]{2,1,0:T(8,128)(2,1)S(1)}, u32[]{:S(2)}, u32[]{:S(2)}) collective-permute-start(bf16[1,128,896]{2,1,0:T(8,128)(2,1)S(1)} %maximum_bitcast_fusion.refs_0_), channel_id=1, source_target_pairs={{0,32},{32,0},{1,33},{33,1},{2,34},{34,2},{3,35},{35,3},{4,36},{36... | collective-permute-start | bytes 688136 | tf_op jit(solution)/shard_map/ppermute | solution.py:252
  82.3 13.5 %collective-permute-start.4 = (bf16[1,128,896]{2,1,0:T(8,128)(2,1)S(1)}, bf16[1,128,896]{2,1,0:T(8,128)(2,1)S(1)}, u32[]{:S(2)}, u32[]{:S(2)}) collective-permute-start(bf16[1,128,896]{2,1,0:T(8,128)(2,1)S(1)} %maximum_bitcast_fusion.refs_0_), channel_id=1, source_target_pairs={{0,64},{64,0},{128,192},{192,128},{256,320},{320,256},{384,448},{4... | collective-permute-start | bytes 688136 | tf_op jit(solution)/shard_map/ppermute | solution.py:261
  85.7 12.1 %copy-start.3 = (bf16[1,128,896]{2,1,0:T(8,128)(2,1)}, bf16[1,128,896]{2,1,0:T(8,128)(2,1)S(1)}, u32[]{:S(2)}) copy-start(bf16[1,128,896]{2,1,0:T(8,128)(2,1)S(1)} %collective-permute-done.3.refs_1_) | copy-start | bytes 688132
  85.7 12.1 %collective-permute-start.5 = (bf16[1,128,896]{2,1,0:T(8,128)(2,1)S(1)}, bf16[1,128,896]{2,1,0:T(8,128)(2,1)S(1)}, u32[]{:S(2)}, u32[]{:S(2)}) collective-permute-start(bf16[1,128,896]{2,1,0:T(8,128)(2,1)S(1)} %collective-permute-done.3.refs_1_), channel_id=1, source_target_pairs={{0,448},{64,128},{128,64},{192,256},{256,192},{320,384},{384,320},... | collective-permute-start | bytes 688136 | tf_op jit(solution)/shard_map/ppermute | solution.py:261
  91.8 34.6 %all-to-all-start.3 = ((bf16[4,64,8,512]{3,2,1,0:T(8,128)(2,1)}), bf16[4,64,8,512]{3,2,1,0:T(8,128)(2,1)S(1)}, u32[]{:S(2)}, u32[]{:S(2)}) async-start(bf16[4,64,8,512]{3,2,1,0:T(8,128)(2,1)} %broadcast_in_dim.28), calls=%async_computation.3 | async-start | bytes 4194304 | tf_op jit(solution)/shard_map/all_to_all | solution.py:295
  95.8 38.1 %copy-start.4 = (bf16[1,128,896]{2,1,0:T(8,128)(2,1)}, bf16[1,128,896]{2,1,0:T(8,128)(2,1)S(1)}, u32[]{:S(2)}) copy-start(bf16[1,128,896]{2,1,0:T(8,128)(2,1)S(1)} %collective-permute-done.4.refs_2_) | copy-start | bytes 688132
  95.9 11.2 %collective-permute-start.6 = (bf16[2,128,896]{2,1,0:T(8,128)(2,1)S(1)}, bf16[2,128,896]{2,1,0:T(8,128)(2,1)S(1)}, u32[]{:S(2)}, u32[]{:S(2)}) collective-permute-start(bf16[2,128,896]{2,1,0:T(8,128)(2,1)S(1)} %pad_maximum_fusion), channel_id=1, source_target_pairs={{0,448},{64,128},{128,64},{192,256},{256,192},{320,384},{384,320},... | collective-permute-start | bytes 1376264 | tf_op jit(solution)/shard_map/ppermute | solution.py:261
  97.9 36.8 %copy-start.5 = (bf16[1,128,896]{2,1,0:T(8,128)(2,1)}, bf16[1,128,896]{2,1,0:T(8,128)(2,1)S(1)}, u32[]{:S(2)}) copy-start(bf16[1,128,896]{2,1,0:T(8,128)(2,1)S(1)} %collective-permute-done.5.refs_3_) | copy-start | bytes 688132
  97.9 11.1 %collective-permute-start.7 = (bf16[2,128,896]{2,1,0:T(8,128)(2,1)S(1)}, bf16[2,128,896]{2,1,0:T(8,128)(2,1)S(1)}, u32[]{:S(2)}, u32[]{:S(2)}) collective-permute-start(bf16[2,128,896]{2,1,0:T(8,128)(2,1)S(1)} %pad_maximum_fusion.1), channel_id=1, source_target_pairs={{0,64},{64,0},{128,192},{192,128},{256,320},{320,256},{384,448},{4... | collective-permute-start | bytes 1376264 | tf_op jit(solution)/shard_map/ppermute | solution.py:261
  107.2 27.5 %copy-start.6 = (bf16[2,128,896]{2,1,0:T(8,128)(2,1)}, bf16[2,128,896]{2,1,0:T(8,128)(2,1)S(1)}, u32[]{:S(2)}) copy-start(bf16[2,128,896]{2,1,0:T(8,128)(2,1)S(1)} %collective-permute-done.6.refs_4_) | copy-start | bytes 1376260
  107.2 10.5 %collective-permute-start.8 = (bf16[2,128,896]{2,1,0:T(8,128)(2,1)S(1)}, bf16[2,128,896]{2,1,0:T(8,128)(2,1)}, u32[]{:S(2)}, u32[]{:S(2)}) collective-permute-start(bf16[2,128,896]{2,1,0:T(8,128)(2,1)S(1)} %collective-permute-done.6.refs_4_), channel_id=1, source_target_pairs={{0,64},{64,0},{128,192},{192,128},{256,320},{320,256},{384,448},{4... | collective-permute-start | bytes 1376264 | tf_op jit(solution)/shard_map/ppermute | solution.py:261
  109.1 25.5 %copy-start.7 = (bf16[2,128,896]{2,1,0:T(8,128)(2,1)}, bf16[2,128,896]{2,1,0:T(8,128)(2,1)S(1)}, u32[]{:S(2)}) copy-start(bf16[2,128,896]{2,1,0:T(8,128)(2,1)S(1)} %collective-permute-done.7.refs_5_) | copy-start | bytes 1376260
  109.1 14.5 %collective-permute-start.9 = (bf16[2,128,896]{2,1,0:T(8,128)(2,1)S(1)}, bf16[2,128,896]{2,1,0:T(8,128)(2,1)}, u32[]{:S(2)}, u32[]{:S(2)}) collective-permute-start(bf16[2,128,896]{2,1,0:T(8,128)(2,1)S(1)} %collective-permute-done.7.refs_5_), channel_id=1, source_target_pairs={{0,448},{64,128},{128,64},{192,256},{256,192},{320,384},{384,320},... | collective-permute-start | bytes 1376264 | tf_op jit(solution)/shard_map/ppermute | solution.py:261
  117.7 16.9 %collective-permute-start.10 = (bf16[2,128,896]{2,1,0:T(8,128)(2,1)}, bf16[2,128,896]{2,1,0:T(8,128)(2,1)}, u32[]{:S(2)}, u32[]{:S(2)}) collective-permute-start(bf16[2,128,896]{2,1,0:T(8,128)(2,1)} %collective-permute-done.8.refs_6_), channel_id=1, source_target_pairs={{0,448},{64,128},{128,64},{192,256},{256,192},{320,384},{384,320},... | collective-permute-start | bytes 1376264 | tf_op jit(solution)/shard_map/ppermute | solution.py:261
  123.6 11.0 %collective-permute-start.11 = (bf16[2,128,896]{2,1,0:T(8,128)(2,1)}, bf16[2,128,896]{2,1,0:T(8,128)(2,1)}, u32[]{:S(2)}, u32[]{:S(2)}) collective-permute-start(bf16[2,128,896]{2,1,0:T(8,128)(2,1)} %collective-permute-done.9.refs_7_), channel_id=1, source_target_pairs={{0,64},{64,0},{128,192},{192,128},{256,320},{320,256},{384,448},{4... | collective-permute-start | bytes 1376264 | tf_op jit(solution)/shard_map/ppermute | solution.py:261
  126.4 1.3 copy-start
  141.0 13.7 %collective-permute-start.12 = (f32[256,1024]{1,0:T(8,128)}, f32[256,1024]{1,0:T(8,128)S(1)}, u32[]{:S(2)}, u32[]{:S(2)}) collective-permute-start(f32[256,1024]{1,0:T(8,128)} %partial_hidden.3), channel_id=1, source_target_pairs={{0,16},{16,0},{1,17},{17,1},{2,18},{18,2},{3,19},{19,3},{4,20},{20... | collective-permute-start | bytes 3145736 | tf_op jit(solution)/shard_map/ppermute | solution.py:302
  154.7 1.0 copy-start.8

commit v3 on v2

--- a/solution.py
+++ b/solution.py
@@ -25,12 +25,10 @@
 
 
 def optimizer_kernel(
-    place_ref, master_ref, first_ref, second_ref, teacher_ref, parts_ref,
+    master_ref, first_ref, second_ref, teacher_ref, gradient_ref,
     master_out, first_out, second_out, teacher_out, columns_out,
 ):
-    gradient = parts_ref[0].astype(f32)
-    for member in range(1, 4):
-        gradient = gradient + parts_ref[member].astype(f32)
+    gradient = gradient_ref[...].astype(f32)
     first_full = beta_one * first_ref[...].astype(f32) + (1.0 - beta_one) * gradient
     second_full = (
         beta_two * second_ref[...].astype(f32) + (1.0 - beta_two) * gradient * gradient
@@ -44,31 +42,28 @@
     first_out[...] = first_full.astype(bf16)
     second_out[...] = second_full.astype(bf16)
     teacher_out[...] = teacher_new
-    columns_out[0] = teacher_new.astype(bf16)
-
-
-def optimizer_step(place, master_weight, first_moment, second_moment, teacher_weight, parts):
-    block = pl.BlockSpec((32, WIDTH), lambda k, place: (0, (place[0] + k) % 4))
+    for line in range(2):
+        columns_out[line, 0] = teacher_new.astype(bf16)
+
+
+def optimizer_step(master_weight, first_moment, second_moment, teacher_weight, gradient):
+    block = pl.BlockSpec((32, WIDTH), lambda k: (0, k))
     shape = master_weight.shape
     return pl.pallas_call(
         optimizer_kernel,
-        grid_spec=pltpu.PrefetchScalarGridSpec(
-            num_scalar_prefetch=1,
-            grid=(4,),
-            in_specs=[block] * 4
-            + [pl.BlockSpec((4, 32, WIDTH), lambda k, place: (0, 0, (place[0] + k) % 4))],
-            out_specs=[block] * 4 + [pl.BlockSpec((1, 32, WIDTH), lambda k, place: (k, 0, 0))],
-        ),
+        grid=(4,),
+        in_specs=[block] * 5,
+        out_specs=[block] * 4 + [pl.BlockSpec((2, 1, 32, WIDTH), lambda k: (0, k, 0, 0))],
         out_shape=[
             jax.ShapeDtypeStruct(shape, f32),
             jax.ShapeDtypeStruct(shape, bf16),
             jax.ShapeDtypeStruct(shape, bf16),
             jax.ShapeDtypeStruct(shape, f32),
-            jax.ShapeDtypeStruct((4, 32, WIDTH), bf16),
+            jax.ShapeDtypeStruct((2, 4, 32, WIDTH), bf16),
         ],
         cost_estimate=pl.CostEstimate(flops=1 << 21, bytes_accessed=1 << 23, transcendentals=0),
         name="optimizer_step",
-    )(place, master_weight, first_moment, second_moment, teacher_weight, parts)
+    )(master_weight, first_moment, second_moment, teacher_weight, gradient)
 
 
 def turn_table_kernel(table_ref, out_ref, wide, turned):
@@ -128,34 +123,29 @@
     )(ids, table)
 
 
-def turn_tokens_kernel(place_ref, in_ref, out_ref, square_ref):
+def turn_tokens_kernel(in_ref, out_ref, square_ref):
     @pl.when(pl.program_id(0) == 0)
     def _():
         square_ref[...] = jnp.zeros_like(square_ref)
 
     for line in range(2):
         rows = [
-            in_ref[t, 0, line, (place_ref[0] + 4 - k) % 4].astype(f32)
-            for k in range(4)
-            for t in range(4)
+            in_ref[t, 0, line, d].astype(f32) for d in range(4) for t in range(4)
         ]
         turned = jnp.concatenate(rows, axis=0).T
         square_ref[...] += turned * turned
         out_ref[:, pl.ds(line * 128, 128)] = turned.astype(bf16)
 
 
-def turn_tokens(place, stacked):
+def turn_tokens(stacked):
     count = stacked.shape[-1]
     return pl.pallas_call(
         turn_tokens_kernel,
-        grid_spec=pltpu.PrefetchScalarGridSpec(
-            num_scalar_prefetch=1,
-            grid=(8,),
-            in_specs=[pl.BlockSpec((4, 1, 2, 4, 8, count), lambda i, place: (0, i, 0, 0, 0, 0))],
-            out_specs=(
-                pl.BlockSpec((count, 256), lambda i, place: (0, i)),
-                pl.BlockSpec((count, 128), lambda i, place: (0, 0)),
-            ),
+        grid=(8,),
+        in_specs=[pl.BlockSpec((4, 1, 2, 4, 8, count), lambda i: (0, i, 0, 0, 0, 0))],
+        out_specs=(
+            pl.BlockSpec((count, 256), lambda i: (0, i)),
+            pl.BlockSpec((count, 128), lambda i: (0, 0)),
         ),
         out_shape=(
             jax.ShapeDtypeStruct((count, 2048), bf16),
@@ -163,46 +153,43 @@
         ),
         cost_estimate=pl.CostEstimate(flops=1 << 21, bytes_accessed=1 << 23, transcendentals=0),
         name="turn_tokens",
-    )(place, stacked)
-
-
-def hidden_kernel(group_ref, place_ref, side_ref, square_ref, *refs):
-    pieces, (out_ref, rows, sems) = refs[:-3], refs[-3:]
-    copies = []
-    for piece in pieces:
-        for j in range(piece.shape[0]):
-            start = pl.multiple_of(place_ref[len(copies)] * 128, 128)
-            copies.append(
-                pltpu.make_async_copy(piece.at[j], rows.at[pl.ds(start, 128)], sems.at[len(copies)])
-            )
-            copies[-1].start()
-    out_ref[:, WIDTH:] = square_ref[...]
-    for copy in copies:
-        copy.wait()
-    out_ref[:, :WIDTH] = jnp.dot(side_ref[...], rows[...], preferred_element_type=f32)
-
-
-def partial_hidden(place, group, side, square, pieces):
-    total = sum(piece.shape[0] for piece in pieces)
+    )(stacked)
+
+
+def hidden_kernel(group_ref, side_ref, square_ref, rows_ref, out_ref):
+    product = jnp.dot(side_ref[...], rows_ref[...], preferred_element_type=f32)
+
+    @pl.when(pl.program_id(0) == 0)
+    def _():
+        out_ref[:, :WIDTH] = product
+        out_ref[:, WIDTH:] = square_ref[...]
+
+    @pl.when(pl.program_id(0) > 0)
+    def _():
+        out_ref[:, :WIDTH] += product
+
+
+def partial_hidden(group, side, square, rows):
+    steps = 4
+    depth = rows.shape[0] // steps
     return pl.pallas_call(
         hidden_kernel,
         grid_spec=pltpu.PrefetchScalarGridSpec(
-            num_scalar_prefetch=2,
-            grid=(1,),
+            num_scalar_prefetch=1,
+            grid=(steps,),
             in_specs=[
-                pl.BlockSpec((TOKENS, 2048), lambda i, group, place: (group[0], 0)),
-                pl.BlockSpec((TOKENS, 128), lambda i, group, place: (group[0], 0)),
-            ]
-            + [pl.BlockSpec(memory_space=pl.ANY)] * len(pieces),
-            out_specs=pl.BlockSpec((TOKENS, 1024), lambda i, group, place: (0, 0)),
-            scratch_shapes=[VMEM((2048, WIDTH), bf16), pltpu.SemaphoreType.DMA((total,))],
+                pl.BlockSpec((TOKENS, depth), lambda i, group: (group[0], i)),
+                pl.BlockSpec((TOKENS, 128), lambda i, group: (group[0], 0)),
+                pl.BlockSpec((depth, WIDTH), lambda i, group: (i, 0)),
+            ],
+            out_specs=pl.BlockSpec((TOKENS, 1024), lambda i, group: (0, 0)),
         ),
         out_shape=jax.ShapeDtypeStruct((TOKENS, 1024), f32),
         cost_estimate=pl.CostEstimate(
             flops=2 * TOKENS * 2048 * WIDTH, bytes_accessed=6 << 20, transcendentals=0
         ),
         name="partial_hidden",
-    )(group, place, side, square, *pieces)
+    )(group, side, square, rows)
 
 
 def label_kernel(own_ref, other_ref, pair_ref, head_ref, out_ref):
@@ -236,37 +223,6 @@
     )(own, other, pairs, head)
 
 
-def send_columns(columns):
-    got = [columns[0]]
-    for hop in range(1, 4):
-        got.append(lax.ppermute(columns[hop], "dp", [(i, (i + hop) % 4) for i in range(4)]))
-    return jnp.concatenate(got)[None]
-
-
-def exchange_rows(block):
-    count = 8
-    up = [(i, i ^ 1) for i in range(count)]
-    down = [(i, (i - 1) % count) if i % 2 == 0 else (i, (i + 1) % count) for i in range(count)]
-    z, line = lax.axis_index("z"), lax.axis_index("yl")
-    sign = 1 - 2 * (z % 2)
-    halves = [block, lax.ppermute(block, "yl", [(0, 1), (1, 0)])]
-    lines = [line, 1 - line]
-    pieces, places = [], []
-    last = list(halves)
-    for half in range(2):
-        pieces.append(halves[half])
-        places.append(z * 2 + lines[half])
-    for step in range(4):
-        for half in range(2):
-            got = lax.ppermute(last[half], "z", up if (step + half) % 2 == 0 else down)
-            way = sign if half == 0 else -sign
-            offsets = ((1,), (-1, -2), (2, 3), (-3, -4))[step]
-            pieces.append(got)
-            places += [((z + way * k + 16) % count) * 2 + lines[half] for k in offsets]
-            last[half] = jnp.concatenate([halves[half], got]) if step == 0 else got
-    return pieces, jnp.stack(places).astype(jnp.int32)
-
-
 def shards(
     master_weight,
     first_moment,
@@ -281,26 +237,25 @@
     every_id = lax.all_to_all(
         jnp.broadcast_to(token_ids[None], (32, 1, TOKENS)), ("z", "yl", "c"), 0, 0, tiled=True
     )
-    parts = lax.all_to_all(grad_parts.reshape(4, 32, -1), "dp", 0, 0, tiled=True)
+    gradient = lax.psum_scatter(grad_parts[0], "dp", scatter_dimension=0, tiled=True)
     table = turn_table(embed_table)
     picked = pick_tokens(every_id.reshape(16, 1, 2 * TOKENS), table)
     received = lax.all_to_all(
         picked.reshape(64, 8, 2 * TOKENS), ("z", "yl", "dp"), 0, 0, tiled=True
     )
-    place = lax.axis_index("dp").astype(jnp.int32).reshape(1)
     master_new, first_new, second_new, teacher_new, columns = optimizer_step(
-        place, master_weight, first_moment, second_moment, teacher_weight, parts
-    )
-    block = send_columns(columns)
+        master_weight, first_moment, second_moment, teacher_weight, gradient
+    )
+    block = lax.all_to_all(columns.reshape(8, 32, WIDTH), ("yl", "dp"), 0, 0, tiled=True)
+    rows = lax.all_gather(block.reshape(256, WIDTH), "z", axis=0, tiled=True)
     stacked = lax.all_to_all(
         jnp.broadcast_to(received[None], (4, 64, 8, 2 * TOKENS)), "t", 0, 0, tiled=True
     )
-    side, square = turn_tokens(place, stacked.reshape(4, 8, 2, 4, 8, 2 * TOKENS))
-    pieces, places = exchange_rows(block)
+    side, square = turn_tokens(stacked.reshape(4, 8, 2, 4, 8, 2 * TOKENS))
     core = lax.axis_index("c").astype(jnp.int32).reshape(1)
-    sent = partial_hidden(places, 1 - core, side, square, pieces)
+    sent = partial_hidden(1 - core, side, square, rows)
     other = lax.ppermute(sent, "c", [(0, 1), (1, 0)])
-    own = partial_hidden(places, core, side, square, pieces)
+    own = partial_hidden(core, side, square, rows)
     terms = label_pairs(own, other, pair_ids, class_head[0])
     every_term = lax.all_to_all(
         jnp.broadcast_to(terms[None], (16, PAIRS, 256)), ("dp", "t"), 0, 0, tiled=True

time: 183 us -> 212 us (1.16)
  waiting for transfers between devices: 21.6 us -> 68.3 us
  starting transfers between devices: 64.2 us -> 23.1 us
  blocking collectives: 42.1 us -> 56.9 us
  between operations: 1.15 us -> 14.1 us
  Pallas kernels: 44.7 us -> 42 us
    ppermute x12 -> x0, starting transfers between devices: 41.4 us -> none  [the longest x8 24.4 us: exchange_rows(): got = lax.ppermute(last[half], 'z', up if (step + half) % 2 == 0 else down)]
    reduce_scatter x0 -> x1, waiting for transfers between devices: none -> 41.1 us  [shards(): lax.psum_scatter(grad_parts[0], 'dp', scatter_dimension=0, tiled=True)]
    all_to_all x1, waiting for transfers between devices: 0.01 us -> 23 us  [shards(): lax.all_to_all(jnp.broadcast_to(received[None], (4, 64, 8, 2 * TOKENS)),...]
    all_to_all x1 -> x2, blocking collectives: 21 us -> 41.6 us  [the longest x1 24.1 us: shards(): lax.all_to_all(picked.reshape(64, 8, 2 * TOKENS), ('z', 'yl', 'dp'), 0, 0...]
    ppermute x12 -> x0, waiting for transfers between devices: 17 us -> none  [the longest x8 13.3 us: exchange_rows(): got = lax.ppermute(last[half], 'z', up if (step + half) % 2 == 0 else down)]
    all_to_all x1, blocking collectives: 21.1 us -> 15.3 us  [shards(): lax.all_to_all(jnp.broadcast_to(terms[None], (16, PAIRS, 256)), ('dp', 't...]
    pallas_call x2, Pallas kernels: 12.8 us -> 10.4 us  [partial_hidden(): pl.pallas_call(hidden_kernel, grid_spec=pltpu.PrefetchScalarGridSpec(num_...]
    all_to_all x2 -> x1, starting transfers between devices: 11.6 us -> 12.8 us  [shards(): lax.all_to_all(jnp.broadcast_to(token_ids[None], (32, 1, TOKENS)), ('z',...]
  transfers between devices with their start and end apart: 16 -> 5, of which waited for: 7 -> 3; matrix products, arithmetic and copies ran while one was open for 2% -> 1% of each run, Pallas kernels for 19% -> 14%
where the time goes in v3:
time: 212 us; the launch traced here: 211 us
  waiting for transfers between devices  68.3 us (32%)
  blocking collectives  56.9 us (27%)
  Pallas kernels  42 us (20%)
  starting transfers between devices  23.1 us (11%)
  between operations  14.1 us (7%)
  local copies, waits for them, and re-layouts  5.72 us (3%)
    reduce_scatter x1, waiting for transfers between devices, shards(): lax.psum_scatter(grad_parts[0], 'dp', scatter_dimension=0, tiled=True)  41.1 us
    all_to_all x1, blocking collectives, shards(): lax.all_to_all(picked.reshape(64, 8, 2 * TOKENS), ('z', 'yl', 'dp'), 0, 0...  24.1 us
    all_to_all x1, waiting for transfers between devices, shards(): lax.all_to_all(jnp.broadcast_to(received[None], (4, 64, 8, 2 * TOKENS)),...  23 us
    all_to_all x1, blocking collectives, shards(): lax.all_to_all(columns.reshape(8, 32, WIDTH), ('yl', 'dp'), 0, 0, tiled=T...  17.5 us
    all_to_all x1, blocking collectives, shards(): lax.all_to_all(jnp.broadcast_to(terms[None], (16, PAIRS, 256)), ('dp', 't...  15.3 us
    pallas_call x1, Pallas kernels, pick_tokens(): pl.pallas_call(pick_kernel, grid=(chips,), in_specs=[pl.BlockSpec((1, 1,...  13.8 us
    all_to_all x1, starting transfers between devices, shards(): lax.all_to_all(jnp.broadcast_to(token_ids[None], (32, 1, TOKENS)), ('z',...  12.8 us
    pallas_call x2, Pallas kernels, partial_hidden(): pl.pallas_call(hidden_kernel, grid_spec=pltpu.PrefetchScalarGridSpec(num_...  10.4 us
  transfers between devices with their start and end apart: 5, of which 3 were waited for; matrix products, arithmetic and copies ran while one was open for 1% of the time, Pallas kernels for 14%

profile of v3, /device:TPU:1, one launch (start us, length us, event | category | flops | bytes accessed | tf_op | source)
XLA Modules:
  0.0 210.7 jit_solution(7079972354110229237)
XLA Ops:
  7.2 0.0 copy-start.3
  7.2 0.0 reduce-scatter.2.cloned.1.call-start
  7.2 0.7 reduce-scatter.2.cloned.1.call-update
  7.9 0.0 all-gather.2.cloned.1.call-start
  8.0 41.1 %reduce-scatter.2.cloned.1.call-done.gradient_ref = bf16[32,3584]{1,0:T(8,128)(2,1)} async-done(((bf16[128,3584]{1,0:T(8,128)(2,1)}), bf16[32,3584]{1,0:T(8,128)(2,1)}) %reduce-scatter.2.cloned.1.call-update) | async-done | bytes 229392 | tf_op jit(solution)/shard_map/reduce_scatter | solution.py:240
  49.0 3.7 %optimizer_step.1 = (f32[32,3584]{1,0:T(8,128)}, bf16[32,3584]{1,0:T(8,128)(2,1)}, bf16[32,3584]{1,0:T(8,128)(2,1)}, f32[32,3584]{1,0:T(8,128)}, bf16[2,4,32,896]{3,2,1,0:T(8,128)(2,1)}) custom-call(f32[32,3584]{1,0:T(8,128)} %master_ref.1, bf16[32,3584]{1,0:T(8,128)(2,1)} %first_ref.1, bf16[32,3584]{1,0:T(8,128)(2,1)} %second_ref.1, ...), custom_call_target="tpu_custom_call" | custom-call | flops 2097152 | bytes 8388608 | tf_op jit(solution)/shard_map/optimizer_step/pallas_call | solution.py:52
  52.7 17.5 %all_to_all.25 = bf16[8,32,896]{2,1,0:T(8,128)(2,1)} all-to-all(bf16[8,32,896]{2,1,0:T(8,128)(2,1)} %bitcast.19), channel_id=1, replica_groups=mesh['z'=8,'yl'=2,'c'=2,'dp'=4,'t'=4] {'yl','dp'}, dimensions={0} | all-to-all | bytes 917504 | tf_op jit(solution)/shard_map/all_to_all | solution.py:249
  70.2 0.0 all-gather.2.cloned.1.call-update
  70.3 0.0 copy-done.3
  70.3 0.6 broadcast_in_dim.11
  70.9 12.8 %all-to-all-start = ((s32[32,1,256]{2,1,0:T(1,128)}), s32[32,1,256]{2,1,0:T(1,128)S(1)}, u32[]{:S(2)}, u32[]{:S(2)}) async-start(s32[32,1,256]{2,1,0:T(1,128)} %broadcast_in_dim.11), calls=%async_computation.1 | async-start | bytes 65536 | tf_op jit(solution)/shard_map/all_to_all | solution.py:237
  83.7 4.7 %turn_table.1.table_ref = bf16[1024,512]{1,0:T(8,128)(2,1)} custom-call(bf16[501,8,128]{2,1,0:T(8,128)(2,1)} %bitcast.15), custom_call_target="tpu_custom_call" | custom-call | bytes 16777216 | tf_op jit(solution)/shard_map/turn_table/pallas_call | solution.py:81
  88.4 3.4 %all-to-all-done = s32[32,1,256]{2,1,0:T(1,128)S(1)} async-done(((s32[32,1,256]{2,1,0:T(1,128)}), s32[32,1,256]{2,1,0:T(1,128)S(1)}, u32[]{:S(2)}, u32[]{:S(2)}) %all-to-all-start) | async-done | bytes 32800 | tf_op jit(solution)/shard_map/all_to_all | solution.py:237
  91.8 0.0 copy-start.2
  91.8 0.6 copy-done.2
  92.4 13.8 %pick_tokens.1 = bf16[16,4,8,512]{3,2,1,0:T(8,128)(2,1)} custom-call(s32[16,1,512]{2,1,0:T(1,128)} %bitcast.20, bf16[1024,512]{1,0:T(8,128)(2,1)} %turn_table.1.table_ref), custom_call_target="tpu_custom_call" | custom-call | flops 8589934592 | bytes 2097152 | tf_op jit(solution)/shard_map/pick_tokens/pallas_call | solution.py:110
  106.2 24.1 %all_to_all.26 = bf16[64,8,512]{2,1,0:T(8,128)(2,1)S(1)} all-to-all(bf16[64,8,512]{2,1,0:T(8,128)(2,1)} %bitcast.17), channel_id=1, replica_groups=mesh['z'=8,'yl'=2,'c'=2,'dp'=4,'t'=4] {'z','yl','dp'}, dimensions={0} | all-to-all | bytes 1048576 | tf_op jit(solution)/shard_map/all_to_all | solution.py:243
  130.3 1.5 broadcast_in_dim.12
  131.8 4.1 %all-to-all-start.2 = ((bf16[4,64,8,512]{3,2,1,0:T(8,128)(2,1)}), bf16[4,64,8,512]{3,2,1,0:T(8,128)(2,1)S(1)}, u32[]{:S(2)}, u32[]{:S(2)}) async-start(bf16[4,64,8,512]{3,2,1,0:T(8,128)(2,1)} %broadcast_in_dim.12), calls=%async_computation.3 | async-start | bytes 4194304 | tf_op jit(solution)/shard_map/all_to_all | solution.py:251
  135.9 23.0 %all-to-all-done.2 = bf16[4,64,8,512]{3,2,1,0:T(8,128)(2,1)S(1)} async-done(((bf16[4,64,8,512]{3,2,1,0:T(8,128)(2,1)}), bf16[4,64,8,512]{3,2,1,0:T(8,128)(2,1)S(1)}, u32[]{:S(2)}, u32[]{:S(2)}) %all-to-all-start.2) | async-done | bytes 2097184 | tf_op jit(solution)/shard_map/all_to_all | solution.py:251
  158.9 0.0 copy-start
  158.9 1.3 copy-done
  160.3 6.2 %turn_tokens.1 = (bf16[512,2048]{1,0:T(8,128)(2,1)}, f32[512,128]{1,0:T(8,128)}) custom-call(bf16[4,8,2,4,8,512]{5,4,3,2,1,0:T(8,128)(2,1)} %bitcast.13), custom_call_target="tpu_custom_call" | custom-call | flops 2097152 | bytes 8388608 | tf_op jit(solution)/shard_map/turn_tokens/pallas_call | solution.py:142
  166.5 5.2 %partial_hidden.3 = f32[256,1024]{1,0:T(8,128)} custom-call(s32[1]{0:T(128)S(6)} %sub.3.group_ref, bf16[512,2048]{1,0:T(8,128)(2,1)} %get-tuple-element.16.side_ref, f32[512,128]{1,0:T(8,128)} %get-tuple-element.17.square_ref, bf16[2048,896]{1,0:T(8,128)(2,1)} %all-gather.2.cloned.1.call-done.rows_ref), custom_call_target="tpu_custom_call" | custom-call | flops 939524096 | bytes 6291456 | tf_op jit(solution)/shard_map/partial_hidden/pallas_call | solution.py:175
  171.7 6.1 %collective-permute-start = (f32[256,1024]{1,0:T(8,128)}, f32[256,1024]{1,0:T(8,128)S(1)}, u32[]{:S(2)}, u32[]{:S(2)}) collective-permute-start(f32[256,1024]{1,0:T(8,128)} %partial_hidden.3), channel_id=1, source_target_pairs={{0,16},{16,0},{1,17},{17,1},{2,18},{18,2},{3,19},{19,3},{4,20},{20... | collective-permute-start | bytes 3145736 | tf_op jit(solution)/shard_map/ppermute | solution.py:257
  177.8 5.2 %partial_hidden.2.own_ref = f32[256,1024]{1,0:T(8,128)} custom-call(s32[1]{0:T(128)} %bitcast.1.group_ref, bf16[512,2048]{1,0:T(8,128)(2,1)} %get-tuple-element.16.side_ref, f32[512,128]{1,0:T(8,128)} %get-tuple-element.17.square_ref, bf16[2048,896]{1,0:T(8,128)(2,1)} %all-gather.2.cloned.1.call-done.rows_ref), custom_call_target="tpu_custom_call" | custom-call | flops 939524096 | bytes 6291456 | tf_op jit(solution)/shard_map/partial_hidden/pallas_call | solution.py:175
  183.1 0.0 collective-permute-done.other_ref
  183.1 1.0 copy-done.1
  184.0 3.2 %label_pairs.1 = f32[8,256]{1,0:T(8,128)} custom-call(f32[256,1024]{1,0:T(8,128)} %partial_hidden.2.own_ref, f32[256,1024]{1,0:T(8,128)} %copy-done.1, s32[1,256]{1,0:T(1,128)} %pair_ref.1, bf16[896,256]{1,0:T(8,128)(2,1)} %bitcast.18), custom_call_target="tpu_custom_call" | custom-call | flops 14680064 | bytes 3145728 | tf_op jit(solution)/shard_map/label_pairs/pallas_call | solution.py:214
  187.2 0.7 broadcast_in_dim.26
  187.9 15.3 %all_to_all.27 = f32[16,8,256]{2,1,0:T(8,128)S(1)} all-to-all(f32[16,8,256]{2,1,0:T(8,128)S(1)} %broadcast_in_dim.26), channel_id=1, replica_groups=mesh['z'=8,'yl'=2,'c'=2,'dp'=4,'t'=4] {'dp','t'}, dimensions={0} | all-to-all | bytes 262144 | tf_op jit(solution)/shard_map/all_to_all | solution.py:260
  203.3 0.6 reduce_sum.9
  (2 shorter events, 0.0 us)
Async XLA Ops:
  7.2 63.1 %copy-start.3 = (s32[1,256]{1,0:T(1,128)S(1)}, s32[1,256]{1,0:T(1,128)}, u32[]{:S(2)}) copy-start(s32[1,256]{1,0:T(1,128)} %param.15) | copy-start | bytes 3076
  7.2 41.9 %reduce-scatter.2.cloned.1.call-start = ((), (), s32[]{:S(2)}) async-start(), calls=%async_computation.6 | async-start | bytes 1146880 | tf_op jit(solution)/shard_map/reduce_scatter | solution.py:240
  7.9 158.6 %all-gather.2.cloned.1.call-start = ((), (), s32[]{:S(2)}) async-start(), calls=%async_computation.7 | async-start | bytes 4128768 | tf_op jit(solution)/shard_map/all_gather | solution.py:250
  70.9 20.9 %all-to-all-start = ((s32[32,1,256]{2,1,0:T(1,128)}), s32[32,1,256]{2,1,0:T(1,128)S(1)}, u32[]{:S(2)}, u32[]{:S(2)}) async-start(s32[32,1,256]{2,1,0:T(1,128)} %broadcast_in_dim.11), calls=%async_computation.1 | async-start | bytes 65536 | tf_op jit(solution)/shard_map/all_to_all | solution.py:237
  91.8 0.6 copy-start.2
  131.8 27.1 %all-to-all-start.2 = ((bf16[4,64,8,512]{3,2,1,0:T(8,128)(2,1)}), bf16[4,64,8,512]{3,2,1,0:T(8,128)(2,1)S(1)}, u32[]{:S(2)}, u32[]{:S(2)}) async-start(bf16[4,64,8,512]{3,2,1,0:T(8,128)(2,1)} %broadcast_in_dim.12), calls=%async_computation.3 | async-start | bytes 4194304 | tf_op jit(solution)/shard_map/all_to_all | solution.py:251
  158.9 1.3 copy-start
  171.7 11.4 %collective-permute-start = (f32[256,1024]{1,0:T(8,128)}, f32[256,1024]{1,0:T(8,128)S(1)}, u32[]{:S(2)}, u32[]{:S(2)}) collective-permute-start(f32[256,1024]{1,0:T(8,128)} %partial_hidden.3), channel_id=1, source_target_pairs={{0,16},{16,0},{1,17},{17,1},{2,18},{18,2},{3,19},{19,3},{4,20},{20... | collective-permute-start | bytes 3145736 | tf_op jit(solution)/shard_map/ppermute | solution.py:257
  183.1 1.0 copy-start.1
Sparse Core Ops, SparseCore 0:
  10.8 38.1 reduce-scatter.1
  70.4 65.6 all-gather.1

commit v4 on v3

--- a/solution.py
+++ b/solution.py
@@ -85,6 +85,7 @@
         out_specs=pl.BlockSpec(memory_space=VMEM),
         scratch_shapes=[VMEM((UPPER, 8, 128), f32), VMEM((128, 8, UPPER), f32)],
         cost_estimate=pl.CostEstimate(flops=0, bytes_accessed=1 << 24, transcendentals=0),
+        compiler_params=pltpu.CompilerParams(vmem_limit_bytes=16 << 20),
         name="turn_table",
     )(tiles)
 
@@ -101,8 +102,7 @@
         lines = jnp.dot(table_ref[pl.ds(part * 256, 256), :], hot, preferred_element_type=f32)
         for k in range(32):
             picked = jnp.where(lower == part * 32 + k, lines[k * 8 : (k + 1) * 8, :], picked)
-    for copy in range(out_ref.shape[1]):
-        out_ref[0, copy] = picked.astype(bf16)
+    out_ref[0] = picked.astype(bf16)
 
 
 def pick_tokens(ids, table):
@@ -114,38 +114,42 @@
             pl.BlockSpec((1, 1, count), lambda i: (i, 0, 0)),
             pl.BlockSpec((1024, UPPER), lambda i: (0, 0)),
         ],
-        out_specs=pl.BlockSpec((1, 4, 8, count), lambda i: (i, 0, 0, 0)),
-        out_shape=jax.ShapeDtypeStruct((chips, 4, 8, count), bf16),
+        out_specs=pl.BlockSpec((1, 8, count), lambda i: (i, 0, 0)),
+        out_shape=jax.ShapeDtypeStruct((chips, 8, count), bf16),
         cost_estimate=pl.CostEstimate(
             flops=2 * 1024 * UPPER * chips * count, bytes_accessed=1 << 21, transcendentals=0
         ),
+        compiler_params=pltpu.CompilerParams(vmem_limit_bytes=20 << 20),
         name="pick_tokens",
     )(ids, table)
 
 
-def turn_tokens_kernel(in_ref, out_ref, square_ref):
+def turn_tokens_kernel(place_ref, in_ref, out_ref, square_ref):
     @pl.when(pl.program_id(0) == 0)
     def _():
         square_ref[...] = jnp.zeros_like(square_ref)
 
     for line in range(2):
         rows = [
-            in_ref[t, 0, line, d].astype(f32) for d in range(4) for t in range(4)
+            in_ref[t, place_ref[0] ^ d, 0, line].astype(f32) for d in range(4) for t in range(4)
         ]
         turned = jnp.concatenate(rows, axis=0).T
         square_ref[...] += turned * turned
         out_ref[:, pl.ds(line * 128, 128)] = turned.astype(bf16)
 
 
-def turn_tokens(stacked):
+def turn_tokens(place, stacked):
     count = stacked.shape[-1]
     return pl.pallas_call(
         turn_tokens_kernel,
-        grid=(8,),
-        in_specs=[pl.BlockSpec((4, 1, 2, 4, 8, count), lambda i: (0, i, 0, 0, 0, 0))],
-        out_specs=(
-            pl.BlockSpec((count, 256), lambda i: (0, i)),
-            pl.BlockSpec((count, 128), lambda i: (0, 0)),
+        grid_spec=pltpu.PrefetchScalarGridSpec(
+            num_scalar_prefetch=1,
+            grid=(8,),
+            in_specs=[pl.BlockSpec((4, 4, 1, 2, 8, count), lambda i, place: (0, 0, i, 0, 0, 0))],
+            out_specs=(
+                pl.BlockSpec((count, 256), lambda i, place: (0, i)),
+                pl.BlockSpec((count, 128), lambda i, place: (0, 0)),
+            ),
         ),
         out_shape=(
             jax.ShapeDtypeStruct((count, 2048), bf16),
@@ -153,7 +157,7 @@
         ),
         cost_estimate=pl.CostEstimate(flops=1 << 21, bytes_accessed=1 << 23, transcendentals=0),
         name="turn_tokens",
-    )(stacked)
+    )(place, stacked)
 
 
 def hidden_kernel(group_ref, side_ref, square_ref, rows_ref, out_ref):
@@ -219,6 +223,7 @@
         cost_estimate=pl.CostEstimate(
             flops=2 * 32 * TOKENS * WIDTH, bytes_accessed=3 << 20, transcendentals=TOKENS * WIDTH
         ),
+        compiler_params=pltpu.CompilerParams(vmem_limit_bytes=16 << 20),
         name="label_pairs",
     )(own, other, pairs, head)
 
@@ -241,17 +246,22 @@
     table = turn_table(embed_table)
     picked = pick_tokens(every_id.reshape(16, 1, 2 * TOKENS), table)
     received = lax.all_to_all(
-        picked.reshape(64, 8, 2 * TOKENS), ("z", "yl", "dp"), 0, 0, tiled=True
+        picked, ("z", "yl"), 0, 0, tiled=True
     )
     master_new, first_new, second_new, teacher_new, columns = optimizer_step(
         master_weight, first_moment, second_moment, teacher_weight, gradient
     )
     block = lax.all_to_all(columns.reshape(8, 32, WIDTH), ("yl", "dp"), 0, 0, tiled=True)
     rows = lax.all_gather(block.reshape(256, WIDTH), "z", axis=0, tiled=True)
+    parts = [received]
+    for k in (1, 3, 2):
+        parts.append(lax.ppermute(received, "dp", [(i, i ^ k) for i in range(4)]))
+    near = jnp.stack([parts[0], parts[1], parts[3], parts[2]])
     stacked = lax.all_to_all(
-        jnp.broadcast_to(received[None], (4, 64, 8, 2 * TOKENS)), "t", 0, 0, tiled=True
-    )
-    side, square = turn_tokens(stacked.reshape(4, 8, 2, 4, 8, 2 * TOKENS))
+        jnp.broadcast_to(near[None], (4, 4, 16, 8, 2 * TOKENS)), "t", 0, 0, tiled=True
+    )
+    place = lax.axis_index("dp").astype(jnp.int32).reshape(1)
+    side, square = turn_tokens(place, stacked.reshape(4, 4, 8, 2, 8, 2 * TOKENS))
     core = lax.axis_index("c").astype(jnp.int32).reshape(1)
     sent = partial_hidden(1 - core, side, square, rows)
     other = lax.ppermute(sent, "c", [(0, 1), (1, 0)])

time: 212 us -> 216 us (1.019)
  waiting for transfers between devices: 68.3 us -> 85.2 us
  blocking collectives: 56.9 us -> 42.6 us
  starting transfers between devices: 23.1 us -> 32 us
  Pallas kernels: 42 us -> 35.6 us
    all_to_all x1, blocking collectives: 24.1 us -> 11.7 us  [shards(): received = lax.all_to_all(picked, ('z', 'yl'), 0, 0, tiled=True)]
    ppermute x0 -> x3, waiting for transfers between devices: none -> 12.2 us  [shards(): parts.append(lax.ppermute(received, 'dp', [(i, i ^ k) for i in range(4)]))]
    ppermute x0 -> x3, starting transfers between devices: none -> 11.4 us  [shards(): parts.append(lax.ppermute(received, 'dp', [(i, i ^ k) for i in range(4)]))]
    all_to_all x1, waiting for transfers between devices: 23 us -> 25.7 us  [shards(): lax.all_to_all(jnp.broadcast_to(near[None], (4, 4, 16, 8, 2 * TOKENS)), '...]
    ppermute x1, starting transfers between devices: 6.14 us -> 3.66 us  [shards(): other = lax.ppermute(sent, 'c', [(0, 1), (1, 0)])]
    pallas_call x1, Pallas kernels: 3.19 us -> 0.92 us  [label_pairs(): pl.pallas_call(label_kernel, out_shape=jax.ShapeDtypeStruct((PAIRS, 256),...]
  transfers between devices with their start and end apart: 5 -> 8, of which waited for: 3 -> 5; matrix products, arithmetic and copies ran while one was open for 1% -> 1% of each run, Pallas kernels for 14% -> 12%
where the time goes in v4:
time: 216 us; the launch traced here: 215 us
  waiting for transfers between devices  85.2 us (39%)
  blocking collectives  42.6 us (20%)
  Pallas kernels  35.6 us (16%)
  starting transfers between devices  32 us (15%)
  between operations  14.2 us (7%)
  local copies, waits for them, and re-layouts  4.74 us (2%)
    reduce_scatter x1, waiting for transfers between devices, shards(): lax.psum_scatter(grad_parts[0], 'dp', scatter_dimension=0, tiled=True)  41.1 us
    all_to_all x1, waiting for transfers between devices, shards(): lax.all_to_all(jnp.broadcast_to(near[None], (4, 4, 16, 8, 2 * TOKENS)), '...  25.7 us
    all_to_all x1, blocking collectives, shards(): lax.all_to_all(columns.reshape(8, 32, WIDTH), ('yl', 'dp'), 0, 0, tiled=T...  17.5 us
    all_to_all x1, blocking collectives, shards(): lax.all_to_all(jnp.broadcast_to(terms[None], (16, PAIRS, 256)), ('dp', 't...  13.5 us
    all_to_all x1, starting transfers between devices, shards(): lax.all_to_all(jnp.broadcast_to(token_ids[None], (32, 1, TOKENS)), ('z',...  12.8 us
    ppermute x3, waiting for transfers between devices, shards(): parts.append(lax.ppermute(received, 'dp', [(i, i ^ k) for i in range(4)]))  12.2 us
    pallas_call x1, Pallas kernels, pick_tokens(): pl.pallas_call(pick_kernel, grid=(chips,), in_specs=[pl.BlockSpec((1, 1,...  11.8 us
    all_to_all x1, blocking collectives, shards(): received = lax.all_to_all(picked, ('z', 'yl'), 0, 0, tiled=True)  11.7 us
  transfers between devices with their start and end apart: 8, of which 5 were waited for; matrix products, arithmetic and copies ran while one was open for 1% of the time, Pallas kernels for 12%

profile of v4, /device:TPU:1, one launch (start us, length us, event | category | flops | bytes accessed | tf_op | source)
XLA Modules:
  0.0 215.0 jit_solution(15519605936980623315)
XLA Ops:
  7.2 0.0 reduce-scatter.2.cloned.1.call-start
  7.2 0.7 reduce-scatter.2.cloned.1.call-update
  7.9 0.0 all-gather.2.cloned.1.call-start
  8.0 41.1 %reduce-scatter.2.cloned.1.call-done.gradient_ref = bf16[32,3584]{1,0:T(8,128)(2,1)} async-done(((bf16[128,3584]{1,0:T(8,128)(2,1)}), bf16[32,3584]{1,0:T(8,128)(2,1)}) %reduce-scatter.2.cloned.1.call-update) | async-done | bytes 229392 | tf_op jit(solution)/shard_map/reduce_scatter | solution.py:245
  49.0 3.7 %optimizer_step.1 = (f32[32,3584]{1,0:T(8,128)}, bf16[32,3584]{1,0:T(8,128)(2,1)}, bf16[32,3584]{1,0:T(8,128)(2,1)}, f32[32,3584]{1,0:T(8,128)}, bf16[2,4,32,896]{3,2,1,0:T(8,128)(2,1)}) custom-call(f32[32,3584]{1,0:T(8,128)} %master_ref.1, bf16[32,3584]{1,0:T(8,128)(2,1)} %first_ref.1, bf16[32,3584]{1,0:T(8,128)(2,1)} %second_ref.1, ...), custom_call_target="tpu_custom_call" | custom-call | flops 2097152 | bytes 8388608 | tf_op jit(solution)/shard_map/optimizer_step/pallas_call | solution.py:52
  52.7 17.5 %all_to_all.25 = bf16[8,32,896]{2,1,0:T(8,128)(2,1)} all-to-all(bf16[8,32,896]{2,1,0:T(8,128)(2,1)} %bitcast.24), channel_id=1, replica_groups=mesh['z'=8,'yl'=2,'c'=2,'dp'=4,'t'=4] {'yl','dp'}, dimensions={0} | all-to-all | bytes 917504 | tf_op jit(solution)/shard_map/all_to_all | solution.py:254
  70.3 0.0 all-gather.2.cloned.1.call-update
  70.3 0.6 broadcast_in_dim.11
  70.9 12.8 %all-to-all-start = ((s32[32,1,256]{2,1,0:T(1,128)}), s32[32,1,256]{2,1,0:T(1,128)S(1)}, u32[]{:S(2)}, u32[]{:S(2)}) async-start(s32[32,1,256]{2,1,0:T(1,128)} %broadcast_in_dim.11), calls=%async_computation.1 | async-start | bytes 65536 | tf_op jit(solution)/shard_map/all_to_all | solution.py:242
  83.7 2.5 %turn_table.1.table_ref = bf16[1024,512]{1,0:T(8,128)(2,1)S(1)} custom-call(bf16[501,8,128]{2,1,0:T(8,128)(2,1)S(1)} %bitcast.17), custom_call_target="tpu_custom_call" | custom-call | bytes 16777216 | tf_op jit(solution)/shard_map/turn_table/pallas_call | solution.py:81
  86.3 5.6 %all-to-all-done = s32[32,1,256]{2,1,0:T(1,128)S(1)} async-done(((s32[32,1,256]{2,1,0:T(1,128)}), s32[32,1,256]{2,1,0:T(1,128)S(1)}, u32[]{:S(2)}, u32[]{:S(2)}) %all-to-all-start) | async-done | bytes 32800 | tf_op jit(solution)/shard_map/all_to_all | solution.py:242
  91.8 11.8 %pick_tokens.1 = bf16[16,8,512]{2,1,0:T(8,128)(2,1)S(1)} custom-call(s32[16,1,512]{2,1,0:T(1,128)S(1)} %bitcast.19, bf16[1024,512]{1,0:T(8,128)(2,1)S(1)} %turn_table.1.table_ref), custom_call_target="tpu_custom_call" | custom-call | flops 8589934592 | bytes 2097152 | tf_op jit(solution)/shard_map/pick_tokens/pallas_call | solution.py:110
  103.6 11.7 %all_to_all.26 = bf16[16,8,512]{2,1,0:T(8,128)(2,1)S(1)} all-to-all(bf16[16,8,512]{2,1,0:T(8,128)(2,1)S(1)} %pick_tokens.1), channel_id=1, replica_groups=mesh['z'=8,'yl'=2,'c'=2,'dp'=4,'t'=4] {'z','yl'}, dimensions={0} | all-to-all | bytes 262144 | tf_op jit(solution)/shard_map/all_to_all | solution.py:248
  115.3 2.3 %collective-permute-start.2 = (bf16[16,8,512]{2,1,0:T(8,128)(2,1)S(1)}, bf16[16,8,512]{2,1,0:T(8,128)(2,1)S(1)}, u32[]{:S(2)}, u32[]{:S(2)}) collective-permute-start(bf16[16,8,512]{2,1,0:T(8,128)(2,1)S(1)} %all_to_all.26), channel_id=1, source_target_pairs={{0,12},{4,8},{8,4},{12,0},{1,13},{5,9},{9,5},{13,1},{2,14},{6,10},... | collective-permute-start | bytes 393224 | tf_op jit(solution)/shard_map/ppermute | solution.py:258
  117.6 4.9 %collective-permute-start.1 = (bf16[16,8,512]{2,1,0:T(8,128)(2,1)S(1)}, bf16[16,8,512]{2,1,0:T(8,128)(2,1)S(1)}, u32[]{:S(2)}, u32[]{:S(2)}) collective-permute-start(bf16[16,8,512]{2,1,0:T(8,128)(2,1)S(1)} %all_to_all.26), channel_id=1, source_target_pairs={{0,8},{4,12},{8,0},{12,4},{1,9},{5,13},{9,1},{13,5},{2,10},{6,14},... | collective-permute-start | bytes 393224 | tf_op jit(solution)/shard_map/ppermute | solution.py:258
  122.4 4.2 %collective-permute-start = (bf16[16,8,512]{2,1,0:T(8,128)(2,1)S(1)}, bf16[16,8,512]{2,1,0:T(8,128)(2,1)S(1)}, u32[]{:S(2)}, u32[]{:S(2)}) collective-permute-start(bf16[16,8,512]{2,1,0:T(8,128)(2,1)S(1)} %all_to_all.26), channel_id=1, source_target_pairs={{0,4},{4,0},{8,12},{12,8},{1,5},{5,1},{9,13},{13,9},{2,6},{6,2},{1... | collective-permute-start | bytes 393224 | tf_op jit(solution)/shard_map/ppermute | solution.py:258
  126.7 0.0 collective-permute-done.2
  126.7 4.1 %collective-permute-done.1 = bf16[16,8,512]{2,1,0:T(8,128)(2,1)S(1)} collective-permute-done((bf16[16,8,512]{2,1,0:T(8,128)(2,1)S(1)}, bf16[16,8,512]{2,1,0:T(8,128)(2,1)S(1)}, u32[]{:S(2)}, u32[]{:S(2)}) %collective-permute-start.1) | collective-permute-done | bytes 131104 | tf_op jit(solution)/shard_map/ppermute | solution.py:258
  130.8 8.0 %collective-permute-done = bf16[16,8,512]{2,1,0:T(8,128)(2,1)S(1)} collective-permute-done((bf16[16,8,512]{2,1,0:T(8,128)(2,1)S(1)}, bf16[16,8,512]{2,1,0:T(8,128)(2,1)S(1)}, u32[]{:S(2)}, u32[]{:S(2)}) %collective-permute-start) | collective-permute-done | bytes 131104 | tf_op jit(solution)/shard_map/ppermute | solution.py:258
  138.8 0.1 pad_maximum_fusion
  138.9 1.5 broadcast_in_dim.12
  140.5 4.1 %all-to-all-start.2 = ((bf16[4,4,16,8,512]{4,3,2,1,0:T(8,128)(2,1)}), bf16[4,4,16,8,512]{4,3,2,1,0:T(8,128)(2,1)S(1)}, u32[]{:S(2)}, u32[]{:S(2)}) async-start(bf16[4,4,16,8,512]{4,3,2,1,0:T(8,128)(2,1)} %broadcast_in_dim.12), calls=%async_computation.3 | async-start | bytes 4194304 | tf_op jit(solution)/shard_map/all_to_all | solution.py:260
  144.6 25.7 %all-to-all-done.2 = bf16[4,4,16,8,512]{4,3,2,1,0:T(8,128)(2,1)S(1)} async-done(((bf16[4,4,16,8,512]{4,3,2,1,0:T(8,128)(2,1)}), bf16[4,4,16,8,512]{4,3,2,1,0:T(8,128)(2,1)S(1)}, u32[]{:S(2)}, u32[]{:S(2)}) %all-to-all-start.2) | async-done | bytes 2097184 | tf_op jit(solution)/shard_map/all_to_all | solution.py:260
  170.2 1.3 copy-done.4
  171.5 6.2 %turn_tokens.1 = (bf16[512,2048]{1,0:T(8,128)(2,1)}, f32[512,128]{1,0:T(8,128)}) custom-call(s32[1]{0:T(128)} %bitcast.2.place_ref, bf16[4,4,8,2,8,512]{5,4,3,2,1,0:T(8,128)(2,1)} %bitcast.20), custom_call_target="tpu_custom_call" | custom-call | flops 2097152 | bytes 8388608 | tf_op jit(solution)/shard_map/turn_tokens/pallas_call | solution.py:143
  177.8 5.2 %partial_hidden.3 = f32[256,1024]{1,0:T(8,128)} custom-call(s32[1]{0:T(128)S(6)} %sub.3.group_ref, bf16[512,2048]{1,0:T(8,128)(2,1)} %get-tuple-element.16.side_ref, f32[512,128]{1,0:T(8,128)} %get-tuple-element.17.square_ref, bf16[2048,896]{1,0:T(8,128)(2,1)} %all-gather.2.cloned.1.call-done.rows_ref), custom_call_target="tpu_custom_call" | custom-call | flops 939524096 | bytes 6291456 | tf_op jit(solution)/shard_map/partial_hidden/pallas_call | solution.py:179
  183.0 3.7 %collective-permute-start.3 = (f32[256,1024]{1,0:T(8,128)}, f32[256,1024]{1,0:T(8,128)S(1)}, u32[]{:S(2)}, u32[]{:S(2)}) collective-permute-start(f32[256,1024]{1,0:T(8,128)} %partial_hidden.3), channel_id=1, source_target_pairs={{0,16},{16,0},{1,17},{17,1},{2,18},{18,2},{3,19},{19,3},{4,20},{20... | collective-permute-start | bytes 3145736 | tf_op jit(solution)/shard_map/ppermute | solution.py:267
  186.6 5.2 %partial_hidden.2.own_ref = f32[256,1024]{1,0:T(8,128)} custom-call(s32[1]{0:T(128)} %bitcast.1.group_ref, bf16[512,2048]{1,0:T(8,128)(2,1)} %get-tuple-element.16.side_ref, f32[512,128]{1,0:T(8,128)} %get-tuple-element.17.square_ref, bf16[2048,896]{1,0:T(8,128)(2,1)} %all-gather.2.cloned.1.call-done.rows_ref), custom_call_target="tpu_custom_call" | custom-call | flops 939524096 | bytes 6291456 | tf_op jit(solution)/shard_map/partial_hidden/pallas_call | solution.py:179
  191.9 1.2 copy-done
  193.1 0.9 label_pairs.1
  194.0 13.5 %all_to_all.27 = f32[16,8,256]{2,1,0:T(8,128)S(1)} all-to-all(f32[16,8,256]{2,1,0:T(8,128)S(1)} %broadcast_in_dim.26), channel_id=1, replica_groups=mesh['z'=8,'yl'=2,'c'=2,'dp'=4,'t'=4] {'dp','t'}, dimensions={0} | all-to-all | bytes 262144 | tf_op jit(solution)/shard_map/all_to_all | solution.py:270
  207.5 0.6 reduce_sum.9
  (13 shorter events, 0.0 us)
Async XLA Ops:
  7.2 63.1 %copy-start.5 = (s32[1,256]{1,0:T(1,128)S(1)}, s32[1,256]{1,0:T(1,128)}, u32[]{:S(2)}) copy-start(s32[1,256]{1,0:T(1,128)} %param.15) | copy-start | bytes 3076
  7.2 76.5 %copy-start.1 = (bf16[8,64128]{1,0:T(8,128)(2,1)S(1)}, bf16[8,64128]{1,0:T(8,128)(2,1)}, u32[]{:S(2)}) copy-start(bf16[8,64128]{1,0:T(8,128)(2,1)} %param.14) | copy-start | bytes 3078148
  7.2 41.9 %reduce-scatter.2.cloned.1.call-start = ((), (), s32[]{:S(2)}) async-start(), calls=%async_computation.6 | async-start | bytes 1146880 | tf_op jit(solution)/shard_map/reduce_scatter | solution.py:245
  7.9 169.9 %all-gather.2.cloned.1.call-start = ((), (), s32[]{:S(2)}) async-start(), calls=%async_computation.7 | async-start | bytes 4128768 | tf_op jit(solution)/shard_map/all_gather | solution.py:255
  70.9 20.9 %all-to-all-start = ((s32[32,1,256]{2,1,0:T(1,128)}), s32[32,1,256]{2,1,0:T(1,128)S(1)}, u32[]{:S(2)}, u32[]{:S(2)}) async-start(s32[32,1,256]{2,1,0:T(1,128)} %broadcast_in_dim.11), calls=%async_computation.1 | async-start | bytes 65536 | tf_op jit(solution)/shard_map/all_to_all | solution.py:242
  115.3 11.4 %collective-permute-start.2 = (bf16[16,8,512]{2,1,0:T(8,128)(2,1)S(1)}, bf16[16,8,512]{2,1,0:T(8,128)(2,1)S(1)}, u32[]{:S(2)}, u32[]{:S(2)}) collective-permute-start(bf16[16,8,512]{2,1,0:T(8,128)(2,1)S(1)} %all_to_all.26), channel_id=1, source_target_pairs={{0,12},{4,8},{8,4},{12,0},{1,13},{5,9},{9,5},{13,1},{2,14},{6,10},... | collective-permute-start | bytes 393224 | tf_op jit(solution)/shard_map/ppermute | solution.py:258
  117.6 13.3 %collective-permute-start.1 = (bf16[16,8,512]{2,1,0:T(8,128)(2,1)S(1)}, bf16[16,8,512]{2,1,0:T(8,128)(2,1)S(1)}, u32[]{:S(2)}, u32[]{:S(2)}) collective-permute-start(bf16[16,8,512]{2,1,0:T(8,128)(2,1)S(1)} %all_to_all.26), channel_id=1, source_target_pairs={{0,8},{4,12},{8,0},{12,4},{1,9},{5,13},{9,1},{13,5},{2,10},{6,14},... | collective-permute-start | bytes 393224 | tf_op jit(solution)/shard_map/ppermute | solution.py:258
  122.4 16.4 %collective-permute-start = (bf16[16,8,512]{2,1,0:T(8,128)(2,1)S(1)}, bf16[16,8,512]{2,1,0:T(8,128)(2,1)S(1)}, u32[]{:S(2)}, u32[]{:S(2)}) collective-permute-start(bf16[16,8,512]{2,1,0:T(8,128)(2,1)S(1)} %all_to_all.26), channel_id=1, source_target_pairs={{0,4},{4,0},{8,12},{12,8},{1,5},{5,1},{9,13},{13,9},{2,6},{6,2},{1... | collective-permute-start | bytes 393224 | tf_op jit(solution)/shard_map/ppermute | solution.py:258
  140.5 29.8 %all-to-all-start.2 = ((bf16[4,4,16,8,512]{4,3,2,1,0:T(8,128)(2,1)}), bf16[4,4,16,8,512]{4,3,2,1,0:T(8,128)(2,1)S(1)}, u32[]{:S(2)}, u32[]{:S(2)}) async-start(bf16[4,4,16,8,512]{4,3,2,1,0:T(8,128)(2,1)} %broadcast_in_dim.12), calls=%async_computation.3 | async-start | bytes 4194304 | tf_op jit(solution)/shard_map/all_to_all | solution.py:260
  170.2 1.3 copy-start.4
  183.0 8.9 %copy-start.2 = (bf16[1,896,256]{2,1,0:T(8,128)(2,1)S(1)}, bf16[1,896,256]{2,1,0:T(8,128)(2,1)}, u32[]{:S(2)}) copy-start(bf16[1,896,256]{2,1,0:T(8,128)(2,1)} %param.17) | copy-start | bytes 1376260
  183.0 8.9 %copy-start.3 = (s32[1,256]{1,0:T(1,128)S(1)}, s32[1,256]{1,0:T(1,128)}, u32[]{:S(2)}) copy-start(s32[1,256]{1,0:T(1,128)} %pair_ref.1) | copy-start | bytes 3076
  183.0 8.9 %collective-permute-start.3 = (f32[256,1024]{1,0:T(8,128)}, f32[256,1024]{1,0:T(8,128)S(1)}, u32[]{:S(2)}, u32[]{:S(2)}) collective-permute-start(f32[256,1024]{1,0:T(8,128)} %partial_hidden.3), channel_id=1, source_target_pairs={{0,16},{16,0},{1,17},{17,1},{2,18},{18,2},{3,19},{19,3},{4,20},{20... | collective-permute-start | bytes 3145736 | tf_op jit(solution)/shard_map/ppermute | solution.py:267
  191.9 1.2 copy-start
Sparse Core Ops, SparseCore 0:
  10.9 38.1 reduce-scatter.1
  70.4 57.2 all-gather.1

commit v5 on v4

--- a/solution.py
+++ b/solution.py
@@ -62,8 +62,12 @@
             jax.ShapeDtypeStruct((2, 4, 32, WIDTH), bf16),
         ],
         cost_estimate=pl.CostEstimate(flops=1 << 21, bytes_accessed=1 << 23, transcendentals=0),
+        compiler_params=pltpu.CompilerParams(vmem_limit_bytes=16 << 20),
         name="optimizer_step",
-    )(master_weight, first_moment, second_moment, teacher_weight, gradient)
+    )(
+        master_weight, first_moment, second_moment, teacher_weight,
+        pltpu.with_memory_space_constraint(gradient, pltpu.HBM),
+    )
 
 
 def turn_table_kernel(table_ref, out_ref, wide, turned):
@@ -124,76 +128,71 @@
     )(ids, table)
 
 
-def turn_tokens_kernel(place_ref, in_ref, out_ref, square_ref):
-    @pl.when(pl.program_id(0) == 0)
-    def _():
-        square_ref[...] = jnp.zeros_like(square_ref)
-
-    for line in range(2):
+def turn_tokens_kernel(place_ref, in_ref, out_ref):
+    for pair in range(4):
         rows = [
-            in_ref[t, place_ref[0] ^ d, 0, line].astype(f32) for d in range(4) for t in range(4)
+            in_ref[place_ref[0] ^ d, pair * 4 + line].astype(f32)
+            for line in range(4)
+            for d in range(4)
         ]
-        turned = jnp.concatenate(rows, axis=0).T
-        square_ref[...] += turned * turned
-        out_ref[:, pl.ds(line * 128, 128)] = turned.astype(bf16)
-
-
-def turn_tokens(place, stacked):
-    count = stacked.shape[-1]
+        turned = jnp.concatenate(rows, axis=0).T.astype(bf16)
+        for copy in range(4):
+            out_ref[copy, :, pair * 128 : (pair + 1) * 128] = turned
+
+
+def turn_tokens(place, near):
+    count = near.shape[-1]
     return pl.pallas_call(
         turn_tokens_kernel,
         grid_spec=pltpu.PrefetchScalarGridSpec(
             num_scalar_prefetch=1,
-            grid=(8,),
-            in_specs=[pl.BlockSpec((4, 4, 1, 2, 8, count), lambda i, place: (0, 0, i, 0, 0, 0))],
-            out_specs=(
-                pl.BlockSpec((count, 256), lambda i, place: (0, i)),
-                pl.BlockSpec((count, 128), lambda i, place: (0, 0)),
-            ),
-        ),
-        out_shape=(
-            jax.ShapeDtypeStruct((count, 2048), bf16),
-            jax.ShapeDtypeStruct((count, 128), f32),
-        ),
-        cost_estimate=pl.CostEstimate(flops=1 << 21, bytes_accessed=1 << 23, transcendentals=0),
+            grid=(1,),
+            in_specs=[pl.BlockSpec((4, 16, 8, count), lambda i, place: (0, 0, 0, 0))],
+            out_specs=pl.BlockSpec((4, count, 512), lambda i, place: (0, 0, 0)),
+        ),
+        out_shape=jax.ShapeDtypeStruct((4, count, 512), bf16),
+        cost_estimate=pl.CostEstimate(flops=1 << 21, bytes_accessed=1 << 22, transcendentals=0),
         name="turn_tokens",
-    )(place, stacked)
-
-
-def hidden_kernel(group_ref, side_ref, square_ref, rows_ref, out_ref):
-    product = jnp.dot(side_ref[...], rows_ref[...], preferred_element_type=f32)
+    )(place, near)
+
+
+def hidden_kernel(group_ref, side_ref, rows_ref, out_ref):
+    side = side_ref[0]
+    product = jnp.dot(side, rows_ref[...].reshape(512, WIDTH), preferred_element_type=f32)
+    wide = side.astype(f32)
+    square = wide * wide
+    square = (square[:, :128] + square[:, 128:256]) + (square[:, 256:384] + square[:, 384:])
 
     @pl.when(pl.program_id(0) == 0)
     def _():
         out_ref[:, :WIDTH] = product
-        out_ref[:, WIDTH:] = square_ref[...]
+        out_ref[:, WIDTH:] = square
 
     @pl.when(pl.program_id(0) > 0)
     def _():
         out_ref[:, :WIDTH] += product
-
-
-def partial_hidden(group, side, square, rows):
-    steps = 4
-    depth = rows.shape[0] // steps
+        out_ref[:, WIDTH:] += square
+
+
+def partial_hidden(group, side, rows):
     return pl.pallas_call(
         hidden_kernel,
         grid_spec=pltpu.PrefetchScalarGridSpec(
             num_scalar_prefetch=1,
-            grid=(steps,),
+            grid=(4,),
             in_specs=[
-                pl.BlockSpec((TOKENS, depth), lambda i, group: (group[0], i)),
-                pl.BlockSpec((TOKENS, 128), lambda i, group: (group[0], 0)),
-                pl.BlockSpec((depth, WIDTH), lambda i, group: (i, 0)),
+                pl.BlockSpec((1, TOKENS, 512), lambda t, group: (t, group[0], 0)),
+                pl.BlockSpec((8, 1, 64, WIDTH), lambda t, group: (0, t, 0, 0)),
             ],
-            out_specs=pl.BlockSpec((TOKENS, 1024), lambda i, group: (0, 0)),
+            out_specs=pl.BlockSpec((TOKENS, 1024), lambda t, group: (0, 0)),
         ),
         out_shape=jax.ShapeDtypeStruct((TOKENS, 1024), f32),
         cost_estimate=pl.CostEstimate(
             flops=2 * TOKENS * 2048 * WIDTH, bytes_accessed=6 << 20, transcendentals=0
         ),
+        compiler_params=pltpu.CompilerParams(vmem_limit_bytes=24 << 20),
         name="partial_hidden",
-    )(group, side, square, rows)
+    )(group, side, pltpu.with_memory_space_constraint(rows, pltpu.HBM))
 
 
 def label_kernel(own_ref, other_ref, pair_ref, head_ref, out_ref):
@@ -252,20 +251,20 @@
         master_weight, first_moment, second_moment, teacher_weight, gradient
     )
     block = lax.all_to_all(columns.reshape(8, 32, WIDTH), ("yl", "dp"), 0, 0, tiled=True)
-    rows = lax.all_gather(block.reshape(256, WIDTH), "z", axis=0, tiled=True)
+    sorted_block = block.reshape(8, 4, 8, WIDTH).transpose(1, 0, 2, 3).reshape(256, WIDTH)
+    rows = lax.all_gather(sorted_block, "z", axis=0, tiled=True)
     parts = [received]
     for k in (1, 3, 2):
         parts.append(lax.ppermute(received, "dp", [(i, i ^ k) for i in range(4)]))
     near = jnp.stack([parts[0], parts[1], parts[3], parts[2]])
-    stacked = lax.all_to_all(
-        jnp.broadcast_to(near[None], (4, 4, 16, 8, 2 * TOKENS)), "t", 0, 0, tiled=True
-    )
     place = lax.axis_index("dp").astype(jnp.int32).reshape(1)
-    side, square = turn_tokens(place, stacked.reshape(4, 4, 8, 2, 8, 2 * TOKENS))
+    turned = turn_tokens(place, near)
+    side = lax.all_to_all(turned, "t", 0, 0, tiled=True)
+    rows = rows.reshape(8, 4, 64, WIDTH)
     core = lax.axis_index("c").astype(jnp.int32).reshape(1)
-    sent = partial_hidden(1 - core, side, square, rows)
+    sent = partial_hidden(1 - core, side, rows)
     other = lax.ppermute(sent, "c", [(0, 1), (1, 0)])
-    own = partial_hidden(core, side, square, rows)
+    own = partial_hidden(core, side, rows)
     terms = label_pairs(own, other, pair_ids, class_head[0])
     every_term = lax.all_to_all(
         jnp.broadcast_to(terms[None], (16, PAIRS, 256)), ("dp", "t"), 0, 0, tiled=True

time: 216 us -> 211 us (0.977)
  Pallas kernels: 35.6 us -> 29.8 us
    pallas_call x1, Pallas kernels: 6.24 us -> 2.87 us  [turn_tokens(): pl.pallas_call(turn_tokens_kernel, grid_spec=pltpu.PrefetchScalarGridSpec...]
  transfers between devices with their start and end apart: 8 -> 8, of which waited for: 5 -> 5; matrix products, arithmetic and copies ran while one was open for 1% -> 1% of each run, Pallas kernels for 12% -> 10%
where the time goes in v5:
time: 211 us; the launch traced here: 210 us
  waiting for transfers between devices  85.2 us (40%)
  blocking collectives  42.3 us (20%)
  starting transfers between devices  32 us (15%)
  Pallas kernels  29.8 us (14%)
  between operations  14.2 us (7%)
  local copies, waits for them, and re-layouts  5.39 us (3%)
    reduce_scatter x1, waiting for transfers between devices, shards(): lax.psum_scatter(grad_parts[0], 'dp', scatter_dimension=0, tiled=True)  41.1 us
    all_to_all x1, waiting for transfers between devices, shards(): side = lax.all_to_all(turned, 't', 0, 0, tiled=True)  25.7 us
    all_to_all x1, blocking collectives, shards(): lax.all_to_all(columns.reshape(8, 32, WIDTH), ('yl', 'dp'), 0, 0, tiled=T...  17.2 us
    all_to_all x1, blocking collectives, shards(): lax.all_to_all(jnp.broadcast_to(terms[None], (16, PAIRS, 256)), ('dp', 't...  13.5 us
    all_to_all x1, starting transfers between devices, shards(): lax.all_to_all(jnp.broadcast_to(token_ids[None], (32, 1, TOKENS)), ('z',...  12.8 us
    ppermute x3, waiting for transfers between devices, shards(): parts.append(lax.ppermute(received, 'dp', [(i, i ^ k) for i in range(4)]))  12.2 us
    pallas_call x1, Pallas kernels, pick_tokens(): pl.pallas_call(pick_kernel, grid=(chips,), in_specs=[pl.BlockSpec((1, 1,...  11.8 us
    all_to_all x1, blocking collectives, shards(): received = lax.all_to_all(picked, ('z', 'yl'), 0, 0, tiled=True)  11.6 us
  transfers between devices with their start and end apart: 8, of which 5 were waited for; matrix products, arithmetic and copies ran while one was open for 1% of the time, Pallas kernels for 10%

profile of v5, /device:TPU:1, one launch (start us, length us, event | category | flops | bytes accessed | tf_op | source)
XLA Modules:
  0.0 210.3 jit_solution(18346806121157843298)
XLA Ops:
  7.2 0.0 reduce-scatter.2.cloned.1.call-start
  7.2 0.7 reduce-scatter.2.cloned.1.call-update
  7.9 0.0 all-gather.2.cloned.1.call-start
  8.0 41.1 %reduce-scatter.2.cloned.1.call-done.gradient_ref = bf16[32,3584]{1,0:T(8,128)(2,1)} async-done(((bf16[128,3584]{1,0:T(8,128)(2,1)}), bf16[32,3584]{1,0:T(8,128)(2,1)}) %reduce-scatter.2.cloned.1.call-update) | async-done | bytes 229392 | tf_op jit(solution)/shard_map/reduce_scatter | solution.py:244
  49.0 1.0 copy-done.2
  50.0 1.0 copy-done.3
  51.1 0.9 copy-done.4
  52.0 0.9 copy-done.5
  52.9 3.3 %optimizer_step.1 = (f32[32,3584]{1,0:T(8,128)}, bf16[32,3584]{1,0:T(8,128)(2,1)}, bf16[32,3584]{1,0:T(8,128)(2,1)}, f32[32,3584]{1,0:T(8,128)}, bf16[2,4,32,896]{3,2,1,0:T(8,128)(2,1)S(1)}) custom-call(f32[32,3584]{1,0:T(8,128)S(1)} %copy-done.2, bf16[32,3584]{1,0:T(8,128)(2,1)S(1)} %copy-done.4, bf16[32,3584]{1,0:T(8,128)(2,1)S(1)} %copy-done.5, ...), custom_call_target="tpu_custom_call" | custom-call | flops 2097152 | bytes 8388608 | tf_op jit(solution)/shard_map/optimizer_step/pallas_call | solution.py:52
  56.3 17.2 %all_to_all.25 = bf16[8,32,896]{2,1,0:T(8,128)(2,1)S(1)} all-to-all(bf16[8,32,896]{2,1,0:T(8,128)(2,1)S(1)} %bitcast.22), channel_id=1, replica_groups=mesh['z'=8,'yl'=2,'c'=2,'dp'=4,'t'=4] {'yl','dp'}, dimensions={0} | all-to-all | bytes 917504 | tf_op jit(solution)/shard_map/all_to_all | solution.py:253
  73.4 0.8 copy.16
  74.3 0.6 broadcast_in_dim.18
  74.9 12.8 %all-to-all-start = ((s32[32,1,256]{2,1,0:T(1,128)}), s32[32,1,256]{2,1,0:T(1,128)S(1)}, u32[]{:S(2)}, u32[]{:S(2)}) async-start(s32[32,1,256]{2,1,0:T(1,128)} %broadcast_in_dim.18), calls=%async_computation.1 | async-start | bytes 65536 | tf_op jit(solution)/shard_map/all_to_all | solution.py:241
  87.7 2.5 %turn_table.1.table_ref = bf16[1024,512]{1,0:T(8,128)(2,1)S(1)} custom-call(bf16[501,8,128]{2,1,0:T(8,128)(2,1)S(1)} %bitcast.20), custom_call_target="tpu_custom_call" | custom-call | bytes 16777216 | tf_op jit(solution)/shard_map/turn_table/pallas_call | solution.py:85
  90.3 5.6 %all-to-all-done = s32[32,1,256]{2,1,0:T(1,128)S(1)} async-done(((s32[32,1,256]{2,1,0:T(1,128)}), s32[32,1,256]{2,1,0:T(1,128)S(1)}, u32[]{:S(2)}, u32[]{:S(2)}) %all-to-all-start) | async-done | bytes 32800 | tf_op jit(solution)/shard_map/all_to_all | solution.py:241
  95.8 11.8 %pick_tokens.1 = bf16[16,8,512]{2,1,0:T(8,128)(2,1)S(1)} custom-call(s32[16,1,512]{2,1,0:T(1,128)S(1)} %bitcast.23, bf16[1024,512]{1,0:T(8,128)(2,1)S(1)} %turn_table.1.table_ref), custom_call_target="tpu_custom_call" | custom-call | flops 8589934592 | bytes 2097152 | tf_op jit(solution)/shard_map/pick_tokens/pallas_call | solution.py:114
  107.6 11.6 %all_to_all.26 = bf16[16,8,512]{2,1,0:T(8,128)(2,1)S(1)} all-to-all(bf16[16,8,512]{2,1,0:T(8,128)(2,1)S(1)} %pick_tokens.1), channel_id=1, replica_groups=mesh['z'=8,'yl'=2,'c'=2,'dp'=4,'t'=4] {'z','yl'}, dimensions={0} | all-to-all | bytes 262144 | tf_op jit(solution)/shard_map/all_to_all | solution.py:247
  119.2 2.3 %collective-permute-start.2 = (bf16[16,8,512]{2,1,0:T(8,128)(2,1)S(1)}, bf16[16,8,512]{2,1,0:T(8,128)(2,1)S(1)}, u32[]{:S(2)}, u32[]{:S(2)}) collective-permute-start(bf16[16,8,512]{2,1,0:T(8,128)(2,1)S(1)} %all_to_all.26), channel_id=1, source_target_pairs={{0,12},{4,8},{8,4},{12,0},{1,13},{5,9},{9,5},{13,1},{2,14},{6,10},... | collective-permute-start | bytes 393224 | tf_op jit(solution)/shard_map/ppermute | solution.py:258
  121.6 4.9 %collective-permute-start.1 = (bf16[16,8,512]{2,1,0:T(8,128)(2,1)S(1)}, bf16[16,8,512]{2,1,0:T(8,128)(2,1)S(1)}, u32[]{:S(2)}, u32[]{:S(2)}) collective-permute-start(bf16[16,8,512]{2,1,0:T(8,128)(2,1)S(1)} %all_to_all.26), channel_id=1, source_target_pairs={{0,8},{4,12},{8,0},{12,4},{1,9},{5,13},{9,1},{13,5},{2,10},{6,14},... | collective-permute-start | bytes 393224 | tf_op jit(solution)/shard_map/ppermute | solution.py:258
  126.4 4.2 %collective-permute-start = (bf16[16,8,512]{2,1,0:T(8,128)(2,1)S(1)}, bf16[16,8,512]{2,1,0:T(8,128)(2,1)S(1)}, u32[]{:S(2)}, u32[]{:S(2)}) collective-permute-start(bf16[16,8,512]{2,1,0:T(8,128)(2,1)S(1)} %all_to_all.26), channel_id=1, source_target_pairs={{0,4},{4,0},{8,12},{12,8},{1,5},{5,1},{9,13},{13,9},{2,6},{6,2},{1... | collective-permute-start | bytes 393224 | tf_op jit(solution)/shard_map/ppermute | solution.py:258
  130.6 4.2 %collective-permute-done.1 = bf16[16,8,512]{2,1,0:T(8,128)(2,1)S(1)} collective-permute-done((bf16[16,8,512]{2,1,0:T(8,128)(2,1)S(1)}, bf16[16,8,512]{2,1,0:T(8,128)(2,1)S(1)}, u32[]{:S(2)}, u32[]{:S(2)}) %collective-permute-start.1) | collective-permute-done | bytes 131104 | tf_op jit(solution)/shard_map/ppermute | solution.py:258
  134.8 8.0 %collective-permute-done = bf16[16,8,512]{2,1,0:T(8,128)(2,1)S(1)} collective-permute-done((bf16[16,8,512]{2,1,0:T(8,128)(2,1)S(1)}, bf16[16,8,512]{2,1,0:T(8,128)(2,1)S(1)}, u32[]{:S(2)}, u32[]{:S(2)}) %collective-permute-start) | collective-permute-done | bytes 131104 | tf_op jit(solution)/shard_map/ppermute | solution.py:258
  142.8 0.9 pad_maximum_fusion.in_ref
  143.7 2.9 %turn_tokens.1 = bf16[4,512,512]{2,1,0:T(8,128)(2,1)} custom-call(s32[1]{0:T(128)} %bitcast.2.place_ref, bf16[4,16,8,512]{3,2,1,0:T(8,128)(2,1)} %pad_maximum_fusion.in_ref), custom_call_target="tpu_custom_call" | custom-call | flops 2097152 | bytes 4194304 | tf_op jit(solution)/shard_map/turn_tokens/pallas_call | solution.py:145
  146.6 4.1 %all-to-all-start.2 = ((bf16[4,512,512]{2,1,0:T(8,128)(2,1)}), bf16[4,512,512]{2,1,0:T(8,128)(2,1)S(1)}, u32[]{:S(2)}, u32[]{:S(2)}) async-start(bf16[4,512,512]{2,1,0:T(8,128)(2,1)} %turn_tokens.1), calls=%async_computation.3 | async-start | bytes 4194304 | tf_op jit(solution)/shard_map/all_to_all | solution.py:262
  150.7 25.7 %all-to-all-done.2.side_ref = bf16[4,512,512]{2,1,0:T(8,128)(2,1)S(1)} async-done(((bf16[4,512,512]{2,1,0:T(8,128)(2,1)}), bf16[4,512,512]{2,1,0:T(8,128)(2,1)S(1)}, u32[]{:S(2)}, u32[]{:S(2)}) %all-to-all-start.2) | async-done | bytes 2097184 | tf_op jit(solution)/shard_map/all_to_all | solution.py:262
  176.3 4.2 %partial_hidden.3 = f32[256,1024]{1,0:T(8,128)S(1)} custom-call(s32[1]{0:T(128)S(6)} %sub.3.group_ref, bf16[4,512,512]{2,1,0:T(8,128)(2,1)S(1)} %all-to-all-done.2.side_ref, bf16[8,4,64,896]{3,2,1,0:T(8,128)(2,1)} %bitcast.24), custom_call_target="tpu_custom_call" | custom-call | flops 939524096 | bytes 6291456 | tf_op jit(solution)/shard_map/partial_hidden/pallas_call | solution.py:178
  180.5 3.7 %collective-permute-start.3 = (f32[256,1024]{1,0:T(8,128)S(1)}, f32[256,1024]{1,0:T(8,128)S(1)}, u32[]{:S(2)}, u32[]{:S(2)}) collective-permute-start(f32[256,1024]{1,0:T(8,128)S(1)} %partial_hidden.3), channel_id=1, source_target_pairs={{0,16},{16,0},{1,17},{17,1},{2,18},{18,2},{3,19},{19,3},{4,20},{20... | collective-permute-start | bytes 3145736 | tf_op jit(solution)/shard_map/ppermute | solution.py:266
  184.2 4.2 %partial_hidden.2.own_ref = f32[256,1024]{1,0:T(8,128)S(1)} custom-call(s32[1]{0:T(128)} %bitcast.1.group_ref, bf16[4,512,512]{2,1,0:T(8,128)(2,1)S(1)} %all-to-all-done.2.side_ref, bf16[8,4,64,896]{3,2,1,0:T(8,128)(2,1)} %bitcast.25), custom_call_target="tpu_custom_call" | custom-call | flops 939524096 | bytes 6291456 | tf_op jit(solution)/shard_map/partial_hidden/pallas_call | solution.py:178
  188.4 0.9 label_pairs.1
  189.4 13.5 %all_to_all.27 = f32[16,8,256]{2,1,0:T(8,128)S(1)} all-to-all(f32[16,8,256]{2,1,0:T(8,128)S(1)} %broadcast_in_dim.19), channel_id=1, replica_groups=mesh['z'=8,'yl'=2,'c'=2,'dp'=4,'t'=4] {'dp','t'}, dimensions={0} | all-to-all | bytes 262144 | tf_op jit(solution)/shard_map/all_to_all | solution.py:269
  202.9 0.6 reduce_sum.9
  (17 shorter events, 0.1 us)
Async XLA Ops:
  7.2 41.9 %reduce-scatter.2.cloned.1.call-start = ((), (), s32[]{:S(2)}) async-start(), calls=%async_computation.6 | async-start | bytes 1146880 | tf_op jit(solution)/shard_map/reduce_scatter | solution.py:244
  7.2 67.1 %copy-start.7 = (s32[1,256]{1,0:T(1,128)S(1)}, s32[1,256]{1,0:T(1,128)}, u32[]{:S(2)}) copy-start(s32[1,256]{1,0:T(1,128)} %param.15) | copy-start | bytes 3076
  7.9 79.8 %copy-start = (bf16[8,64128]{1,0:T(8,128)(2,1)S(1)}, bf16[8,64128]{1,0:T(8,128)(2,1)}, u32[]{:S(2)}) copy-start(bf16[8,64128]{1,0:T(8,128)(2,1)} %param.14) | copy-start | bytes 3078148
  7.9 168.4 %all-gather.2.cloned.1.call-start = ((), (), s32[]{:S(2)}) async-start(), calls=%async_computation.7 | async-start | bytes 4128768 | tf_op jit(solution)/shard_map/all_gather | solution.py:255
  49.0 1.0 copy-start.2
  50.0 1.0 copy-start.3
  51.1 0.9 copy-start.4
  52.0 0.9 copy-start.5
  74.9 20.9 %all-to-all-start = ((s32[32,1,256]{2,1,0:T(1,128)}), s32[32,1,256]{2,1,0:T(1,128)S(1)}, u32[]{:S(2)}, u32[]{:S(2)}) async-start(s32[32,1,256]{2,1,0:T(1,128)} %broadcast_in_dim.18), calls=%async_computation.1 | async-start | bytes 65536 | tf_op jit(solution)/shard_map/all_to_all | solution.py:241
  119.2 11.4 %collective-permute-start.2 = (bf16[16,8,512]{2,1,0:T(8,128)(2,1)S(1)}, bf16[16,8,512]{2,1,0:T(8,128)(2,1)S(1)}, u32[]{:S(2)}, u32[]{:S(2)}) collective-permute-start(bf16[16,8,512]{2,1,0:T(8,128)(2,1)S(1)} %all_to_all.26), channel_id=1, source_target_pairs={{0,12},{4,8},{8,4},{12,0},{1,13},{5,9},{9,5},{13,1},{2,14},{6,10},... | collective-permute-start | bytes 393224 | tf_op jit(solution)/shard_map/ppermute | solution.py:258
  121.6 13.2 %collective-permute-start.1 = (bf16[16,8,512]{2,1,0:T(8,128)(2,1)S(1)}, bf16[16,8,512]{2,1,0:T(8,128)(2,1)S(1)}, u32[]{:S(2)}, u32[]{:S(2)}) collective-permute-start(bf16[16,8,512]{2,1,0:T(8,128)(2,1)S(1)} %all_to_all.26), channel_id=1, source_target_pairs={{0,8},{4,12},{8,0},{12,4},{1,9},{5,13},{9,1},{13,5},{2,10},{6,14},... | collective-permute-start | bytes 393224 | tf_op jit(solution)/shard_map/ppermute | solution.py:258
  126.4 16.4 %collective-permute-start = (bf16[16,8,512]{2,1,0:T(8,128)(2,1)S(1)}, bf16[16,8,512]{2,1,0:T(8,128)(2,1)S(1)}, u32[]{:S(2)}, u32[]{:S(2)}) collective-permute-start(bf16[16,8,512]{2,1,0:T(8,128)(2,1)S(1)} %all_to_all.26), channel_id=1, source_target_pairs={{0,4},{4,0},{8,12},{12,8},{1,5},{5,1},{9,13},{13,9},{2,6},{6,2},{1... | collective-permute-start | bytes 393224 | tf_op jit(solution)/shard_map/ppermute | solution.py:258
  146.6 29.8 %all-to-all-start.2 = ((bf16[4,512,512]{2,1,0:T(8,128)(2,1)}), bf16[4,512,512]{2,1,0:T(8,128)(2,1)S(1)}, u32[]{:S(2)}, u32[]{:S(2)}) async-start(bf16[4,512,512]{2,1,0:T(8,128)(2,1)} %turn_tokens.1), calls=%async_computation.3 | async-start | bytes 4194304 | tf_op jit(solution)/shard_map/all_to_all | solution.py:262
  180.5 7.9 %copy-start.1 = (bf16[1,896,256]{2,1,0:T(8,128)(2,1)S(1)}, bf16[1,896,256]{2,1,0:T(8,128)(2,1)}, u32[]{:S(2)}) copy-start(bf16[1,896,256]{2,1,0:T(8,128)(2,1)} %param.17) | copy-start | bytes 1376260
  180.5 7.9 %copy-start.6 = (s32[1,256]{1,0:T(1,128)S(1)}, s32[1,256]{1,0:T(1,128)}, u32[]{:S(2)}) copy-start(s32[1,256]{1,0:T(1,128)} %pair_ref.1) | copy-start | bytes 3076
  180.5 7.9 %collective-permute-start.3 = (f32[256,1024]{1,0:T(8,128)S(1)}, f32[256,1024]{1,0:T(8,128)S(1)}, u32[]{:S(2)}, u32[]{:S(2)}) collective-permute-start(f32[256,1024]{1,0:T(8,128)S(1)} %partial_hidden.3), channel_id=1, source_target_pairs={{0,16},{16,0},{1,17},{17,1},{2,18},{18,2},{3,19},{19,3},{4,20},{20... | collective-permute-start | bytes 3145736 | tf_op jit(solution)/shard_map/ppermute | solution.py:266
Sparse Core Ops, SparseCore 0:
  10.8 38.1 reduce-scatter.1
  74.4 57.2 all-gather.1

commit v6 on v5

--- a/solution.py
+++ b/solution.py
@@ -24,10 +24,7 @@
 VMEM = pltpu.VMEM
 
 
-def optimizer_kernel(
-    master_ref, first_ref, second_ref, teacher_ref, gradient_ref,
-    master_out, first_out, second_out, teacher_out, columns_out,
-):
+def updated(master_ref, first_ref, second_ref, teacher_ref, gradient_ref):
     gradient = gradient_ref[...].astype(f32)
     first_full = beta_one * first_ref[...].astype(f32) + (1.0 - beta_one) * gradient
     second_full = (
@@ -38,36 +35,56 @@
         first_full / (jnp.sqrt(second_full) + 1e-08) + decay_rate * master
     )
     teacher_new = ema_keep * teacher_ref[...] + (1.0 - ema_keep) * master_new
-    master_out[...] = master_new
-    first_out[...] = first_full.astype(bf16)
-    second_out[...] = second_full.astype(bf16)
-    teacher_out[...] = teacher_new
+    return master_new, first_full, second_full, teacher_new
+
+
+def columns_kernel(master_ref, first_ref, second_ref, teacher_ref, gradient_ref, columns_out):
+    teacher = updated(master_ref, first_ref, second_ref, teacher_ref, gradient_ref)[3]
     for line in range(2):
-        columns_out[line, 0] = teacher_new.astype(bf16)
-
-
-def optimizer_step(master_weight, first_moment, second_moment, teacher_weight, gradient):
-    block = pl.BlockSpec((32, WIDTH), lambda k: (0, k))
-    shape = master_weight.shape
+        columns_out[line, 0] = teacher.astype(bf16)
+
+
+def optimizer_kernel(
+    master_ref, first_ref, second_ref, teacher_ref, gradient_ref,
+    master_out, first_out, second_out, teacher_out,
+):
+    master, first, second, teacher = updated(
+        master_ref, first_ref, second_ref, teacher_ref, gradient_ref
+    )
+    master_out[...] = master
+    first_out[...] = first.astype(bf16)
+    second_out[...] = second.astype(bf16)
+    teacher_out[...] = teacher
+
+
+BLOCK = pl.BlockSpec((32, WIDTH), lambda k: (0, k))
+UPDATE = dict(
+    grid=(4,),
+    in_specs=[BLOCK] * 5,
+    cost_estimate=pl.CostEstimate(flops=1 << 21, bytes_accessed=1 << 22, transcendentals=0),
+    compiler_params=pltpu.CompilerParams(vmem_limit_bytes=16 << 20),
+)
+
+
+def teacher_columns(*state):
+    return pl.pallas_call(
+        columns_kernel,
+        out_specs=pl.BlockSpec((2, 1, 32, WIDTH), lambda k: (0, k, 0, 0)),
+        out_shape=jax.ShapeDtypeStruct((2, 4, 32, WIDTH), bf16),
+        name="teacher_columns",
+        **UPDATE,
+    )(*state)
+
+
+def optimizer_step(*state):
+    shape = state[0].shape
     return pl.pallas_call(
         optimizer_kernel,
-        grid=(4,),
-        in_specs=[block] * 5,
-        out_specs=[block] * 4 + [pl.BlockSpec((2, 1, 32, WIDTH), lambda k: (0, k, 0, 0))],
-        out_shape=[
-            jax.ShapeDtypeStruct(shape, f32),
-            jax.ShapeDtypeStruct(shape, bf16),
-            jax.ShapeDtypeStruct(shape, bf16),
-            jax.ShapeDtypeStruct(shape, f32),
-            jax.ShapeDtypeStruct((2, 4, 32, WIDTH), bf16),
-        ],
-        cost_estimate=pl.CostEstimate(flops=1 << 21, bytes_accessed=1 << 23, transcendentals=0),
-        compiler_params=pltpu.CompilerParams(vmem_limit_bytes=16 << 20),
+        out_specs=[BLOCK] * 4,
+        out_shape=[jax.ShapeDtypeStruct(shape, kind) for kind in (f32, bf16, bf16, f32)],
         name="optimizer_step",
-    )(
-        master_weight, first_moment, second_moment, teacher_weight,
-        pltpu.with_memory_space_constraint(gradient, pltpu.HBM),
-    )
+        **UPDATE,
+    )(*state)
 
 
 def turn_table_kernel(table_ref, out_ref, wide, turned):
@@ -95,7 +112,7 @@
 
 
 def pick_kernel(ids_ref, table_ref, out_ref):
-    ids = ids_ref[0]
+    ids = jnp.concatenate([ids_ref[0], ids_ref[1]], axis=1)
     count = ids.shape[1]
     upper = ids >> 7
     lower = jnp.broadcast_to(ids & 127, (8, count))
@@ -110,12 +127,12 @@
 
 
 def pick_tokens(ids, table):
-    chips, _, count = ids.shape
+    chips, count = ids.shape[0] // 2, 2 * ids.shape[2]
     return pl.pallas_call(
         pick_kernel,
         grid=(chips,),
         in_specs=[
-            pl.BlockSpec((1, 1, count), lambda i: (i, 0, 0)),
+            pl.BlockSpec((2, 1, TOKENS), lambda i: (i, 0, 0)),
             pl.BlockSpec((1024, UPPER), lambda i: (0, 0)),
         ],
         out_specs=pl.BlockSpec((1, 8, count), lambda i: (i, 0, 0)),
@@ -243,13 +260,16 @@
     )
     gradient = lax.psum_scatter(grad_parts[0], "dp", scatter_dimension=0, tiled=True)
     table = turn_table(embed_table)
-    picked = pick_tokens(every_id.reshape(16, 1, 2 * TOKENS), table)
+    picked = pick_tokens(every_id, table)
     received = lax.all_to_all(
         picked, ("z", "yl"), 0, 0, tiled=True
     )
-    master_new, first_new, second_new, teacher_new, columns = optimizer_step(
-        master_weight, first_moment, second_moment, teacher_weight, gradient
-    )
+    state = (
+        master_weight, first_moment, second_moment, teacher_weight,
+        pltpu.with_memory_space_constraint(gradient, pltpu.HBM),
+    )
+    columns = teacher_columns(*state)
+    master_new, first_new, second_new, teacher_new = optimizer_step(*state)
     block = lax.all_to_all(columns.reshape(8, 32, WIDTH), ("yl", "dp"), 0, 0, tiled=True)
     sorted_block = block.reshape(8, 4, 8, WIDTH).transpose(1, 0, 2, 3).reshape(256, WIDTH)
     rows = lax.all_gather(sorted_block, "z", axis=0, tiled=True)

time: 211 us -> 210 us (level)
  the two profiles are of different devices: /device:TPU:1 before, /device:TPU:8 now
where the time goes in v6:
time: 210 us; the launch traced here: 209 us
  waiting for transfers between devices  91 us (43%)
  starting transfers between devices  32.3 us (15%)
  Pallas kernels  32.1 us (15%)
  blocking collectives  31.9 us (15%)
  between operations  14.3 us (7%)
  local copies, waits for them, and re-layouts  6.08 us (3%)
    reduce_scatter x1, waiting for transfers between devices, shards(): lax.psum_scatter(grad_parts[0], 'dp', scatter_dimension=0, tiled=True)  42.5 us
    all_to_all x1, waiting for transfers between devices, shards(): side = lax.all_to_all(turned, 't', 0, 0, tiled=True)  26.5 us
    all_to_all x1, blocking collectives, shards(): lax.all_to_all(columns.reshape(8, 32, WIDTH), ('yl', 'dp'), 0, 0, tiled=T...  18.7 us
    all_to_all x1, blocking collectives, shards(): received = lax.all_to_all(picked, ('z', 'yl'), 0, 0, tiled=True)  13.2 us
    ppermute x3, starting transfers between devices, shards(): parts.append(lax.ppermute(received, 'dp', [(i, i ^ k) for i in range(4)]))  12.2 us
    pallas_call x1, Pallas kernels, pick_tokens(): pl.pallas_call(pick_kernel, grid=(chips,), in_specs=[pl.BlockSpec((2, 1,...  11.8 us
    ppermute x3, waiting for transfers between devices, shards(): parts.append(lax.ppermute(received, 'dp', [(i, i ^ k) for i in range(4)]))  9.12 us
    all_to_all x1, starting transfers between devices, shards(): lax.all_to_all(jnp.broadcast_to(token_ids[None], (32, 1, TOKENS)), ('z',...  8.85 us
  transfers between devices with their start and end apart: 9, of which 6 were waited for; matrix products, arithmetic and copies ran while one was open for 1% of the time, Pallas kernels for 12%

profile of v6, /device:TPU:8, one launch (start us, length us, event | category | flops | bytes accessed | tf_op | source)
XLA Modules:
  0.0 209.2 jit_solution(4804739196262725745)
XLA Ops:
  7.2 0.7 reduce-scatter.2.cloned.1.call-update
  7.9 42.5 %reduce-scatter.2.cloned.1.call-done.gradient_ref = bf16[32,3584]{1,0:T(8,128)(2,1)} async-done(((bf16[128,3584]{1,0:T(8,128)(2,1)}), bf16[32,3584]{1,0:T(8,128)(2,1)}) %reduce-scatter.2.cloned.1.call-update) | async-done | bytes 229392 | tf_op jit(solution)/shard_map/reduce_scatter | solution.py:261
  50.4 1.0 copy-done
  51.4 1.0 copy-done.2
  52.5 0.9 copy-done.5
  53.4 0.9 copy-done.7
  54.3 2.2 %teacher_columns.1 = bf16[2,4,32,896]{3,2,1,0:T(8,128)(2,1)S(1)} custom-call(f32[32,3584]{1,0:T(8,128)S(1)} %copy-done, bf16[32,3584]{1,0:T(8,128)(2,1)S(1)} %copy-done.5, bf16[32,3584]{1,0:T(8,128)(2,1)S(1)} %copy-done.7, f32[32,3584]{1,0:T(8,128)S(1)} %copy-done.2, bf16[32,3584]{1,0:T(8,128)(2,1)} %reduce-scatter.2.cloned.1.call-done.gradient_ref), custom_call_target="tpu_custom_call" | custom-call | flops 2097152 | bytes 4194304 | tf_op jit(solution)/shard_map/teacher_columns/pallas_call | solution.py:70
  56.6 18.7 %all_to_all.25 = bf16[8,32,896]{2,1,0:T(8,128)(2,1)S(1)} all-to-all(bf16[8,32,896]{2,1,0:T(8,128)(2,1)S(1)} %bitcast.19), channel_id=1, replica_groups=mesh['z'=8,'yl'=2,'c'=2,'dp'=4,'t'=4] {'yl','dp'}, dimensions={0} | all-to-all | bytes 917504 | tf_op jit(solution)/shard_map/all_to_all | solution.py:273
  75.3 0.8 copy.15
  76.1 0.6 broadcast_in_dim.18
  76.7 8.8 %all-to-all-start = ((s32[32,1,256]{2,1,0:T(1,128)}), s32[32,1,256]{2,1,0:T(1,128)S(1)}, u32[]{:S(2)}, u32[]{:S(2)}) async-start(s32[32,1,256]{2,1,0:T(1,128)} %broadcast_in_dim.18), calls=%async_computation.1 | async-start | bytes 65536 | tf_op jit(solution)/shard_map/all_to_all | solution.py:258
  85.6 2.5 %turn_table.1.table_ref = bf16[1024,512]{1,0:T(8,128)(2,1)S(1)} custom-call(bf16[501,8,128]{2,1,0:T(8,128)(2,1)S(1)} %bitcast.20), custom_call_target="tpu_custom_call" | custom-call | bytes 16777216 | tf_op jit(solution)/shard_map/turn_table/pallas_call | solution.py:102
  88.2 4.8 %all-to-all-done.ids_ref = s32[32,1,256]{2,1,0:T(1,128)S(1)} async-done(((s32[32,1,256]{2,1,0:T(1,128)}), s32[32,1,256]{2,1,0:T(1,128)S(1)}, u32[]{:S(2)}, u32[]{:S(2)}) %all-to-all-start) | async-done | bytes 32800 | tf_op jit(solution)/shard_map/all_to_all | solution.py:258
  93.0 11.8 %pick_tokens.1 = bf16[16,8,512]{2,1,0:T(8,128)(2,1)S(1)} custom-call(s32[32,1,256]{2,1,0:T(1,128)S(1)} %all-to-all-done.ids_ref, bf16[1024,512]{1,0:T(8,128)(2,1)S(1)} %turn_table.1.table_ref), custom_call_target="tpu_custom_call" | custom-call | flops 8589934592 | bytes 2097152 | tf_op jit(solution)/shard_map/pick_tokens/pallas_call | solution.py:131
  104.8 13.2 %all_to_all.26 = bf16[16,8,512]{2,1,0:T(8,128)(2,1)S(1)} all-to-all(bf16[16,8,512]{2,1,0:T(8,128)(2,1)S(1)} %pick_tokens.1), channel_id=1, replica_groups=mesh['z'=8,'yl'=2,'c'=2,'dp'=4,'t'=4] {'z','yl'}, dimensions={0} | all-to-all | bytes 262144 | tf_op jit(solution)/shard_map/all_to_all | solution.py:264
  118.1 2.2 %collective-permute-start = (bf16[16,8,512]{2,1,0:T(8,128)(2,1)S(1)}, bf16[16,8,512]{2,1,0:T(8,128)(2,1)S(1)}, u32[]{:S(2)}, u32[]{:S(2)}) collective-permute-start(bf16[16,8,512]{2,1,0:T(8,128)(2,1)S(1)} %all_to_all.26), channel_id=1, source_target_pairs={{0,4},{4,0},{8,12},{12,8},{1,5},{5,1},{9,13},{13,9},{2,6},{6,2},{1... | collective-permute-start | bytes 393224 | tf_op jit(solution)/shard_map/ppermute | solution.py:278
  120.2 4.6 %collective-permute-start.1 = (bf16[16,8,512]{2,1,0:T(8,128)(2,1)S(1)}, bf16[16,8,512]{2,1,0:T(8,128)(2,1)S(1)}, u32[]{:S(2)}, u32[]{:S(2)}) collective-permute-start(bf16[16,8,512]{2,1,0:T(8,128)(2,1)S(1)} %all_to_all.26), channel_id=1, source_target_pairs={{0,8},{4,12},{8,0},{12,4},{1,9},{5,13},{9,1},{13,5},{2,10},{6,14},... | collective-permute-start | bytes 393224 | tf_op jit(solution)/shard_map/ppermute | solution.py:278
  124.9 5.4 %collective-permute-start.2 = (bf16[16,8,512]{2,1,0:T(8,128)(2,1)S(1)}, bf16[16,8,512]{2,1,0:T(8,128)(2,1)S(1)}, u32[]{:S(2)}, u32[]{:S(2)}) collective-permute-start(bf16[16,8,512]{2,1,0:T(8,128)(2,1)S(1)} %all_to_all.26), channel_id=1, source_target_pairs={{0,12},{4,8},{8,4},{12,0},{1,13},{5,9},{9,5},{13,1},{2,14},{6,10},... | collective-permute-start | bytes 393224 | tf_op jit(solution)/shard_map/ppermute | solution.py:278
  130.3 4.0 %collective-permute-done.1 = bf16[16,8,512]{2,1,0:T(8,128)(2,1)S(1)} collective-permute-done((bf16[16,8,512]{2,1,0:T(8,128)(2,1)S(1)}, bf16[16,8,512]{2,1,0:T(8,128)(2,1)S(1)}, u32[]{:S(2)}, u32[]{:S(2)}) %collective-permute-start.1) | collective-permute-done | bytes 131104 | tf_op jit(solution)/shard_map/ppermute | solution.py:278
  134.3 5.1 %collective-permute-done.2 = bf16[16,8,512]{2,1,0:T(8,128)(2,1)S(1)} collective-permute-done((bf16[16,8,512]{2,1,0:T(8,128)(2,1)S(1)}, bf16[16,8,512]{2,1,0:T(8,128)(2,1)S(1)}, u32[]{:S(2)}, u32[]{:S(2)}) %collective-permute-start.2) | collective-permute-done | bytes 131104 | tf_op jit(solution)/shard_map/ppermute | solution.py:278
  139.4 0.9 pad_maximum_fusion.in_ref
  140.3 2.9 %turn_tokens.1 = bf16[4,512,512]{2,1,0:T(8,128)(2,1)} custom-call(s32[1]{0:T(128)} %bitcast.2.place_ref, bf16[4,16,8,512]{3,2,1,0:T(8,128)(2,1)} %pad_maximum_fusion.in_ref), custom_call_target="tpu_custom_call" | custom-call | flops 2097152 | bytes 4194304 | tf_op jit(solution)/shard_map/turn_tokens/pallas_call | solution.py:162
  143.2 4.4 %all-to-all-start.2 = ((bf16[4,512,512]{2,1,0:T(8,128)(2,1)}), bf16[4,512,512]{2,1,0:T(8,128)(2,1)S(1)}, u32[]{:S(2)}, u32[]{:S(2)}) async-start(bf16[4,512,512]{2,1,0:T(8,128)(2,1)} %turn_tokens.1), calls=%async_computation.3 | async-start | bytes 4194304 | tf_op jit(solution)/shard_map/all_to_all | solution.py:282
  147.6 26.5 %all-to-all-done.2.side_ref = bf16[4,512,512]{2,1,0:T(8,128)(2,1)S(1)} async-done(((bf16[4,512,512]{2,1,0:T(8,128)(2,1)}), bf16[4,512,512]{2,1,0:T(8,128)(2,1)S(1)}, u32[]{:S(2)}, u32[]{:S(2)}) %all-to-all-start.2) | async-done | bytes 2097184 | tf_op jit(solution)/shard_map/all_to_all | solution.py:282
  174.1 4.2 %partial_hidden.3 = f32[256,1024]{1,0:T(8,128)S(1)} custom-call(s32[1]{0:T(128)S(6)} %sub.3.group_ref, bf16[4,512,512]{2,1,0:T(8,128)(2,1)S(1)} %all-to-all-done.2.side_ref, bf16[8,4,64,896]{3,2,1,0:T(8,128)(2,1)} %bitcast.22), custom_call_target="tpu_custom_call" | custom-call | flops 939524096 | bytes 6291456 | tf_op jit(solution)/shard_map/partial_hidden/pallas_call | solution.py:195
  178.3 2.1 collective-permute-start.3
  180.3 4.2 %partial_hidden.2.own_ref = f32[256,1024]{1,0:T(8,128)S(1)} custom-call(s32[1]{0:T(128)} %bitcast.1.group_ref, bf16[4,512,512]{2,1,0:T(8,128)(2,1)S(1)} %all-to-all-done.2.side_ref, bf16[8,4,64,896]{3,2,1,0:T(8,128)(2,1)} %bitcast.23), custom_call_target="tpu_custom_call" | custom-call | flops 939524096 | bytes 6291456 | tf_op jit(solution)/shard_map/partial_hidden/pallas_call | solution.py:195
  184.6 0.9 label_pairs.1
  185.5 0.7 broadcast_in_dim.19
  186.2 4.8 %all-to-all-start.4 = ((f32[16,8,256]{2,1,0:T(8,128)}), f32[16,8,256]{2,1,0:T(8,128)S(1)}, u32[]{:S(2)}, u32[]{:S(2)}) async-start(f32[16,8,256]{2,1,0:T(8,128)} %broadcast_in_dim.19), calls=%async_computation.5 | async-start | bytes 262144 | tf_op jit(solution)/shard_map/all_to_all | solution.py:289
  191.0 3.3 %optimizer_step.1 = (f32[32,3584]{1,0:T(8,128)}, bf16[32,3584]{1,0:T(8,128)(2,1)}, bf16[32,3584]{1,0:T(8,128)(2,1)}, f32[32,3584]{1,0:T(8,128)}) custom-call(f32[32,3584]{1,0:T(8,128)S(1)} %copy-done.1, bf16[32,3584]{1,0:T(8,128)(2,1)S(1)} %copy-done.6, bf16[32,3584]{1,0:T(8,128)(2,1)S(1)} %copy-done.8, f32[32,3584]{1,0:T(8,128)S(1)} %copy-done.3, ...), custom_call_target="tpu_custom_call" | custom-call | flops 2097152 | bytes 4194304 | tf_op jit(solution)/shard_map/optimizer_step/pallas_call | solution.py:81
  194.4 7.4 %all-to-all-done.4 = f32[16,8,256]{2,1,0:T(8,128)S(1)} async-done(((f32[16,8,256]{2,1,0:T(8,128)}), f32[16,8,256]{2,1,0:T(8,128)S(1)}, u32[]{:S(2)}, u32[]{:S(2)}) %all-to-all-start.4) | async-done | bytes 131104 | tf_op jit(solution)/shard_map/all_to_all | solution.py:289
  (27 shorter events, 0.8 us)
Async XLA Ops:
  7.2 43.3 %reduce-scatter.2.cloned.1.call-start = ((), (), s32[]{:S(2)}) async-start(), calls=%async_computation.6 | async-start | bytes 1146880 | tf_op jit(solution)/shard_map/reduce_scatter | solution.py:261
  7.2 68.9 %copy-start.11 = (s32[1,256]{1,0:T(1,128)S(1)}, s32[1,256]{1,0:T(1,128)}, u32[]{:S(2)}) copy-start(s32[1,256]{1,0:T(1,128)} %param.15) | copy-start | bytes 3076
  7.9 166.2 %all-gather.2.cloned.1.call-start = ((), (), s32[]{:S(2)}) async-start(), calls=%async_computation.7 | async-start | bytes 4128768 | tf_op jit(solution)/shard_map/all_gather | solution.py:275
  50.4 1.0 copy-start
  51.4 1.0 copy-start.2
  52.5 0.9 copy-start.5
  53.4 0.9 copy-start.7
  54.3 31.3 %copy-start.4 = (bf16[8,64128]{1,0:T(8,128)(2,1)S(1)}, bf16[8,64128]{1,0:T(8,128)(2,1)}, u32[]{:S(2)}) copy-start(bf16[8,64128]{1,0:T(8,128)(2,1)} %param.14) | copy-start | bytes 3078148
  76.7 16.2 %all-to-all-start = ((s32[32,1,256]{2,1,0:T(1,128)}), s32[32,1,256]{2,1,0:T(1,128)S(1)}, u32[]{:S(2)}, u32[]{:S(2)}) async-start(s32[32,1,256]{2,1,0:T(1,128)} %broadcast_in_dim.18), calls=%async_computation.1 | async-start | bytes 65536 | tf_op jit(solution)/shard_map/all_to_all | solution.py:258
  118.1 12.2 %collective-permute-start = (bf16[16,8,512]{2,1,0:T(8,128)(2,1)S(1)}, bf16[16,8,512]{2,1,0:T(8,128)(2,1)S(1)}, u32[]{:S(2)}, u32[]{:S(2)}) collective-permute-start(bf16[16,8,512]{2,1,0:T(8,128)(2,1)S(1)} %all_to_all.26), channel_id=1, source_target_pairs={{0,4},{4,0},{8,12},{12,8},{1,5},{5,1},{9,13},{13,9},{2,6},{6,2},{1... | collective-permute-start | bytes 393224 | tf_op jit(solution)/shard_map/ppermute | solution.py:278
  120.2 14.1 %collective-permute-start.1 = (bf16[16,8,512]{2,1,0:T(8,128)(2,1)S(1)}, bf16[16,8,512]{2,1,0:T(8,128)(2,1)S(1)}, u32[]{:S(2)}, u32[]{:S(2)}) collective-permute-start(bf16[16,8,512]{2,1,0:T(8,128)(2,1)S(1)} %all_to_all.26), channel_id=1, source_target_pairs={{0,8},{4,12},{8,0},{12,4},{1,9},{5,13},{9,1},{13,5},{2,10},{6,14},... | collective-permute-start | bytes 393224 | tf_op jit(solution)/shard_map/ppermute | solution.py:278
  124.9 14.5 %collective-permute-start.2 = (bf16[16,8,512]{2,1,0:T(8,128)(2,1)S(1)}, bf16[16,8,512]{2,1,0:T(8,128)(2,1)S(1)}, u32[]{:S(2)}, u32[]{:S(2)}) collective-permute-start(bf16[16,8,512]{2,1,0:T(8,128)(2,1)S(1)} %all_to_all.26), channel_id=1, source_target_pairs={{0,12},{4,8},{8,4},{12,0},{1,13},{5,9},{9,5},{13,1},{2,14},{6,10},... | collective-permute-start | bytes 393224 | tf_op jit(solution)/shard_map/ppermute | solution.py:278
  143.2 30.9 %all-to-all-start.2 = ((bf16[4,512,512]{2,1,0:T(8,128)(2,1)}), bf16[4,512,512]{2,1,0:T(8,128)(2,1)S(1)}, u32[]{:S(2)}, u32[]{:S(2)}) async-start(bf16[4,512,512]{2,1,0:T(8,128)(2,1)} %turn_tokens.1), calls=%async_computation.3 | async-start | bytes 4194304 | tf_op jit(solution)/shard_map/all_to_all | solution.py:282
  178.3 6.3 %copy-start.9 = (bf16[1,896,256]{2,1,0:T(8,128)(2,1)S(1)}, bf16[1,896,256]{2,1,0:T(8,128)(2,1)}, u32[]{:S(2)}) copy-start(bf16[1,896,256]{2,1,0:T(8,128)(2,1)} %param.17) | copy-start | bytes 1376260
  178.3 6.3 %copy-start.10 = (s32[1,256]{1,0:T(1,128)S(1)}, s32[1,256]{1,0:T(1,128)}, u32[]{:S(2)}) copy-start(s32[1,256]{1,0:T(1,128)} %pair_ref.1) | copy-start | bytes 3076
  178.3 6.3 %collective-permute-start.3 = (f32[256,1024]{1,0:T(8,128)S(1)}, f32[256,1024]{1,0:T(8,128)S(1)}, u32[]{:S(2)}, u32[]{:S(2)}) collective-permute-start(f32[256,1024]{1,0:T(8,128)S(1)} %partial_hidden.3), channel_id=1, source_target_pairs={{0,16},{16,0},{1,17},{17,1},{2,18},{18,2},{3,19},{19,3},{4,20},{20... | collective-permute-start | bytes 3145736 | tf_op jit(solution)/shard_map/ppermute | solution.py:286
  184.5 6.5 %copy-start.1 = (f32[32,3584]{1,0:T(8,128)S(1)}, f32[32,3584]{1,0:T(8,128)}, u32[]{:S(2)}) copy-start(f32[32,3584]{1,0:T(8,128)} %master_ref.3) | copy-start | bytes 1376260
  184.6 6.5 %copy-start.3 = (f32[32,3584]{1,0:T(8,128)S(1)}, f32[32,3584]{1,0:T(8,128)}, u32[]{:S(2)}) copy-start(f32[32,3584]{1,0:T(8,128)} %teacher_ref.3) | copy-start | bytes 1376260
  184.6 6.5 %copy-start.6 = (bf16[32,3584]{1,0:T(8,128)(2,1)S(1)}, bf16[32,3584]{1,0:T(8,128)(2,1)}, u32[]{:S(2)}) copy-start(bf16[32,3584]{1,0:T(8,128)(2,1)} %first_ref.3) | copy-start | bytes 688132
  184.6 6.5 %copy-start.8 = (bf16[32,3584]{1,0:T(8,128)(2,1)S(1)}, bf16[32,3584]{1,0:T(8,128)(2,1)}, u32[]{:S(2)}) copy-start(bf16[32,3584]{1,0:T(8,128)(2,1)} %second_ref.3) | copy-start | bytes 688132
  186.2 15.5 %all-to-all-start.4 = ((f32[16,8,256]{2,1,0:T(8,128)}), f32[16,8,256]{2,1,0:T(8,128)S(1)}, u32[]{:S(2)}, u32[]{:S(2)}) async-start(f32[16,8,256]{2,1,0:T(8,128)} %broadcast_in_dim.19), calls=%async_computation.5 | async-start | bytes 262144 | tf_op jit(solution)/shard_map/all_to_all | solution.py:289
Sparse Core Ops, SparseCore 0:
  10.8 39.5 reduce-scatter.1
  76.2 53.4 all-gather.1

commit v7 on v6

--- a/solution.py
+++ b/solution.py
@@ -112,35 +112,38 @@
 
 
 def pick_kernel(ids_ref, table_ref, out_ref):
-    ids = jnp.concatenate([ids_ref[0], ids_ref[1]], axis=1)
+    groups = ids_ref.shape[0]
+    ids = jnp.concatenate([ids_ref[group] for group in range(groups)], axis=1)
     count = ids.shape[1]
     upper = ids >> 7
     lower = jnp.broadcast_to(ids & 127, (8, count))
     rows = lax.broadcasted_iota(jnp.int32, (UPPER, count), 0)
     hot = jnp.where(rows == upper, 1.0, 0.0).astype(bf16)
+    lines = jnp.dot(table_ref[...], hot, preferred_element_type=f32)
     picked = jnp.zeros((8, count), f32)
-    for part in range(4):
-        lines = jnp.dot(table_ref[pl.ds(part * 256, 256), :], hot, preferred_element_type=f32)
-        for k in range(32):
-            picked = jnp.where(lower == part * 32 + k, lines[k * 8 : (k + 1) * 8, :], picked)
-    out_ref[0] = picked.astype(bf16)
+    for k in range(128):
+        picked = jnp.where(lower == k, lines[k * 8 : (k + 1) * 8, :], picked)
+    width = out_ref.shape[2]
+    for chip in range(out_ref.shape[0]):
+        out_ref[chip] = picked[:, chip * width : (chip + 1) * width].astype(bf16)
 
 
 def pick_tokens(ids, table):
-    chips, count = ids.shape[0] // 2, 2 * ids.shape[2]
+    groups, width = 16, 2 * TOKENS
+    chips, steps = ids.shape[0] // 2, ids.shape[0] // groups
     return pl.pallas_call(
         pick_kernel,
-        grid=(chips,),
+        grid=(steps,),
         in_specs=[
-            pl.BlockSpec((2, 1, TOKENS), lambda i: (i, 0, 0)),
+            pl.BlockSpec((groups, 1, TOKENS), lambda i: (i, 0, 0)),
             pl.BlockSpec((1024, UPPER), lambda i: (0, 0)),
         ],
-        out_specs=pl.BlockSpec((1, 8, count), lambda i: (i, 0, 0)),
-        out_shape=jax.ShapeDtypeStruct((chips, 8, count), bf16),
+        out_specs=pl.BlockSpec((groups // 2, 8, width), lambda i: (i, 0, 0)),
+        out_shape=jax.ShapeDtypeStruct((chips, 8, width), bf16),
         cost_estimate=pl.CostEstimate(
-            flops=2 * 1024 * UPPER * chips * count, bytes_accessed=1 << 21, transcendentals=0
-        ),
-        compiler_params=pltpu.CompilerParams(vmem_limit_bytes=20 << 20),
+            flops=2 * 1024 * UPPER * chips * width, bytes_accessed=1 << 21, transcendentals=0
+        ),
+        compiler_params=pltpu.CompilerParams(vmem_limit_bytes=40 << 20),
         name="pick_tokens",
     )(ids, table)
 
@@ -174,11 +177,16 @@
 
 
 def hidden_kernel(group_ref, side_ref, rows_ref, out_ref):
-    side = side_ref[0]
-    product = jnp.dot(side, rows_ref[...].reshape(512, WIDTH), preferred_element_type=f32)
-    wide = side.astype(f32)
-    square = wide * wide
-    square = (square[:, :128] + square[:, 128:256]) + (square[:, 256:384] + square[:, 384:])
+    product, square = 0.0, 0.0
+    for t in range(side_ref.shape[0]):
+        side = side_ref[t]
+        product = product + jnp.dot(
+            side, rows_ref[:, t].reshape(512, WIDTH), preferred_element_type=f32
+        )
+        wide = side.astype(f32)
+        terms = wide * wide
+        for k in range(4):
+            square = square + terms[:, k * 128 : (k + 1) * 128]
 
     @pl.when(pl.program_id(0) == 0)
     def _():
@@ -196,10 +204,10 @@
         hidden_kernel,
         grid_spec=pltpu.PrefetchScalarGridSpec(
             num_scalar_prefetch=1,
-            grid=(4,),
+            grid=(2,),
             in_specs=[
-                pl.BlockSpec((1, TOKENS, 512), lambda t, group: (t, group[0], 0)),
-                pl.BlockSpec((8, 1, 64, WIDTH), lambda t, group: (0, t, 0, 0)),
+                pl.BlockSpec((2, TOKENS, 512), lambda t, group: (t, group[0], 0)),
+                pl.BlockSpec((8, 2, 64, WIDTH), lambda t, group: (0, t, 0, 0)),
             ],
             out_specs=pl.BlockSpec((TOKENS, 1024), lambda t, group: (0, 0)),
         ),

time: 210 us -> 206 us (0.981)
  Pallas kernels: 32.1 us -> 27.4 us
    pallas_call x1, Pallas kernels: 11.8 us -> 9.09 us  [pick_tokens(): pl.pallas_call(pick_kernel, grid=(steps,), in_specs=[pl.BlockSpec((groups...]
  transfers between devices with their start and end apart: 9 -> 9, of which waited for: 6 -> 6; matrix products, arithmetic and copies ran while one was open for 1% -> 1% of each run, Pallas kernels for 12% -> 10%
where the time goes in v7:
time: 206 us; the launch traced here: 205 us
  waiting for transfers between devices  91 us (44%)
  starting transfers between devices  32.4 us (16%)
  blocking collectives  31.9 us (15%)
  Pallas kernels  27.4 us (13%)
  between operations  14.3 us (7%)
  local copies, waits for them, and re-layouts  6.08 us (3%)
    reduce_scatter x1, waiting for transfers between devices, shards(): lax.psum_scatter(grad_parts[0], 'dp', scatter_dimension=0, tiled=True)  42.5 us
    all_to_all x1, waiting for transfers between devices, shards(): side = lax.all_to_all(turned, 't', 0, 0, tiled=True)  26.5 us
    all_to_all x1, blocking collectives, shards(): lax.all_to_all(columns.reshape(8, 32, WIDTH), ('yl', 'dp'), 0, 0, tiled=T...  18.7 us
    all_to_all x1, blocking collectives, shards(): received = lax.all_to_all(picked, ('z', 'yl'), 0, 0, tiled=True)  13.2 us
    ppermute x3, starting transfers between devices, shards(): parts.append(lax.ppermute(received, 'dp', [(i, i ^ k) for i in range(4)]))  12.2 us
    ppermute x3, waiting for transfers between devices, shards(): parts.append(lax.ppermute(received, 'dp', [(i, i ^ k) for i in range(4)]))  9.14 us
    pallas_call x1, Pallas kernels, pick_tokens(): pl.pallas_call(pick_kernel, grid=(steps,), in_specs=[pl.BlockSpec((groups...  9.09 us
    all_to_all x1, starting transfers between devices, shards(): lax.all_to_all(jnp.broadcast_to(token_ids[None], (32, 1, TOKENS)), ('z',...  8.85 us
  transfers between devices with their start and end apart: 9, of which 6 were waited for; matrix products, arithmetic and copies ran while one was open for 1% of the time, Pallas kernels for 10%

profile of v7, /device:TPU:8, one launch (start us, length us, event | category | flops | bytes accessed | tf_op | source)
XLA Modules:
  0.0 204.6 jit_solution(2112936037968963433)
XLA Ops:
  7.2 0.7 reduce-scatter.2.cloned.1.call-update
  7.9 42.5 %reduce-scatter.2.cloned.1.call-done.gradient_ref = bf16[32,3584]{1,0:T(8,128)(2,1)} async-done(((bf16[128,3584]{1,0:T(8,128)(2,1)}), bf16[32,3584]{1,0:T(8,128)(2,1)}) %reduce-scatter.2.cloned.1.call-update) | async-done | bytes 229392 | tf_op jit(solution)/shard_map/reduce_scatter | solution.py:269
  50.4 1.0 copy-done
  51.4 1.0 copy-done.2
  52.5 0.9 copy-done.5
  53.4 0.9 copy-done.7
  54.3 2.2 %teacher_columns.1 = bf16[2,4,32,896]{3,2,1,0:T(8,128)(2,1)S(1)} custom-call(f32[32,3584]{1,0:T(8,128)S(1)} %copy-done, bf16[32,3584]{1,0:T(8,128)(2,1)S(1)} %copy-done.5, bf16[32,3584]{1,0:T(8,128)(2,1)S(1)} %copy-done.7, f32[32,3584]{1,0:T(8,128)S(1)} %copy-done.2, bf16[32,3584]{1,0:T(8,128)(2,1)} %reduce-scatter.2.cloned.1.call-done.gradient_ref), custom_call_target="tpu_custom_call" | custom-call | flops 2097152 | bytes 4194304 | tf_op jit(solution)/shard_map/teacher_columns/pallas_call | solution.py:70
  56.6 18.7 %all_to_all.25 = bf16[8,32,896]{2,1,0:T(8,128)(2,1)S(1)} all-to-all(bf16[8,32,896]{2,1,0:T(8,128)(2,1)S(1)} %bitcast.19), channel_id=1, replica_groups=mesh['z'=8,'yl'=2,'c'=2,'dp'=4,'t'=4] {'yl','dp'}, dimensions={0} | all-to-all | bytes 917504 | tf_op jit(solution)/shard_map/all_to_all | solution.py:281
  75.3 0.8 copy.15
  76.1 0.6 broadcast_in_dim.18
  76.7 8.8 %all-to-all-start = ((s32[32,1,256]{2,1,0:T(1,128)}), s32[32,1,256]{2,1,0:T(1,128)S(1)}, u32[]{:S(2)}, u32[]{:S(2)}) async-start(s32[32,1,256]{2,1,0:T(1,128)} %broadcast_in_dim.18), calls=%async_computation.1 | async-start | bytes 65536 | tf_op jit(solution)/shard_map/all_to_all | solution.py:266
  85.6 2.5 %turn_table.1.table_ref = bf16[1024,512]{1,0:T(8,128)(2,1)S(1)} custom-call(bf16[501,8,128]{2,1,0:T(8,128)(2,1)S(1)} %bitcast.20), custom_call_target="tpu_custom_call" | custom-call | bytes 16777216 | tf_op jit(solution)/shard_map/turn_table/pallas_call | solution.py:102
  88.2 4.8 %all-to-all-done.ids_ref = s32[32,1,256]{2,1,0:T(1,128)S(1)} async-done(((s32[32,1,256]{2,1,0:T(1,128)}), s32[32,1,256]{2,1,0:T(1,128)S(1)}, u32[]{:S(2)}, u32[]{:S(2)}) %all-to-all-start) | async-done | bytes 32800 | tf_op jit(solution)/shard_map/all_to_all | solution.py:266
  93.0 9.1 %pick_tokens.1 = bf16[16,8,512]{2,1,0:T(8,128)(2,1)S(1)} custom-call(s32[32,1,256]{2,1,0:T(1,128)S(1)} %all-to-all-done.ids_ref, bf16[1024,512]{1,0:T(8,128)(2,1)S(1)} %turn_table.1.table_ref), custom_call_target="tpu_custom_call" | custom-call | flops 8589934592 | bytes 2097152 | tf_op jit(solution)/shard_map/pick_tokens/pallas_call | solution.py:134
  102.1 13.2 %all_to_all.26 = bf16[16,8,512]{2,1,0:T(8,128)(2,1)S(1)} all-to-all(bf16[16,8,512]{2,1,0:T(8,128)(2,1)S(1)} %pick_tokens.1), channel_id=1, replica_groups=mesh['z'=8,'yl'=2,'c'=2,'dp'=4,'t'=4] {'z','yl'}, dimensions={0} | all-to-all | bytes 262144 | tf_op jit(solution)/shard_map/all_to_all | solution.py:272
  115.3 2.2 %collective-permute-start = (bf16[16,8,512]{2,1,0:T(8,128)(2,1)S(1)}, bf16[16,8,512]{2,1,0:T(8,128)(2,1)S(1)}, u32[]{:S(2)}, u32[]{:S(2)}) collective-permute-start(bf16[16,8,512]{2,1,0:T(8,128)(2,1)S(1)} %all_to_all.26), channel_id=1, source_target_pairs={{0,4},{4,0},{8,12},{12,8},{1,5},{5,1},{9,13},{13,9},{2,6},{6,2},{1... | collective-permute-start | bytes 393224 | tf_op jit(solution)/shard_map/ppermute | solution.py:286
  117.5 4.6 %collective-permute-start.1 = (bf16[16,8,512]{2,1,0:T(8,128)(2,1)S(1)}, bf16[16,8,512]{2,1,0:T(8,128)(2,1)S(1)}, u32[]{:S(2)}, u32[]{:S(2)}) collective-permute-start(bf16[16,8,512]{2,1,0:T(8,128)(2,1)S(1)} %all_to_all.26), channel_id=1, source_target_pairs={{0,8},{4,12},{8,0},{12,4},{1,9},{5,13},{9,1},{13,5},{2,10},{6,14},... | collective-permute-start | bytes 393224 | tf_op jit(solution)/shard_map/ppermute | solution.py:286
  122.1 5.4 %collective-permute-start.2 = (bf16[16,8,512]{2,1,0:T(8,128)(2,1)S(1)}, bf16[16,8,512]{2,1,0:T(8,128)(2,1)S(1)}, u32[]{:S(2)}, u32[]{:S(2)}) collective-permute-start(bf16[16,8,512]{2,1,0:T(8,128)(2,1)S(1)} %all_to_all.26), channel_id=1, source_target_pairs={{0,12},{4,8},{8,4},{12,0},{1,13},{5,9},{9,5},{13,1},{2,14},{6,10},... | collective-permute-start | bytes 393224 | tf_op jit(solution)/shard_map/ppermute | solution.py:286
  127.6 3.9 %collective-permute-done.1 = bf16[16,8,512]{2,1,0:T(8,128)(2,1)S(1)} collective-permute-done((bf16[16,8,512]{2,1,0:T(8,128)(2,1)S(1)}, bf16[16,8,512]{2,1,0:T(8,128)(2,1)S(1)}, u32[]{:S(2)}, u32[]{:S(2)}) %collective-permute-start.1) | collective-permute-done | bytes 131104 | tf_op jit(solution)/shard_map/ppermute | solution.py:286
  131.4 5.3 %collective-permute-done.2 = bf16[16,8,512]{2,1,0:T(8,128)(2,1)S(1)} collective-permute-done((bf16[16,8,512]{2,1,0:T(8,128)(2,1)S(1)}, bf16[16,8,512]{2,1,0:T(8,128)(2,1)S(1)}, u32[]{:S(2)}, u32[]{:S(2)}) %collective-permute-start.2) | collective-permute-done | bytes 131104 | tf_op jit(solution)/shard_map/ppermute | solution.py:286
  136.7 0.9 pad_maximum_fusion.in_ref
  137.6 2.9 %turn_tokens.1 = bf16[4,512,512]{2,1,0:T(8,128)(2,1)} custom-call(s32[1]{0:T(128)} %bitcast.2.place_ref, bf16[4,16,8,512]{3,2,1,0:T(8,128)(2,1)} %pad_maximum_fusion.in_ref), custom_call_target="tpu_custom_call" | custom-call | flops 2097152 | bytes 4194304 | tf_op jit(solution)/shard_map/turn_tokens/pallas_call | solution.py:165
  140.4 4.4 %all-to-all-start.2 = ((bf16[4,512,512]{2,1,0:T(8,128)(2,1)}), bf16[4,512,512]{2,1,0:T(8,128)(2,1)S(1)}, u32[]{:S(2)}, u32[]{:S(2)}) async-start(bf16[4,512,512]{2,1,0:T(8,128)(2,1)} %turn_tokens.1), calls=%async_computation.3 | async-start | bytes 4194304 | tf_op jit(solution)/shard_map/all_to_all | solution.py:290
  144.8 26.5 %all-to-all-done.2.side_ref = bf16[4,512,512]{2,1,0:T(8,128)(2,1)S(1)} async-done(((bf16[4,512,512]{2,1,0:T(8,128)(2,1)}), bf16[4,512,512]{2,1,0:T(8,128)(2,1)S(1)}, u32[]{:S(2)}, u32[]{:S(2)}) %all-to-all-start.2) | async-done | bytes 2097184 | tf_op jit(solution)/shard_map/all_to_all | solution.py:290
  171.4 3.2 %partial_hidden.3 = f32[256,1024]{1,0:T(8,128)S(1)} custom-call(s32[1]{0:T(128)S(6)} %sub.3.group_ref, bf16[4,512,512]{2,1,0:T(8,128)(2,1)S(1)} %all-to-all-done.2.side_ref, bf16[8,4,64,896]{3,2,1,0:T(8,128)(2,1)} %bitcast.22), custom_call_target="tpu_custom_call" | custom-call | flops 939524096 | bytes 6291456 | tf_op jit(solution)/shard_map/partial_hidden/pallas_call | solution.py:203
  174.6 2.1 %collective-permute-start.3 = (f32[256,1024]{1,0:T(8,128)S(1)}, f32[256,1024]{1,0:T(8,128)S(1)}, u32[]{:S(2)}, u32[]{:S(2)}) collective-permute-start(f32[256,1024]{1,0:T(8,128)S(1)} %partial_hidden.3), channel_id=1, source_target_pairs={{0,16},{16,0},{1,17},{17,1},{2,18},{18,2},{3,19},{19,3},{4,20},{20... | collective-permute-start | bytes 3145736 | tf_op jit(solution)/shard_map/ppermute | solution.py:294
  176.6 3.2 %partial_hidden.2.own_ref = f32[256,1024]{1,0:T(8,128)S(1)} custom-call(s32[1]{0:T(128)} %bitcast.1.group_ref, bf16[4,512,512]{2,1,0:T(8,128)(2,1)S(1)} %all-to-all-done.2.side_ref, bf16[8,4,64,896]{3,2,1,0:T(8,128)(2,1)} %bitcast.23), custom_call_target="tpu_custom_call" | custom-call | flops 939524096 | bytes 6291456 | tf_op jit(solution)/shard_map/partial_hidden/pallas_call | solution.py:203
  179.9 0.9 label_pairs.1
  180.9 0.7 broadcast_in_dim.19
  181.5 4.8 %all-to-all-start.4 = ((f32[16,8,256]{2,1,0:T(8,128)}), f32[16,8,256]{2,1,0:T(8,128)S(1)}, u32[]{:S(2)}, u32[]{:S(2)}) async-start(f32[16,8,256]{2,1,0:T(8,128)} %broadcast_in_dim.19), calls=%async_computation.5 | async-start | bytes 262144 | tf_op jit(solution)/shard_map/all_to_all | solution.py:297
  186.4 3.3 %optimizer_step.1 = (f32[32,3584]{1,0:T(8,128)}, bf16[32,3584]{1,0:T(8,128)(2,1)}, bf16[32,3584]{1,0:T(8,128)(2,1)}, f32[32,3584]{1,0:T(8,128)}) custom-call(f32[32,3584]{1,0:T(8,128)S(1)} %copy-done.1, bf16[32,3584]{1,0:T(8,128)(2,1)S(1)} %copy-done.6, bf16[32,3584]{1,0:T(8,128)(2,1)S(1)} %copy-done.8, f32[32,3584]{1,0:T(8,128)S(1)} %copy-done.3, ...), custom_call_target="tpu_custom_call" | custom-call | flops 2097152 | bytes 4194304 | tf_op jit(solution)/shard_map/optimizer_step/pallas_call | solution.py:81
  189.7 7.4 %all-to-all-done.4 = f32[16,8,256]{2,1,0:T(8,128)S(1)} async-done(((f32[16,8,256]{2,1,0:T(8,128)}), f32[16,8,256]{2,1,0:T(8,128)S(1)}, u32[]{:S(2)}, u32[]{:S(2)}) %all-to-all-start.4) | async-done | bytes 131104 | tf_op jit(solution)/shard_map/all_to_all | solution.py:297
  (27 shorter events, 0.8 us)
Async XLA Ops:
  7.2 43.3 %reduce-scatter.2.cloned.1.call-start = ((), (), s32[]{:S(2)}) async-start(), calls=%async_computation.6 | async-start | bytes 1146880 | tf_op jit(solution)/shard_map/reduce_scatter | solution.py:269
  7.2 68.9 %copy-start.11 = (s32[1,256]{1,0:T(1,128)S(1)}, s32[1,256]{1,0:T(1,128)}, u32[]{:S(2)}) copy-start(s32[1,256]{1,0:T(1,128)} %param.15) | copy-start | bytes 3076
  7.9 163.4 %all-gather.2.cloned.1.call-start = ((), (), s32[]{:S(2)}) async-start(), calls=%async_computation.7 | async-start | bytes 4128768 | tf_op jit(solution)/shard_map/all_gather | solution.py:283
  50.4 1.0 copy-start
  51.4 1.0 copy-start.2
  52.5 0.9 copy-start.5
  53.4 0.9 copy-start.7
  54.3 31.3 %copy-start.4 = (bf16[8,64128]{1,0:T(8,128)(2,1)S(1)}, bf16[8,64128]{1,0:T(8,128)(2,1)}, u32[]{:S(2)}) copy-start(bf16[8,64128]{1,0:T(8,128)(2,1)} %param.14) | copy-start | bytes 3078148
  76.7 16.2 %all-to-all-start = ((s32[32,1,256]{2,1,0:T(1,128)}), s32[32,1,256]{2,1,0:T(1,128)S(1)}, u32[]{:S(2)}, u32[]{:S(2)}) async-start(s32[32,1,256]{2,1,0:T(1,128)} %broadcast_in_dim.18), calls=%async_computation.1 | async-start | bytes 65536 | tf_op jit(solution)/shard_map/all_to_all | solution.py:266
  115.3 12.2 %collective-permute-start = (bf16[16,8,512]{2,1,0:T(8,128)(2,1)S(1)}, bf16[16,8,512]{2,1,0:T(8,128)(2,1)S(1)}, u32[]{:S(2)}, u32[]{:S(2)}) collective-permute-start(bf16[16,8,512]{2,1,0:T(8,128)(2,1)S(1)} %all_to_all.26), channel_id=1, source_target_pairs={{0,4},{4,0},{8,12},{12,8},{1,5},{5,1},{9,13},{13,9},{2,6},{6,2},{1... | collective-permute-start | bytes 393224 | tf_op jit(solution)/shard_map/ppermute | solution.py:286
  117.5 13.9 %collective-permute-start.1 = (bf16[16,8,512]{2,1,0:T(8,128)(2,1)S(1)}, bf16[16,8,512]{2,1,0:T(8,128)(2,1)S(1)}, u32[]{:S(2)}, u32[]{:S(2)}) collective-permute-start(bf16[16,8,512]{2,1,0:T(8,128)(2,1)S(1)} %all_to_all.26), channel_id=1, source_target_pairs={{0,8},{4,12},{8,0},{12,4},{1,9},{5,13},{9,1},{13,5},{2,10},{6,14},... | collective-permute-start | bytes 393224 | tf_op jit(solution)/shard_map/ppermute | solution.py:286
  122.1 14.6 %collective-permute-start.2 = (bf16[16,8,512]{2,1,0:T(8,128)(2,1)S(1)}, bf16[16,8,512]{2,1,0:T(8,128)(2,1)S(1)}, u32[]{:S(2)}, u32[]{:S(2)}) collective-permute-start(bf16[16,8,512]{2,1,0:T(8,128)(2,1)S(1)} %all_to_all.26), channel_id=1, source_target_pairs={{0,12},{4,8},{8,4},{12,0},{1,13},{5,9},{9,5},{13,1},{2,14},{6,10},... | collective-permute-start | bytes 393224 | tf_op jit(solution)/shard_map/ppermute | solution.py:286
  140.4 30.9 %all-to-all-start.2 = ((bf16[4,512,512]{2,1,0:T(8,128)(2,1)}), bf16[4,512,512]{2,1,0:T(8,128)(2,1)S(1)}, u32[]{:S(2)}, u32[]{:S(2)}) async-start(bf16[4,512,512]{2,1,0:T(8,128)(2,1)} %turn_tokens.1), calls=%async_computation.3 | async-start | bytes 4194304 | tf_op jit(solution)/shard_map/all_to_all | solution.py:290
  174.6 5.4 %copy-start.9 = (bf16[1,896,256]{2,1,0:T(8,128)(2,1)S(1)}, bf16[1,896,256]{2,1,0:T(8,128)(2,1)}, u32[]{:S(2)}) copy-start(bf16[1,896,256]{2,1,0:T(8,128)(2,1)} %param.17) | copy-start | bytes 1376260
  174.6 5.4 %copy-start.10 = (s32[1,256]{1,0:T(1,128)S(1)}, s32[1,256]{1,0:T(1,128)}, u32[]{:S(2)}) copy-start(s32[1,256]{1,0:T(1,128)} %pair_ref.1) | copy-start | bytes 3076
  174.6 5.3 %collective-permute-start.3 = (f32[256,1024]{1,0:T(8,128)S(1)}, f32[256,1024]{1,0:T(8,128)S(1)}, u32[]{:S(2)}, u32[]{:S(2)}) collective-permute-start(f32[256,1024]{1,0:T(8,128)S(1)} %partial_hidden.3), channel_id=1, source_target_pairs={{0,16},{16,0},{1,17},{17,1},{2,18},{18,2},{3,19},{19,3},{4,20},{20... | collective-permute-start | bytes 3145736 | tf_op jit(solution)/shard_map/ppermute | solution.py:294
  179.9 6.5 %copy-start.1 = (f32[32,3584]{1,0:T(8,128)S(1)}, f32[32,3584]{1,0:T(8,128)}, u32[]{:S(2)}) copy-start(f32[32,3584]{1,0:T(8,128)} %master_ref.3) | copy-start | bytes 1376260
  179.9 6.5 %copy-start.3 = (f32[32,3584]{1,0:T(8,128)S(1)}, f32[32,3584]{1,0:T(8,128)}, u32[]{:S(2)}) copy-start(f32[32,3584]{1,0:T(8,128)} %teacher_ref.3) | copy-start | bytes 1376260
  179.9 6.5 %copy-start.6 = (bf16[32,3584]{1,0:T(8,128)(2,1)S(1)}, bf16[32,3584]{1,0:T(8,128)(2,1)}, u32[]{:S(2)}) copy-start(bf16[32,3584]{1,0:T(8,128)(2,1)} %first_ref.3) | copy-start | bytes 688132
  179.9 6.5 %copy-start.8 = (bf16[32,3584]{1,0:T(8,128)(2,1)S(1)}, bf16[32,3584]{1,0:T(8,128)(2,1)}, u32[]{:S(2)}) copy-start(bf16[32,3584]{1,0:T(8,128)(2,1)} %second_ref.3) | copy-start | bytes 688132
  181.5 15.6 %all-to-all-start.4 = ((f32[16,8,256]{2,1,0:T(8,128)}), f32[16,8,256]{2,1,0:T(8,128)S(1)}, u32[]{:S(2)}, u32[]{:S(2)}) async-start(f32[16,8,256]{2,1,0:T(8,128)} %broadcast_in_dim.19), calls=%async_computation.5 | async-start | bytes 262144 | tf_op jit(solution)/shard_map/all_to_all | solution.py:297
Sparse Core Ops, SparseCore 0:
  10.8 39.5 reduce-scatter.1
  76.2 53.4 all-gather.1
